TPU v7x, 256 devices: a whole 4x4x8 slice. The times are simulated.
256 devices in a mesh: dp: 64 (over z, y, core), tensor: 4 (over x).
Axes of the slice: x: 4, y: 4, z: 8, core: 2. Of those that a mesh axis runs over, the one named last changes fastest.
Arguments:
- tokens: bfloat16 [32768, 8192], P('dp', 'tensor'), may hold values from -6 to 6
- token_adapter_index: int32 [32768, 1], P('dp'), may hold values from 0 to 63; in each aligned block of 512 rows (0 to 511, 512 to 1023, ...) at most 16 rows name the same one
- frozen_key_value_weight: bfloat16 [8192, 2048], P('tensor'), may hold values from -0.0625 to 0.0625
- adapter_down_weight: bfloat16 [64, 64, 8192], P('dp', None, 'tensor'), may hold values from -0.0625 to 0.0625
- adapter_up_weight: bfloat16 [64, 64, 2048], P('dp', None, 'tensor'), may hold values from -0.75 to 0.75
Outputs:
- projected: bfloat16 [32768, 2048], P('dp', 'tensor')
Inputs may be any that keep to these rules, and one draw needn't show every extreme that they name: `token_adapter_index`: among the tokens of one index of dp, no adapter is named by more than 16 tokens, a bound that some block reaches.
All inputs are finite; a program needn't handle non-finite values.
Results may differ from a plain program's by a relative error of at most 0.0048.
Values may be sent and summed in bfloat16 or wider, within the bound.
No kernel may reach another device: no remote copies, remote signals or barrier semaphores. Data moves between devices by JAX's collectives and lax.ppermute only.
A program may use at most 128 MiB of HBM per device.

v0:
```python
import jax
import jax.numpy as jnp
from jax import lax
from jax.sharding import PartitionSpec as P


def on_device(
    tokens, token_adapter_index, frozen_key_value_weight, adapter_down_weight, adapter_up_weight
):
    holder_count = lax.axis_size("dp")
    token_count = tokens.shape[0]
    feature_count = tokens.shape[1]
    row_capacity = 2 * token_count // holder_count
    adapter_rank_width = adapter_down_weight.shape[1]
    adapter_of = token_adapter_index[:, 0]
    membership = (adapter_of[:, None] == jnp.arange(holder_count, dtype=jnp.int32)[None, :]).astype(
        jnp.int32
    )
    earlier = jnp.cumsum(membership, axis=0) - membership
    position = jnp.sum(earlier * membership, axis=1)
    adapter_slot_index = adapter_of * row_capacity + position
    send_buffer = (
        jnp.zeros((holder_count * row_capacity, feature_count), tokens.dtype)
        .at[adapter_slot_index]
        .set(tokens)
    )
    send_buffer = send_buffer.reshape(holder_count, row_capacity, feature_count)
    partial_value = jnp.dot(tokens, frozen_key_value_weight, preferred_element_type=jnp.float32)
    base_out = lax.psum_scatter(partial_value, "tensor", scatter_dimension=1, tiled=True)
    product = jnp.einsum(
        "acd,ard->acr",
        send_buffer,
        lax.all_gather(adapter_down_weight, "dp", axis=0, tiled=True),
        preferred_element_type=jnp.float32,
    )
    summed = lax.psum(product.reshape(holder_count, row_capacity * adapter_rank_width), "tensor")
    reduced_activations = summed.reshape(holder_count, row_capacity, adapter_rank_width).astype(
        jnp.bfloat16
    )
    adapter_delta = jnp.einsum(
        "flz,fzq->flq",
        reduced_activations,
        lax.all_gather(adapter_up_weight, "dp", axis=0, tiled=True),
        preferred_element_type=jnp.float32,
    ).astype(jnp.bfloat16)
    flattened_delta = adapter_delta.reshape(holder_count * row_capacity, adapter_delta.shape[2])[
        adapter_slot_index
    ]
    return (base_out + flattened_delta.astype(jnp.float32)).astype(jnp.bfloat16)


def solution(mesh):
    placed = (
        P("dp", "tensor"),
        P("dp", None),
        P("tensor", None),
        P("dp", None, "tensor"),
        P("dp", None, "tensor"),
    )
    return jax.shard_map(
        on_device, mesh=mesh, in_specs=placed, out_specs=P("dp", "tensor"), check_vma=False
    )
```

profile of v0, /device:TPU:1, one launch (start us, length us, event | category | flops | bytes accessed | tf_op | source)
XLA Modules:
  0.0 209.0 jit_solution(12527318570697684783)
XLA Ops:
  7.4 0.0 all-gather.3.cloned.1.call-start
  7.4 0.7 all-gather.3.cloned.1.call-update
  8.1 0.0 all-gather.5.cloned.1.call-start
  8.1 0.7 all-gather.5.cloned.1.call-update
  8.8 0.0 reduce-scatter.2.cloned.1.call-start
  8.9 10.5 %fusion.6 = f32[512,2048]{1,0:T(8,128)} fusion(bf16[512,2048]{1,0:T(8,128)(2,1)} %param.5, bf16[2048,2048]{1,0:T(8,128)(2,1)} %param.7), kind=kOutput, calls=%fused_computation.17 | convolution fusion | flops 4294967296 | bytes 14680064 | tf_op jit(solution)/shard_map/dot_general | solution.py:28
  19.4 0.0 copy-start
  19.4 0.0 reduce-scatter.2.cloned.1.call-update
  19.4 0.7 copy-done
  20.1 1.2 reduce-window.6
  21.3 0.2 slice_reduce_fusion
  21.5 0.1 fusion.4
  21.7 7.3 %scatter_custom_fusion = bf16[1024,2048]{1,0:T(8,128)(2,1)} fusion(s32[512]{0:T(512)S(1)} %bitcast.36, bf16[512,2048]{1,0:T(8,128)(2,1)} %param.5, bf16[]{:T(256)} %constant.4.clone.1), kind=kCustom, calls=%fused_computation.2 | custom fusion | bytes 4194816 | tf_op jit(solution)/shard_map/scatter | solution.py:25
  29.0 86.4 %all-gather.3.cloned.1.call-done = bf16[64,64,2048]{2,1,0:T(8,128)(2,1)} async-done(((bf16[1,64,2048]{2,1,0:T(8,128)(2,1)}), bf16[64,64,2048]{2,1,0:T(8,128)(2,1)}) %all-gather.3.cloned.1.call-update) | async-done | bytes 16777232 | tf_op jit(solution)/shard_map/all_gather | solution.py:33
  115.4 11.5 %fusion.7 = f32[64,16,64]{2,1,0:T(8,128)S(1)} fusion(bf16[64,16,2048]{2,1,0:T(8,128)(2,1)} %bitcast.32, bf16[64,64,2048]{2,1,0:T(8,128)(2,1)} %all-gather.3.cloned.1.call-done), kind=kOutput, calls=%fused_computation.18 | convolution fusion | flops 268435456 | bytes 21233664 | tf_op jit(solution)/shard_map/acd,ard->acr/dot_general | solution.py:30
  126.9 0.2 reshape.30
  127.0 16.6 %all-reduce.1 = bf16[64,1024]{1,0:T(8,128)(2,1)S(1)} all-reduce(f32[64,1024]{1,0:T(8,128)S(1)} %reshape.30), channel_id=1, replica_groups=mesh['dp'=64,'tensor'=4] {'tensor'}, use_global_device_ids=true, to_apply=%region_5.6 | all-reduce | flops 65536 | bytes 393216 | tf_op jit(solution)/shard_map/psum | solution.py:36
  143.7 0.2 convert_element_type.25
  143.9 50.7 %all-gather.5.cloned.1.call-done = bf16[64,64,512]{2,1,0:T(8,128)(2,1)} async-done(((bf16[1,64,512]{2,1,0:T(8,128)(2,1)}), bf16[64,64,512]{2,1,0:T(8,128)(2,1)}) %all-gather.5.cloned.1.call-update) | async-done | bytes 4194320 | tf_op jit(solution)/shard_map/all_gather | solution.py:43
  194.6 2.8 %convolution_convert_fusion = bf16[64,16,512]{2,1,0:T(8,128)(2,1)S(1)} fusion(bf16[64,16,64]{2,1,0:T(8,128)(2,1)S(1)} %convert_element_type.25, bf16[64,64,512]{2,1,0:T(8,128)(2,1)} %all-gather.5.cloned.1.call-done), kind=kOutput, calls=%fused_computation.4 | convolution fusion | flops 67633152 | bytes 5373952 | tf_op jit(solution)/shard_map/flz,fzq->flq/dot_general | solution.py:40
  197.4 2.0 gather_fusion
  199.4 0.0 reduce-scatter.2.cloned.1.call-done
  199.4 2.2 %add_convert_fusion = bf16[512,512]{1,0:T(8,128)(2,1)} fusion(f32[512,512]{1,0:T(8,128)} %reduce-scatter.2.cloned.1.call-done, bf16[512,512]{1,0:T(8,128)(2,1)S(1)} %gather_fusion), kind=kLoop, calls=%fused_computation.5 | loop fusion | flops 786432 | bytes 2097152 | tf_op jit(solution)/shard_map/convert_element_type | solution.py:49
  (5 shorter events, 0.1 us)
Async XLA Ops:
  7.4 108.0 %all-gather.3.cloned.1.call-start = ((), (), s32[]{:S(2)}) async-start(), calls=%async_computation.2 | async-start | bytes 17039360 | tf_op jit(solution)/shard_map/all_gather | solution.py:33
  8.1 186.5 %all-gather.5.cloned.1.call-start = ((), (), s32[]{:S(2)}) async-start(), calls=%async_computation.3 | async-start | bytes 4259840 | tf_op jit(solution)/shard_map/all_gather | solution.py:43
  8.8 190.6 %reduce-scatter.2.cloned.1.call-start = ((), (), s32[]{:S(2)}) async-start(), calls=%async_computation.1 | async-start | bytes 5242880 | tf_op jit(solution)/shard_map/reduce_scatter | solution.py:29
  19.4 0.7 copy-start
Sparse Core Ops, SparseCore 0:
  11.3 103.9 all-gather.2
  118.5 76.0 all-gather.4
Sparse Core Ops, SparseCore 1:
  19.5 53.0 reduce-scatter.1
where the time goes:
time: 209 us
  waiting for transfers between devices  139 us (67%)
  matrix products  24.8 us (12%)
  blocking collectives  16.6 us (8%)
  between operations  14.9 us (7%)
  local copies, waits for them, and re-layouts  10.5 us (5%)
  other arithmetic  3.57 us (2%)
    all_gather x1, waiting for transfers between devices, on_device(): lax.all_gather(adapter_down_weight, 'dp', axis=0, tiled=True)  86.4 us
    all_gather x1, waiting for transfers between devices, on_device(): lax.all_gather(adapter_up_weight, 'dp', axis=0, tiled=True)  50.7 us
    psum x1, blocking collectives, on_device(): lax.psum(product.reshape(holder_count, row_capacity * adapter_rank_width)...  16.6 us
    dot_general x1, matrix products, on_device(): jnp.einsum('acd,ard->acr', send_buffer, lax.all_gather(adapter_down_weigh...  11.5 us
    dot_general x1, matrix products, on_device(): jnp.dot(tokens, frozen_key_value_weight, preferred_element_type=jnp.float32)  10.5 us
    scatter x1, local copies, waits for them, and re-layouts, on_device(): send_buffer = jnp.zeros((holder_count * row_capacity, feature_count), tok...  7.26 us
  transfers between devices with their start and end apart: 3, of which 2 were waited for; matrix products, arithmetic and copies ran while one was open for 17% of the time, Pallas kernels for 0%

commit v1 on v0

v1 whole, which is shorter than its diff:
```python
import functools

import jax
import jax.numpy as jnp
from jax import lax
from jax.experimental import pallas as pl
from jax.experimental.pallas import tpu as pltpu
from jax.sharding import Mesh, PartitionSpec as P

F32 = jnp.float32
BF16 = jnp.bfloat16
NZ, NY, NC, NX = 8, 4, 2, 4
GROUP = ("y", "core")
VMEM_LIMIT = 48 * 1024 * 1024
RELATIVE_Z = (0, -1, 1, -2, 2, -3, 3, -4)


def ring(size, step):
    return [(place, (place + step) % size) for place in range(size)]


def estimate(flops, moved):
    return pl.CostEstimate(flops=flops, bytes_accessed=moved, transcendentals=0)


def base_kernel(which, tokens, weight, out, total):
    step = pl.program_id(1)

    @pl.when(step == 0)
    def _():
        total[...] = jnp.zeros_like(total)

    total[...] += jnp.dot(tokens[...], weight[...], preferred_element_type=F32)

    @pl.when(step == pl.num_programs(1) - 1)
    def _():
        out[0] = total[...].astype(out.dtype)


def base_chunks(tokens, weight, which, dtype, depth=512):
    count, inner = tokens.shape
    width = weight.shape[1] // NX
    chunks = which.shape[0]
    return pl.pallas_call(
        base_kernel,
        out_shape=jax.ShapeDtypeStruct((chunks, count, width), dtype),
        grid_spec=pltpu.PrefetchScalarGridSpec(
            num_scalar_prefetch=1,
            grid=(chunks, inner // depth),
            in_specs=[
                pl.BlockSpec((count, depth), lambda j, k, w: (0, k)),
                pl.BlockSpec((depth, width), lambda j, k, w: (k, w[j])),
            ],
            out_specs=pl.BlockSpec((1, count, width), lambda j, k, w: (j, 0, 0)),
            scratch_shapes=[pltpu.VMEM((count, width), F32)],
        ),
        compiler_params=pltpu.CompilerParams(vmem_limit_bytes=VMEM_LIMIT),
        cost_estimate=estimate(2 * chunks * count * inner * width, 4 * chunks * inner * width),
        name="base",
    )(which, tokens, weight)


def down_kernel(chunks, first, last, starts, tokens, owner, *refs):
    panels, refs = refs[:chunks], refs[chunks:]
    if first:
        (out,) = refs
    else:
        before, out = refs
    value = tokens[0]
    named = owner[0]
    lane = lax.broadcasted_iota(jnp.int32, (1, 128), 1) // 64
    total = jnp.zeros((value.shape[0], 128), F32)
    if not first:
        total = before[0].astype(F32)
    for i in range(chunks):
        panel = panels[i][...].reshape(8 * 64, value.shape[1])
        product = lax.dot_general(
            value, panel, (((1,), (1,)), ((), ())), preferred_element_type=F32
        )
        for k in range(4):
            here = named == starts[i] + 2 * k + lane
            total = total + jnp.where(here, product[:, 128 * k : 128 * k + 128], 0.0)
    if last:
        total = total + pltpu.roll(total, 64, 1)
        half = total.shape[0] // 2
        total = jnp.where(lane == 0, total[:half], total[half:])
    out[0] = total.astype(out.dtype)


def down_step(starts, tokens, owner, panels, before, last):
    sources, count, width = tokens.shape
    chunks, first = len(panels), before is None
    rows = count // 2 if last else count
    state = [] if first else [before]
    return pl.pallas_call(
        functools.partial(down_kernel, chunks, first, last),
        out_shape=jax.ShapeDtypeStruct((sources, rows, 128), BF16),
        grid_spec=pltpu.PrefetchScalarGridSpec(
            num_scalar_prefetch=1,
            grid=(sources,),
            in_specs=[
                pl.BlockSpec((1, count, width), lambda s, w: (s, 0, 0)),
                pl.BlockSpec((1, count, 1), lambda s, w: (s, 0, 0)),
            ]
            + [pl.BlockSpec((8, 64, width), lambda s, w: (0, 0, 0))] * chunks
            + [pl.BlockSpec((1, count, 128), lambda s, w: (s, 0, 0))] * len(state),
            out_specs=pl.BlockSpec((1, rows, 128), lambda s, w: (s, 0, 0)),
        ),
        compiler_params=pltpu.CompilerParams(vmem_limit_bytes=VMEM_LIMIT),
        cost_estimate=estimate(
            2 * sources * count * width * 512 * chunks, 2 * sources * count * (width + 128)
        ),
        name="down",
    )(starts, tokens, owner, *panels, *state)


def up_kernel(numbers, owner, low, *refs):
    panels, (keep, fore_a, back_a, fore_b, back_b, out) = refs[: NY * NC], refs[NY * NC :]
    total = low[0].astype(F32)
    for i in range(1, NX):
        total = total + low[i].astype(F32)
    total = total.astype(BF16).astype(F32)
    lane = lax.broadcasted_iota(jnp.int32, (1, 128), 1)
    turned = pltpu.roll(total, 64, 1)
    both = jnp.concatenate(
        [jnp.where(lane < 64, total, turned), jnp.where(lane < 64, turned, total)], axis=0
    )
    named = owner[...]
    delta = jnp.zeros(out.shape, F32)
    for k in range(NY * NC):
        parts = []
        for m in range(NZ // 2):
            number = jnp.where(
                lane < 64, numbers[NZ * k + 2 * m], numbers[NZ * k + 2 * m + 1]
            )
            parts.append(jnp.where(named == number, both, 0.0).astype(BF16))
        left = jnp.concatenate(parts, axis=1)
        delta = delta + jnp.dot(left, panels[k][...], preferred_element_type=F32)
    delta = delta.astype(BF16).astype(F32)
    half = out.shape[0] // 2
    top = keep[:half] + fore_b[...].astype(F32) + back_a[...].astype(F32)
    bottom = keep[half:] + fore_a[...].astype(F32) + back_b[...].astype(F32)
    out[:half] = (top + delta[:half]).astype(out.dtype)
    out[half:] = (bottom + delta[half:]).astype(out.dtype)


def up_step(numbers, owner, low, panels, base):
    count = owner.shape[0]
    width = panels[0].shape[1]
    spec = pl.BlockSpec(memory_space=pltpu.VMEM)
    return pl.pallas_call(
        up_kernel,
        out_shape=jax.ShapeDtypeStruct((count, width), BF16),
        in_specs=[pl.BlockSpec(memory_space=pltpu.SMEM)] + [spec] * (2 + len(panels) + len(base)),
        out_specs=spec,
        compiler_params=pltpu.CompilerParams(vmem_limit_bytes=VMEM_LIMIT),
        cost_estimate=estimate(2 * count * width * 4096, 2 * width * 4096),
        name="up",
    )(numbers, owner, low, *panels, *base)


def z_ring(chunk):
    fore = back = chunk
    found = [chunk]
    for step in range(1, 5):
        fore = lax.ppermute(fore, "z", ring(NZ, 1))
        found.append(fore)
        if step < 4:
            back = lax.ppermute(back, "z", ring(NZ, -1))
            found.append(back)
    return found


def on_device(tokens, owner, weight, down, up):
    z, y, core, x = (lax.axis_index(name) for name in ("z", "y", "core", "x"))
    count, inner = tokens.shape
    size = NY * NC
    width = inner // size
    rank = down.shape[1]

    marks = jnp.zeros((16 * width,), BF16).at[:count].set(owner[:, 0].astype(BF16))
    marks = jnp.broadcast_to(marks.reshape(1, 16, width), (size, 16, width))
    spread = jnp.concatenate([down[0].reshape(rank, size, width).transpose(1, 0, 2), marks], axis=1)
    spread = lax.all_to_all(spread, GROUP, 0, 0, tiled=True)
    owners = spread[:, rank:].reshape(size, 16 * width)[:, :count, None].astype(jnp.int32)
    mine = spread[:, :rank]

    shared = tokens.reshape(count, size, width).transpose(1, 0, 2)
    shared = lax.all_to_all(shared, GROUP, 0, 0, tiled=True)

    two = base_chunks(tokens, weight, ((x + 2) % NX)[None], BF16)[0]
    rest = base_chunks(tokens, weight, jnp.stack([(x + 1) % NX, (x + 3) % NX, x]), F32)
    half = count // 2
    fore = lax.ppermute(two[:half], "x", ring(NX, 1))
    back = lax.ppermute(two[half:], "x", ring(NX, -1))
    fore_a = lax.ppermute(rest[0, half:].astype(BF16), "x", ring(NX, 1))
    back_a = lax.ppermute(rest[1, :half].astype(BF16), "x", ring(NX, -1))
    fore_b = lax.ppermute((rest[0, :half] + fore.astype(F32)).astype(BF16), "x", ring(NX, 1))
    back_b = lax.ppermute((rest[1, half:] + back.astype(F32)).astype(BF16), "x", ring(NX, -1))

    column = jnp.concatenate(z_ring(up[0]), axis=0)
    columns = [column] + [lax.ppermute(column, "y", ring(NY, -step)) for step in (1, 2, 3)]
    columns += [lax.ppermute(value, "core", ring(NC, 1)) for value in columns]
    numbers = jnp.stack(
        [
            ((z + dz) % NZ) * size + ((y + dy) % NY) * NC + (core + dc) % NC
            for dc in range(NC)
            for dy in range(NY)
            for dz in RELATIVE_Z
        ]
    )

    panels = z_ring(mine)
    starts = [((z + dz) % NZ) * size for dz in RELATIVE_Z]
    state = None
    for low, high in ((0, 1), (1, 3), (3, 5), (5, 7), (7, 8)):
        state = down_step(
            jnp.stack(starts[low:high]), shared, owners, panels[low:high], state, high == NZ
        )
    state = lax.all_to_all(state, GROUP, 0, 0, tiled=True)
    part = jnp.sum(state.astype(F32), axis=0).astype(BF16)
    parts = [part] + [lax.ppermute(part, "x", ring(NX, step)) for step in (1, 2, 3)]
    return up_step(
        numbers, owner, jnp.stack(parts), columns, (rest[2], fore_a, back_a, fore_b, back_b)
    )


def solution(mesh):
    fine = Mesh(mesh.devices.reshape(NZ, NY, NC, NX), ("z", "y", "core", "x"))
    dp = ("z", "y", "core")
    placed = (P(dp, "x"), P(dp, None), P("x", None), P(dp, None, "x"), P(dp, None, "x"))
    return jax.shard_map(
        on_device, mesh=fine, in_specs=placed, out_specs=P(dp, "x"), check_vma=False
    )
```

time: 209 us -> 182 us (0.87); the launches traced: 209 us -> 179 us
  waiting for transfers between devices: 139 us -> 41.2 us
  Pallas kernels: 0 us -> 54 us
  starting transfers between devices: 0.08 us -> 52.9 us
  matrix products: 24.8 us -> 0 us
  blocking collectives: 16.6 us -> 0 us
  between operations: 14.9 us -> 0.31 us
  local copies, waits for them, and re-layouts: 10.5 us -> 24.9 us
  other arithmetic: 3.57 us -> 5.94 us
    all_gather x2 -> x0, waiting for transfers between devices: 137 us -> none  [the longest x1 86.4 us: on_device(): lax.all_gather(adapter_down_weight, 'dp', axis=0, tiled=True)]
    pallas_call x0 -> x8, Pallas kernels: none -> 54 us  [the longest x5 33.7 us: down_step(): pl.pallas_call(functools.partial(down_kernel, chunks, first, last), out_s...]
    ppermute x0 -> x30, waiting for transfers between devices: none -> 36.8 us  [the longest x3 15 us: on_device(): lax.ppermute(column, 'y', ring(NY, -step))]
    ppermute x0 -> x30, starting transfers between devices: none -> 32.6 us  [the longest x6 11.6 us: z_ring(): back = lax.ppermute(back, 'z', ring(NZ, -1))]
    dot_general x3 -> x0, matrix products: 24.8 us -> none  [the longest x1 11.5 us: on_device(): jnp.einsum('acd,ard->acr', send_buffer, lax.all_gather(adapter_down_weigh...]
    all_to_all x0 -> x3, starting transfers between devices: none -> 20.2 us  [the longest x1 9.43 us: on_device(): state = lax.all_to_all(state, GROUP, 0, 0, tiled=True)]
    psum x1 -> x0, blocking collectives: 16.6 us -> none  [on_device(): lax.psum(product.reshape(holder_count, row_capacity * adapter_rank_width)...]
    unnamed x2 -> x38, local copies, waits for them, and re-layouts: 0.66 us -> 14.2 us
  transfers between devices with their start and end apart: 3 -> 33, of which waited for: 2 -> 9; matrix products, arithmetic and copies ran while one was open for 17% -> 14% of each run, Pallas kernels for 0% -> 27%
where the time goes in v1:
time: 182 us; the launch traced here: 179 us
  Pallas kernels  54 us (30%)
  starting transfers between devices  52.9 us (29%)
  waiting for transfers between devices  41.2 us (23%)
  local copies, waits for them, and re-layouts  24.9 us (14%)
  other arithmetic  5.94 us (3%)
    pallas_call x5, Pallas kernels, down_step(): pl.pallas_call(functools.partial(down_kernel, chunks, first, last), out_s...  33.7 us
    ppermute x3, waiting for transfers between devices, on_device(): lax.ppermute(column, 'y', ring(NY, -step))  15 us
    pallas_call x2, Pallas kernels, base_chunks(): pl.pallas_call(base_kernel, out_shape=jax.ShapeDtypeStruct((chunks, count...  14.5 us
    unnamed x38, local copies, waits for them, and re-layouts  14.2 us
    ppermute x8, waiting for transfers between devices, z_ring(): fore = lax.ppermute(fore, 'z', ring(NZ, 1))  11.9 us
    ppermute x6, starting transfers between devices, z_ring(): back = lax.ppermute(back, 'z', ring(NZ, -1))  11.6 us
    all_to_all x1, starting transfers between devices, on_device(): state = lax.all_to_all(state, GROUP, 0, 0, tiled=True)  9.43 us
    pallas_call x1, Pallas kernels, up_step(): pl.pallas_call(up_kernel, out_shape=jax.ShapeDtypeStruct((count, width),...  5.83 us
  transfers between devices with their start and end apart: 33, of which 9 were waited for; matrix products, arithmetic and copies ran while one was open for 14% of the time, Pallas kernels for 27%

profile of v1, /device:TPU:1, one launch (start us, length us, event | category | flops | bytes accessed | tf_op | source)
XLA Modules:
  0.0 179.2 jit_solution(3006515907120483587)
XLA Ops:
  2.5 4.0 %collective-permute-start.11 = (bf16[64,512]{1,0:T(8,128)(2,1)}, bf16[64,512]{1,0:T(8,128)(2,1)S(1)}, u32[]{:S(2)}, u32[]{:S(2)}) collective-permute-start(bf16[64,512]{1,0:T(8,128)(2,1)} %bitcast.128), channel_id=1, source_target_pairs={{0,224},{32,0},{64,32},{96,64},{128,96},{160,128},{192,160},{224,1... | collective-permute-start | bytes 196616 | tf_op jit(solution)/shard_map/ppermute | solution.py:169
  9.0 5.4 %all-to-all-start.1 = ((bf16[8,80,256]{2,1,0:T(8,128)(2,1)}), bf16[8,80,256]{2,1,0:T(8,128)(2,1)}, u32[]{:S(2)}, u32[]{:S(2)}) async-start(bf16[8,80,256]{2,1,0:T(8,128)(2,1)} %pad_maximum_fusion), calls=%async_computation.1 | async-start | bytes 655360 | tf_op jit(solution)/shard_map/all_to_all | solution.py:184
  14.5 3.7 %base.3 = bf16[1,512,512]{2,1,0:T(8,128)(2,1)S(1)} custom-call(s32[1]{0:T(128)} %bitcast.88.which, bf16[512,2048]{1,0:T(8,128)(2,1)S(1)} %copy-done.2, bf16[2048,2048]{1,0:T(8,128)(2,1)} %weight.3), custom_call_target="tpu_custom_call" | custom-call | flops 1073741824 | bytes 4194304 | tf_op jit(solution)/shard_map/base/pallas_call | solution.py:44
  24.3 3.9 %copy.8 = bf16[512,8,256]{2,0,1:T(8,128)(2,1)} copy(bf16[512,8,256]{0,2,1:T(8,128)(2,1)} %bitcast.121) | data formatting | bytes 4194304 | tf_op jit(solution)/shard_map/reshape | solution.py:188
  30.0 10.8 %base.2 = f32[3,512,512]{2,1,0:T(8,128)S(1)} custom-call(s32[3]{0:T(128)S(1)} %pad_add_fusion.3.which, bf16[512,2048]{1,0:T(8,128)(2,1)S(1)} %copy-done.3, bf16[2048,2048]{1,0:T(8,128)(2,1)} %weight.3), custom_call_target="tpu_custom_call" | custom-call | flops 3221225472 | bytes 12582912 | tf_op jit(solution)/shard_map/base/pallas_call | solution.py:44
  40.8 5.4 %all-to-all-start = ((bf16[8,512,256]{2,1,0:T(8,128)(2,1)}), bf16[8,512,256]{2,1,0:T(8,128)(2,1)}, u32[]{:S(2)}, u32[]{:S(2)}) async-start(bf16[8,512,256]{2,1,0:T(8,128)(2,1)} %bitcast.120), calls=%async_computation | async-start | bytes 4194304 | tf_op jit(solution)/shard_map/all_to_all | solution.py:189
  53.7 2.7 %collective-permute-start.15 = (bf16[64,512]{1,0:T(8,128)(2,1)S(1)}, bf16[64,512]{1,0:T(8,128)(2,1)S(1)}, u32[]{:S(2)}, u32[]{:S(2)}) collective-permute-start(bf16[64,512]{1,0:T(8,128)(2,1)S(1)} %collective-permute-done.13), channel_id=1, source_target_pairs={{0,224},{32,0},{64,32},{96,64},{128,96},{160,128},{192,160},{224,1... | collective-permute-start | bytes 196616 | tf_op jit(solution)/shard_map/ppermute | solution.py:169
  57.6 5.4 %collective-permute-done.14 = bf16[64,512]{1,0:T(8,128)(2,1)S(1)} collective-permute-done((bf16[64,512]{1,0:T(8,128)(2,1)S(1)}, bf16[64,512]{1,0:T(8,128)(2,1)S(1)}, u32[]{:S(2)}, u32[]{:S(2)}) %collective-permute-start.14) | collective-permute-done | bytes 65568 | tf_op jit(solution)/shard_map/ppermute | solution.py:166
  65.8 6.5 %collective-permute-done.16 = bf16[64,512]{1,0:T(8,128)(2,1)S(1)} collective-permute-done((bf16[64,512]{1,0:T(8,128)(2,1)S(1)}, bf16[64,512]{1,0:T(8,128)(2,1)S(1)}, u32[]{:S(2)}, u32[]{:S(2)}) %collective-permute-start.16) | collective-permute-done | bytes 65568 | tf_op jit(solution)/shard_map/ppermute | solution.py:166
  82.1 5.6 %down.5.refs_2_ = bf16[8,512,128]{2,1,0:T(8,128)(2,1)S(1)} custom-call(s32[1]{0:T(128)} %bitcast.75.starts, bf16[8,512,256]{2,1,0:T(8,128)(2,1)} %all-to-all-done.tokens, s32[8,512,1]{2,1,0:T(8,128)S(1)} %copy-done, bf16[8,64,256]{2,1,0:T(8,128)(2,1)S(1)} %slice.63.refs_0_), custom_call_target="tpu_custom_call" | custom-call | flops 1073741824 | bytes 3145728 | tf_op jit(solution)/shard_map/down/pallas_call | solution.py:95
  87.7 7.3 %down.6.refs_2_ = bf16[8,512,128]{2,1,0:T(8,128)(2,1)S(1)} custom-call(s32[2]{0:T(128)S(1)} %pad_add_fusion.2.starts, bf16[8,512,256]{2,1,0:T(8,128)(2,1)} %all-to-all-done.tokens, s32[8,512,1]{2,1,0:T(8,128)} %copy.14.owner, bf16[8,64,256]{2,1,0:T(8,128)(2,1)S(1)} %copy-done.8, bf16[8,64,256]{2,1,0:T(8,128)(2,1)} %collective-permute-done.4.refs_1_, ...), custom_call_target="tpu_custom_call" | custom-call | flops 2147483648 | bytes 3145728 | tf_op jit(solution)/shard_map/down/pallas_call | solution.py:95
  95.0 7.4 %down.7.refs_2_ = bf16[8,512,128]{2,1,0:T(8,128)(2,1)S(1)} custom-call(s32[2]{0:T(128)S(1)} %pad_add_fusion.1.starts, bf16[8,512,256]{2,1,0:T(8,128)(2,1)} %all-to-all-done.tokens, s32[8,512,1]{2,1,0:T(8,128)} %copy.14.owner, bf16[8,64,256]{2,1,0:T(8,128)(2,1)} %collective-permute-done.1.refs_0_, bf16[8,64,256]{2,1,0:T(8,128)(2,1)} %collective-permute-done.5.refs_1_, ...), custom_call_target="tpu_custom_call" | custom-call | flops 2147483648 | bytes 3145728 | tf_op jit(solution)/shard_map/down/pallas_call | solution.py:95
  102.4 2.8 %collective-permute-start.25 = (bf16[256,512]{1,0:T(8,128)(2,1)}, bf16[256,512]{1,0:T(8,128)(2,1)S(1)}, u32[]{:S(2)}, u32[]{:S(2)}) collective-permute-start(bf16[256,512]{1,0:T(8,128)(2,1)} %get-tuple-element.19), channel_id=1, source_target_pairs={{0,3},{1,0},{2,1},{3,2},{4,7},{5,4},{6,5},{7,6},{8,11},{9,8},{10,9... | collective-permute-start | bytes 786440 | tf_op jit(solution)/shard_map/ppermute | solution.py:197
  105.1 7.4 %down.8.refs_1_ = bf16[8,512,128]{2,1,0:T(8,128)(2,1)S(1)} custom-call(s32[2]{0:T(128)S(1)} %pad_add_fusion.starts, bf16[8,512,256]{2,1,0:T(8,128)(2,1)} %all-to-all-done.tokens, s32[8,512,1]{2,1,0:T(8,128)} %copy.14.owner, bf16[8,64,256]{2,1,0:T(8,128)(2,1)} %collective-permute-done.2.refs_0_, bf16[8,64,256]{2,1,0:T(8,128)(2,1)} %collective-permute-done.6.refs_1_, ...), custom_call_target="tpu_custom_call" | custom-call | flops 2147483648 | bytes 3145728 | tf_op jit(solution)/shard_map/down/pallas_call | solution.py:95
  114.2 6.0 %down.9 = bf16[8,256,128]{2,1,0:T(8,128)(2,1)S(1)} custom-call(s32[1]{0:T(128)} %bitcast.64.starts, bf16[8,512,256]{2,1,0:T(8,128)(2,1)} %all-to-all-done.tokens, s32[8,512,1]{2,1,0:T(8,128)S(1)} %copy-done.1, bf16[8,64,256]{2,1,0:T(8,128)(2,1)} %collective-permute-done.3.refs_0_, bf16[8,512,128]{2,1,0:T(8,128)(2,1)S(1)} %down.8.refs_1_), custom_call_target="tpu_custom_call" | custom-call | flops 1073741824 | bytes 3145728 | tf_op jit(solution)/shard_map/down/pallas_call | solution.py:95
  121.0 9.4 %all-to-all-start.2 = ((bf16[8,256,128]{2,1,0:T(8,128)(2,1)}), bf16[8,256,128]{2,1,0:T(8,128)(2,1)}, u32[]{:S(2)}, u32[]{:S(2)}) async-start(bf16[8,256,128]{2,1,0:T(8,128)(2,1)} %copy-done.4), calls=%async_computation.2 | async-start | bytes 1048576 | tf_op jit(solution)/shard_map/all_to_all | solution.py:220
  130.4 2.9 %collective-permute-start.18 = (bf16[512,512]{1,0:T(8,128)(2,1)}, bf16[512,512]{1,0:T(8,128)(2,1)}, u32[]{:S(2)}, u32[]{:S(2)}) collective-permute-start(bf16[512,512]{1,0:T(8,128)(2,1)} %constant_dynamic-update-slice_fusion.refs_0_), channel_id=1, source_target_pairs={{0,16},{8,24},{16,0},{24,8},{1,17},{9,25},{17,1},{25,9},{2,18},{10... | collective-permute-start | bytes 1572872 | tf_op jit(solution)/shard_map/ppermute | solution.py:202
  135.6 4.4 %all-to-all-done.2 = bf16[8,256,128]{2,1,0:T(8,128)(2,1)} async-done(((bf16[8,256,128]{2,1,0:T(8,128)(2,1)}), bf16[8,256,128]{2,1,0:T(8,128)(2,1)}, u32[]{:S(2)}, u32[]{:S(2)}) %all-to-all-start.2) | async-done | bytes 524320 | tf_op jit(solution)/shard_map/all_to_all | solution.py:220
  141.3 2.7 %collective-permute-done.27.refs_11_ = bf16[256,512]{1,0:T(8,128)(2,1)} collective-permute-done((bf16[256,512]{1,0:T(8,128)(2,1)}, bf16[256,512]{1,0:T(8,128)(2,1)}, u32[]{:S(2)}, u32[]{:S(2)}) %collective-permute-start.27) | collective-permute-done | bytes 262176 | tf_op jit(solution)/shard_map/ppermute | solution.py:198
  146.0 5.3 %collective-permute-done.18.refs_2_ = bf16[512,512]{1,0:T(8,128)(2,1)} collective-permute-done((bf16[512,512]{1,0:T(8,128)(2,1)}, bf16[512,512]{1,0:T(8,128)(2,1)}, u32[]{:S(2)}, u32[]{:S(2)}) %collective-permute-start.18) | collective-permute-done | bytes 524320 | tf_op jit(solution)/shard_map/ppermute | solution.py:202
  152.7 9.7 %collective-permute-done.19.refs_3_ = bf16[512,512]{1,0:T(8,128)(2,1)} collective-permute-done((bf16[512,512]{1,0:T(8,128)(2,1)}, bf16[512,512]{1,0:T(8,128)(2,1)}, u32[]{:S(2)}, u32[]{:S(2)}) %collective-permute-start.19) | collective-permute-done | bytes 524320 | tf_op jit(solution)/shard_map/ppermute | solution.py:202
  164.2 2.8 %collective-permute-done.9 = bf16[256,128]{1,0:T(8,128)(2,1)} collective-permute-done((bf16[256,128]{1,0:T(8,128)(2,1)S(1)}, bf16[256,128]{1,0:T(8,128)(2,1)}, u32[]{:S(2)}, u32[]{:S(2)}) %collective-permute-start.9) | collective-permute-done | bytes 65568 | tf_op jit(solution)/shard_map/ppermute | solution.py:222
  170.2 3.1 %collective-permute-done.29.refs_12_ = bf16[256,512]{1,0:T(8,128)(2,1)S(1)} collective-permute-done((bf16[256,512]{1,0:T(8,128)(2,1)}, bf16[256,512]{1,0:T(8,128)(2,1)S(1)}, u32[]{:S(2)}, u32[]{:S(2)}) %collective-permute-start.29) | collective-permute-done | bytes 262176 | tf_op jit(solution)/shard_map/ppermute | solution.py:199
  173.4 5.8 %up.1 = bf16[512,512]{1,0:T(8,128)(2,1)} custom-call(s32[64]{0:T(128)S(1)} %stack.319.numbers, s32[512,1]{1,0:T(8,128)S(1)} %copy.15.owner, bf16[4,256,128]{2,1,0:T(8,128)(2,1)S(1)} %pad_maximum_fusion.1.low, bf16[512,512]{1,0:T(8,128)(2,1)} %constant_dynamic-update-slice_fusion.refs_0_, bf16[512,512]{1,0:T(8,128)(2,1)} %collective-permute-done.17.refs_1_, ...), custom_call_target="tpu_custom_call" | custom-call | flops 2147483648 | bytes 4194304 | tf_op jit(solution)/shard_map/up/pallas_call | solution.py:151
  (111 shorter events, 48.4 us)
Async XLA Ops:
  0.0 48.6 %collective-permute-start.10 = (bf16[64,512]{1,0:T(8,128)(2,1)}, bf16[64,512]{1,0:T(8,128)(2,1)S(1)}, u32[]{:S(2)}, u32[]{:S(2)}) collective-permute-start(bf16[64,512]{1,0:T(8,128)(2,1)} %bitcast.127), channel_id=1, source_target_pairs={{0,32},{32,64},{64,96},{96,128},{128,160},{160,192},{192,224},{224... | collective-permute-start | bytes 196616 | tf_op jit(solution)/shard_map/ppermute | solution.py:166
  2.5 46.2 %collective-permute-start.11 = (bf16[64,512]{1,0:T(8,128)(2,1)}, bf16[64,512]{1,0:T(8,128)(2,1)S(1)}, u32[]{:S(2)}, u32[]{:S(2)}) collective-permute-start(bf16[64,512]{1,0:T(8,128)(2,1)} %bitcast.128), channel_id=1, source_target_pairs={{0,224},{32,0},{64,32},{96,64},{128,96},{160,128},{192,160},{224,1... | collective-permute-start | bytes 196616 | tf_op jit(solution)/shard_map/ppermute | solution.py:169
  9.0 31.7 %all-to-all-start.1 = ((bf16[8,80,256]{2,1,0:T(8,128)(2,1)}), bf16[8,80,256]{2,1,0:T(8,128)(2,1)}, u32[]{:S(2)}, u32[]{:S(2)}) async-start(bf16[8,80,256]{2,1,0:T(8,128)(2,1)} %pad_maximum_fusion), calls=%async_computation.1 | async-start | bytes 655360 | tf_op jit(solution)/shard_map/all_to_all | solution.py:184
  19.1 111.4 %collective-permute-start.26 = (bf16[256,512]{1,0:T(8,128)(2,1)}, bf16[256,512]{1,0:T(8,128)(2,1)}, u32[]{:S(2)}, u32[]{:S(2)}) collective-permute-start(bf16[256,512]{1,0:T(8,128)(2,1)} %get-tuple-element.22), channel_id=1, source_target_pairs={{0,1},{1,2},{2,3},{3,0},{4,5},{5,6},{6,7},{7,4},{8,9},{9,10},{10,1... | collective-permute-start | bytes 786440 | tf_op jit(solution)/shard_map/ppermute | solution.py:194
  20.3 113.1 %collective-permute-start.28 = (bf16[256,512]{1,0:T(8,128)(2,1)}, bf16[256,512]{1,0:T(8,128)(2,1)}, u32[]{:S(2)}, u32[]{:S(2)}) collective-permute-start(bf16[256,512]{1,0:T(8,128)(2,1)} %get-tuple-element.21), channel_id=1, source_target_pairs={{0,3},{1,0},{2,1},{3,2},{4,7},{5,4},{6,5},{7,6},{8,11},{9,8},{10,9... | collective-permute-start | bytes 786440 | tf_op jit(solution)/shard_map/ppermute | solution.py:195
  40.8 39.7 %all-to-all-start = ((bf16[8,512,256]{2,1,0:T(8,128)(2,1)}), bf16[8,512,256]{2,1,0:T(8,128)(2,1)}, u32[]{:S(2)}, u32[]{:S(2)}) async-start(bf16[8,512,256]{2,1,0:T(8,128)(2,1)} %bitcast.120), calls=%async_computation | async-start | bytes 4194304 | tf_op jit(solution)/shard_map/all_to_all | solution.py:189
  52.9 10.1 %collective-permute-start = (bf16[8,64,256]{2,1,0:T(8,128)(2,1)S(1)}, bf16[8,64,256]{2,1,0:T(8,128)(2,1)S(1)}, u32[]{:S(2)}, u32[]{:S(2)}) collective-permute-start(bf16[8,64,256]{2,1,0:T(8,128)(2,1)S(1)} %slice.63.refs_0_), channel_id=1, source_target_pairs={{0,32},{32,64},{64,96},{96,128},{128,160},{160,192},{192,224},{224... | collective-permute-start | bytes 786440 | tf_op jit(solution)/shard_map/ppermute | solution.py:166
  53.7 11.4 %collective-permute-start.15 = (bf16[64,512]{1,0:T(8,128)(2,1)S(1)}, bf16[64,512]{1,0:T(8,128)(2,1)S(1)}, u32[]{:S(2)}, u32[]{:S(2)}) collective-permute-start(bf16[64,512]{1,0:T(8,128)(2,1)S(1)} %collective-permute-done.13), channel_id=1, source_target_pairs={{0,224},{32,0},{64,32},{96,64},{128,96},{160,128},{192,160},{224,1... | collective-permute-start | bytes 196616 | tf_op jit(solution)/shard_map/ppermute | solution.py:169
  63.0 9.9 %collective-permute-start.4 = (bf16[8,64,256]{2,1,0:T(8,128)(2,1)S(1)}, bf16[8,64,256]{2,1,0:T(8,128)(2,1)}, u32[]{:S(2)}, u32[]{:S(2)}) collective-permute-start(bf16[8,64,256]{2,1,0:T(8,128)(2,1)S(1)} %slice.63.refs_0_), channel_id=1, source_target_pairs={{0,224},{32,0},{64,32},{96,64},{128,96},{160,128},{192,160},{224,1... | collective-permute-start | bytes 786440 | tf_op jit(solution)/shard_map/ppermute | solution.py:169
  63.0 10.2 %collective-permute-start.1 = (bf16[8,64,256]{2,1,0:T(8,128)(2,1)S(1)}, bf16[8,64,256]{2,1,0:T(8,128)(2,1)}, u32[]{:S(2)}, u32[]{:S(2)}) collective-permute-start(bf16[8,64,256]{2,1,0:T(8,128)(2,1)S(1)} %collective-permute-done.refs_0_), channel_id=1, source_target_pairs={{0,32},{32,64},{64,96},{96,128},{128,160},{160,192},{192,224},{224... | collective-permute-start | bytes 786440 | tf_op jit(solution)/shard_map/ppermute | solution.py:166
  72.3 63.3 %collective-permute-start.24 = (bf16[256,512]{1,0:T(8,128)(2,1)}, bf16[256,512]{1,0:T(8,128)(2,1)}, u32[]{:S(2)}, u32[]{:S(2)}) collective-permute-start(bf16[256,512]{1,0:T(8,128)(2,1)} %get-tuple-element.20), channel_id=1, source_target_pairs={{0,1},{1,2},{2,3},{3,0},{4,5},{5,6},{6,7},{7,4},{8,9},{9,10},{10,1... | collective-permute-start | bytes 786440 | tf_op jit(solution)/shard_map/ppermute | solution.py:196
  78.5 23.9 %collective-permute-start.6 = (bf16[8,64,256]{2,1,0:T(8,128)(2,1)}, bf16[8,64,256]{2,1,0:T(8,128)(2,1)}, u32[]{:S(2)}, u32[]{:S(2)}) collective-permute-start(bf16[8,64,256]{2,1,0:T(8,128)(2,1)} %collective-permute-done.5.refs_1_), channel_id=1, source_target_pairs={{0,224},{32,0},{64,32},{96,64},{128,96},{160,128},{192,160},{224,1... | collective-permute-start | bytes 786440 | tf_op jit(solution)/shard_map/ppermute | solution.py:169
  80.5 32.1 %collective-permute-start.3 = (bf16[8,64,256]{2,1,0:T(8,128)(2,1)}, bf16[8,64,256]{2,1,0:T(8,128)(2,1)}, u32[]{:S(2)}, u32[]{:S(2)}) collective-permute-start(bf16[8,64,256]{2,1,0:T(8,128)(2,1)} %collective-permute-done.2.refs_0_), channel_id=1, source_target_pairs={{0,32},{32,64},{64,96},{96,128},{128,160},{160,192},{192,224},{224... | collective-permute-start | bytes 786440 | tf_op jit(solution)/shard_map/ppermute | solution.py:166
  102.4 38.8 %collective-permute-start.25 = (bf16[256,512]{1,0:T(8,128)(2,1)}, bf16[256,512]{1,0:T(8,128)(2,1)S(1)}, u32[]{:S(2)}, u32[]{:S(2)}) collective-permute-start(bf16[256,512]{1,0:T(8,128)(2,1)} %get-tuple-element.19), channel_id=1, source_target_pairs={{0,3},{1,0},{2,1},{3,2},{4,7},{5,4},{6,5},{7,6},{8,11},{9,8},{10,9... | collective-permute-start | bytes 786440 | tf_op jit(solution)/shard_map/ppermute | solution.py:197
  112.5 31.5 %collective-permute-start.17 = (bf16[512,512]{1,0:T(8,128)(2,1)}, bf16[512,512]{1,0:T(8,128)(2,1)}, u32[]{:S(2)}, u32[]{:S(2)}) collective-permute-start(bf16[512,512]{1,0:T(8,128)(2,1)} %constant_dynamic-update-slice_fusion.refs_0_), channel_id=1, source_target_pairs={{0,24},{8,0},{16,8},{24,16},{1,25},{9,1},{17,9},{25,17},{2,26},{10... | collective-permute-start | bytes 1572872 | tf_op jit(solution)/shard_map/ppermute | solution.py:202
  121.0 19.1 %all-to-all-start.2 = ((bf16[8,256,128]{2,1,0:T(8,128)(2,1)}), bf16[8,256,128]{2,1,0:T(8,128)(2,1)}, u32[]{:S(2)}, u32[]{:S(2)}) async-start(bf16[8,256,128]{2,1,0:T(8,128)(2,1)} %copy-done.4), calls=%async_computation.2 | async-start | bytes 1048576 | tf_op jit(solution)/shard_map/all_to_all | solution.py:220
  130.4 20.9 %collective-permute-start.18 = (bf16[512,512]{1,0:T(8,128)(2,1)}, bf16[512,512]{1,0:T(8,128)(2,1)}, u32[]{:S(2)}, u32[]{:S(2)}) collective-permute-start(bf16[512,512]{1,0:T(8,128)(2,1)} %constant_dynamic-update-slice_fusion.refs_0_), channel_id=1, source_target_pairs={{0,16},{8,24},{16,0},{24,8},{1,17},{9,25},{17,1},{25,9},{2,18},{10... | collective-permute-start | bytes 1572872 | tf_op jit(solution)/shard_map/ppermute | solution.py:202
  133.4 29.0 %collective-permute-start.19 = (bf16[512,512]{1,0:T(8,128)(2,1)}, bf16[512,512]{1,0:T(8,128)(2,1)}, u32[]{:S(2)}, u32[]{:S(2)}) collective-permute-start(bf16[512,512]{1,0:T(8,128)(2,1)} %constant_dynamic-update-slice_fusion.refs_0_), channel_id=1, source_target_pairs={{0,8},{8,16},{16,24},{24,0},{1,9},{9,17},{17,25},{25,1},{2,10},{10... | collective-permute-start | bytes 1572872 | tf_op jit(solution)/shard_map/ppermute | solution.py:202
  141.2 21.9 %collective-permute-start.7 = (bf16[256,128]{1,0:T(8,128)(2,1)S(1)}, bf16[256,128]{1,0:T(8,128)(2,1)S(1)}, u32[]{:S(2)}, u32[]{:S(2)}) collective-permute-start(bf16[256,128]{1,0:T(8,128)(2,1)S(1)} %reduce_sum.12), channel_id=1, source_target_pairs={{0,1},{1,2},{2,3},{3,0},{4,5},{5,6},{6,7},{7,4},{8,9},{9,10},{10,1... | collective-permute-start | bytes 196616 | tf_op jit(solution)/shard_map/ppermute | solution.py:222
  144.1 19.1 %collective-permute-start.8 = (bf16[256,128]{1,0:T(8,128)(2,1)S(1)}, bf16[256,128]{1,0:T(8,128)(2,1)S(1)}, u32[]{:S(2)}, u32[]{:S(2)}) collective-permute-start(bf16[256,128]{1,0:T(8,128)(2,1)S(1)} %reduce_sum.12), channel_id=1, source_target_pairs={{0,2},{1,3},{2,0},{3,1},{4,6},{5,7},{6,4},{7,5},{8,10},{9,11},{10,... | collective-permute-start | bytes 196616 | tf_op jit(solution)/shard_map/ppermute | solution.py:222
  144.1 29.3 %collective-permute-start.20 = (bf16[512,512]{1,0:T(8,128)(2,1)}, bf16[512,512]{1,0:T(8,128)(2,1)}, u32[]{:S(2)}, u32[]{:S(2)}) collective-permute-start(bf16[512,512]{1,0:T(8,128)(2,1)} %constant_dynamic-update-slice_fusion.refs_0_), channel_id=1, source_target_pairs={{0,4},{4,0},{1,5},{5,1},{2,6},{6,2},{3,7},{7,3},{8,12},{12,8},{9,1... | collective-permute-start | bytes 1572872 | tf_op jit(solution)/shard_map/ppermute | solution.py:203
  151.3 22.0 %collective-permute-start.21 = (bf16[512,512]{1,0:T(8,128)(2,1)}, bf16[512,512]{1,0:T(8,128)(2,1)}, u32[]{:S(2)}, u32[]{:S(2)}) collective-permute-start(bf16[512,512]{1,0:T(8,128)(2,1)} %collective-permute-done.17.refs_1_), channel_id=1, source_target_pairs={{0,4},{4,0},{1,5},{5,1},{2,6},{6,2},{3,7},{7,3},{8,12},{12,8},{9,1... | collective-permute-start | bytes 1572872 | tf_op jit(solution)/shard_map/ppermute | solution.py:203
  162.3 11.0 %collective-permute-start.22 = (bf16[512,512]{1,0:T(8,128)(2,1)}, bf16[512,512]{1,0:T(8,128)(2,1)}, u32[]{:S(2)}, u32[]{:S(2)}) collective-permute-start(bf16[512,512]{1,0:T(8,128)(2,1)} %collective-permute-done.18.refs_2_), channel_id=1, source_target_pairs={{0,4},{4,0},{1,5},{5,1},{2,6},{6,2},{3,7},{7,3},{8,12},{12,8},{9,1... | collective-permute-start | bytes 1572872 | tf_op jit(solution)/shard_map/ppermute | solution.py:203
  163.1 10.2 %collective-permute-start.23 = (bf16[512,512]{1,0:T(8,128)(2,1)}, bf16[512,512]{1,0:T(8,128)(2,1)}, u32[]{:S(2)}, u32[]{:S(2)}) collective-permute-start(bf16[512,512]{1,0:T(8,128)(2,1)} %collective-permute-done.19.refs_3_), channel_id=1, source_target_pairs={{0,4},{4,0},{1,5},{5,1},{2,6},{6,2},{3,7},{7,3},{8,12},{12,8},{9,1... | collective-permute-start | bytes 1572872 | tf_op jit(solution)/shard_map/ppermute | solution.py:203
  (22 other events, 184.4 us)

commit v2 on v0

v2 whole, which is shorter than its diff:
```python
import jax
import jax.numpy as jnp
from jax import lax
from jax.experimental import pallas as pl
from jax.experimental.pallas import tpu as pltpu
from jax.sharding import Mesh, PartitionSpec as P

F32 = jnp.float32
BF16 = jnp.bfloat16
NZ, NY, NC, NX = 8, 4, 2, 4
COLUMNS = NY * NC
CAP = 16
GROUP = ("y", "core")
VMEM_LIMIT = 48 * 1024 * 1024
RELATIVE_Z = (0, -1, 1, -2, 2, -3, 3, -4)


def ring(size, step):
    return [(place, (place + step) % size) for place in range(size)]


def call(kernel, name, out, grid, ins, outs, flops, moved, prefetch=0, scratch=()):
    return pl.pallas_call(
        kernel,
        out_shape=out,
        grid_spec=pltpu.PrefetchScalarGridSpec(
            num_scalar_prefetch=prefetch,
            grid=grid,
            in_specs=ins,
            out_specs=outs,
            scratch_shapes=scratch,
        ),
        compiler_params=pltpu.CompilerParams(vmem_limit_bytes=VMEM_LIMIT),
        cost_estimate=pl.CostEstimate(flops=flops, bytes_accessed=moved, transcendentals=0),
        name=name,
    )


def base_kernel(which, tokens, weight, out):
    out[0] = jnp.dot(tokens[...], weight[...], preferred_element_type=F32).astype(out.dtype)


def base_chunks(tokens, weight, which, dtype, tile=256):
    count, inner = tokens.shape
    width = weight.shape[1] // NX
    chunks = which.shape[0]
    tiles = width // tile
    return call(
        base_kernel,
        "base",
        jax.ShapeDtypeStruct((chunks, count, width), dtype),
        (chunks, tiles),
        [
            pl.BlockSpec((count, inner), lambda j, n, w: (0, 0)),
            pl.BlockSpec((inner, tile), lambda j, n, w: (0, w[j] * tiles + n)),
        ],
        pl.BlockSpec((1, count, tile), lambda j, n, w: (j, 0, n)),
        2 * chunks * count * inner * width,
        2 * (count + chunks * width) * inner,
        prefetch=1,
    )(which, tokens, weight)


def dispatch_kernel(named, owner, tokens, out, place):
    count = tokens.shape[0]

    @pl.when(pl.program_id(0) == 0)
    def _():
        mine = owner[...]
        above = lax.broadcasted_iota(jnp.int32, (count, count), 0)
        below = lax.broadcasted_iota(jnp.int32, (count, count), 1)
        earlier = (named[...] == mine) & (above < below)
        position = jnp.sum(earlier.astype(jnp.int32), axis=0, keepdims=True)
        place[...] = (mine % COLUMNS) * (NZ * CAP) + (mine // COLUMNS) * CAP + position

    rows = out.shape[1]
    slot = lax.broadcasted_iota(jnp.int32, (rows, count), 0) + pl.program_id(0) * rows
    chosen = (slot == place[...]).astype(BF16)
    out[0] = jnp.dot(chosen, tokens[...], preferred_element_type=F32).astype(BF16)


def dispatch(tokens, owner):
    count, inner = tokens.shape
    rows = NZ * CAP
    return call(
        dispatch_kernel,
        "dispatch",
        jax.ShapeDtypeStruct((COLUMNS, rows, inner), BF16),
        (COLUMNS,),
        [
            pl.BlockSpec((count, 1), lambda d: (0, 0)),
            pl.BlockSpec((1, count), lambda d: (0, 0)),
            pl.BlockSpec((count, inner), lambda d: (0, 0)),
        ],
        pl.BlockSpec((1, rows, inner), lambda d: (d, 0, 0)),
        2 * COLUMNS * rows * count * inner,
        2 * (count + COLUMNS * rows) * inner,
        scratch=[pltpu.VMEM((1, count), jnp.int32)],
    )(owner, owner.reshape(1, count), tokens)


def down_kernel(order, rows, *refs):
    panels, out = refs[:NZ], refs[NZ]
    inner = rows.shape[2]
    value = rows[...].reshape(COLUMNS * CAP, inner)
    for i in range(NZ):

        @pl.when(pl.program_id(0) == i)
        def _():
            product = lax.dot_general(
                value,
                panels[i][:, :inner],
                (((1,), (1,)), ((), ())),
                preferred_element_type=F32,
            )
            half = product.shape[0] // 2
            out[0] = jnp.concatenate([product[:half], product[half:]], axis=1).astype(BF16)


def down_step(order, rows, panels):
    inner = rows.shape[2]
    rank, wide = panels[0].shape
    lines = COLUMNS * CAP // 2
    return call(
        down_kernel,
        "down",
        jax.ShapeDtypeStruct((NZ, lines, 2 * rank), BF16),
        (NZ,),
        [pl.BlockSpec((COLUMNS, CAP, inner), lambda i, o: (0, o[i], 0))]
        + [pl.BlockSpec((rank, wide), lambda i, o: (0, 0))] * NZ,
        pl.BlockSpec((1, lines, 2 * rank), lambda i, o: (i, 0, 0)),
        4 * NZ * lines * inner * rank,
        2 * NZ * (2 * lines + rank) * inner,
        prefetch=1,
    )(order, rows, *panels)


def up_kernel(order, *refs):
    parts, panels, out = refs[:NX], refs[NX : NX + NZ], refs[NX + NZ]
    total = parts[0][0].astype(F32)
    for part in parts[1:]:
        total = total + part[0].astype(F32)
    rank = total.shape[1] // 2
    low = jnp.concatenate([total[:, :rank], total[:, rank:]], axis=0).astype(BF16)
    for i in range(NZ):

        @pl.when(pl.program_id(0) == i)
        def _():
            width = out.shape[2]
            panel = panels[i][:, panels[i].shape[1] - width :]
            delta = jnp.dot(low, panel, preferred_element_type=F32)
            out[...] = delta.astype(BF16).reshape(out.shape)


def up_step(order, parts, panels, width):
    rank, wide = panels[0].shape
    lines = COLUMNS * CAP // 2
    return call(
        up_kernel,
        "up",
        jax.ShapeDtypeStruct((COLUMNS, NZ * CAP, width), BF16),
        (NZ,),
        [pl.BlockSpec((1, lines, 2 * rank), lambda i, o: (i, 0, 0))] * NX
        + [pl.BlockSpec((rank, wide), lambda i, o: (0, 0))] * NZ,
        pl.BlockSpec((COLUMNS, CAP, width), lambda i, o: (0, o[i], 0)),
        4 * NZ * lines * rank * width,
        2 * NZ * (2 * lines + rank) * width,
        prefetch=1,
    )(order, *parts, *panels)


def final_kernel(place, delta, keep, fore_a, back_a, fore_b, back_b, out):
    count = out.shape[0]
    slots = delta.shape[0]
    chosen = (lax.broadcasted_iota(jnp.int32, (count, slots), 1) == place[...]).astype(BF16)
    mine = jnp.dot(chosen, delta[...], preferred_element_type=F32)
    half = count // 2
    top = keep[:half] + fore_b[...].astype(F32) + back_a[...].astype(F32)
    bottom = keep[half:] + fore_a[...].astype(F32) + back_b[...].astype(F32)
    out[:half] = (top + mine[:half]).astype(out.dtype)
    out[half:] = (bottom + mine[half:]).astype(out.dtype)


def final_step(place, delta, base):
    count = place.shape[0]
    slots, width = delta.shape
    tile = 256
    half = pl.BlockSpec((count // 2, tile), lambda n: (0, n))
    return call(
        final_kernel,
        "final",
        jax.ShapeDtypeStruct((count, width), BF16),
        (width // tile,),
        [
            pl.BlockSpec((count, 1), lambda n: (0, 0)),
            pl.BlockSpec((slots, tile), lambda n: (0, n)),
            pl.BlockSpec((count, tile), lambda n: (0, n)),
            half,
            half,
            half,
            half,
        ],
        pl.BlockSpec((count, tile), lambda n: (0, n)),
        2 * count * slots * width,
        2 * (slots + 4 * count) * width,
    )(place, delta, *base)


def z_ring(chunk):
    fore = back = chunk
    found = [chunk]
    for step in range(1, 5):
        fore = lax.ppermute(fore, "z", ring(NZ, 1))
        found.append(fore)
        if step < 4:
            back = lax.ppermute(back, "z", ring(NZ, -1))
            found.append(back)
    return found


def on_device(tokens, owner, weight, down, up):
    z, x = lax.axis_index("z"), lax.axis_index("x")
    count = tokens.shape[0]
    half = count // 2

    rows = lax.all_to_all(dispatch(tokens, owner), GROUP, 0, 0, tiled=True)
    panels = z_ring(jnp.concatenate([down[0], up[0]], axis=1))
    order = jnp.stack([(z + dz) % NZ for dz in RELATIVE_Z])

    two = base_chunks(tokens, weight, ((x + 2) % NX)[None], BF16)[0]
    rest = base_chunks(tokens, weight, jnp.stack([(x + 1) % NX, (x + 3) % NX, x]), F32)
    fore = lax.ppermute(two[:half], "x", ring(NX, 1))
    back = lax.ppermute(two[half:], "x", ring(NX, -1))
    fore_a = lax.ppermute(rest[0, half:].astype(BF16), "x", ring(NX, 1))
    back_a = lax.ppermute(rest[1, :half].astype(BF16), "x", ring(NX, -1))
    fore_b = lax.ppermute((rest[0, :half] + fore.astype(F32)).astype(BF16), "x", ring(NX, 1))
    back_b = lax.ppermute((rest[1, half:] + back.astype(F32)).astype(BF16), "x", ring(NX, -1))

    named = owner[:, 0]
    turn = jnp.arange(count, dtype=jnp.int32)
    earlier = (named[None, :] == named[:, None]) & (turn[None, :] < turn[:, None])
    position = jnp.sum(earlier.astype(jnp.int32), axis=1)
    place = (named % COLUMNS) * (NZ * CAP) + (named // COLUMNS) * CAP + position

    part = down_step(order, rows, panels)
    parts = [part] + [lax.ppermute(part, "x", ring(NX, step)) for step in (1, 2, 3)]
    delta = up_step(order, parts, panels, up.shape[2])
    delta = lax.all_to_all(delta, GROUP, 0, 0, tiled=True)
    return final_step(
        place[:, None],
        delta.reshape(COLUMNS * NZ * CAP, up.shape[2]),
        (rest[2], fore_a, back_a, fore_b, back_b),
    )


def solution(mesh):
    fine = Mesh(mesh.devices.reshape(NZ, NY, NC, NX), ("z", "y", "core", "x"))
    dp = ("z", "y", "core")
    placed = (P(dp, "x"), P(dp, None), P("x", None), P(dp, None, "x"), P(dp, None, "x"))
    return jax.shard_map(
        on_device, mesh=fine, in_specs=placed, out_specs=P(dp, "x"), check_vma=False
    )
```

time: 209 us -> 121 us (0.58)
  waiting for transfers between devices: 139 us -> 29.5 us
  starting transfers between devices: 0.08 us -> 34.7 us
  Pallas kernels: 0 us -> 30.4 us
  matrix products: 24.8 us -> 0 us
  blocking collectives: 16.6 us -> 0 us
  between operations: 14.9 us -> 0.18 us
  local copies, waits for them, and re-layouts: 10.5 us -> 21.1 us
    all_gather x2 -> x0, waiting for transfers between devices: 137 us -> none  [the longest x1 86.4 us: on_device(): lax.all_gather(adapter_down_weight, 'dp', axis=0, tiled=True)]
    pallas_call x0 -> x6, Pallas kernels: none -> 30.4 us  [the longest x2 10.1 us: base_chunks(): call(base_kernel, 'base', jax.ShapeDtypeStruct((chunks, count, width), dt...]
    ppermute x0 -> x16, waiting for transfers between devices: none -> 26.2 us  [the longest x4 16.7 us: z_ring(): fore = lax.ppermute(fore, 'z', ring(NZ, 1))]
    dot_general x3 -> x0, matrix products: 24.8 us -> none  [the longest x1 11.5 us: on_device(): jnp.einsum('acd,ard->acr', send_buffer, lax.all_gather(adapter_down_weigh...]
    ppermute x0 -> x16, starting transfers between devices: none -> 19.6 us  [the longest x3 9.42 us: z_ring(): back = lax.ppermute(back, 'z', ring(NZ, -1))]
    unnamed x2 -> x49, local copies, waits for them, and re-layouts: 0.66 us -> 18 us
    psum x1 -> x0, blocking collectives: 16.6 us -> none  [on_device(): lax.psum(product.reshape(holder_count, row_capacity * adapter_rank_width)...]
    all_to_all x0 -> x2, starting transfers between devices: none -> 15.1 us  [the longest x1 7.8 us: on_device(): rows = lax.all_to_all(dispatch(tokens, owner), GROUP, 0, 0, tiled=True)]
  transfers between devices with their start and end apart: 3 -> 18, of which waited for: 2 -> 7; matrix products, arithmetic and copies ran while one was open for 17% -> 6% of each run, Pallas kernels for 0% -> 18%
where the time goes in v2:
time: 121 us; the launch traced here: 120 us
  starting transfers between devices  34.7 us (29%)
  Pallas kernels  30.4 us (25%)
  waiting for transfers between devices  29.5 us (24%)
  local copies, waits for them, and re-layouts  21.1 us (17%)
  other arithmetic  3.68 us (3%)
    unnamed x49, local copies, waits for them, and re-layouts  18 us
    ppermute x4, waiting for transfers between devices, z_ring(): fore = lax.ppermute(fore, 'z', ring(NZ, 1))  16.7 us
    pallas_call x2, Pallas kernels, base_chunks(): call(base_kernel, 'base', jax.ShapeDtypeStruct((chunks, count, width), dt...  10.1 us
    ppermute x3, starting transfers between devices, z_ring(): back = lax.ppermute(back, 'z', ring(NZ, -1))  9.42 us
    all_to_all x1, starting transfers between devices, on_device(): rows = lax.all_to_all(dispatch(tokens, owner), GROUP, 0, 0, tiled=True)  7.8 us
    pallas_call x1, Pallas kernels, down_step(): call(down_kernel, 'down', jax.ShapeDtypeStruct((NZ, lines, 2 * rank), BF1...  7.4 us
    all_to_all x1, starting transfers between devices, on_device(): delta = lax.all_to_all(delta, GROUP, 0, 0, tiled=True)  7.32 us
    pallas_call x1, Pallas kernels, dispatch(): call(dispatch_kernel, 'dispatch', jax.ShapeDtypeStruct((COLUMNS, rows, in...  5.65 us
  transfers between devices with their start and end apart: 18, of which 7 were waited for; matrix products, arithmetic and copies ran while one was open for 6% of the time, Pallas kernels for 18%

profile of v2, /device:TPU:1, one launch (start us, length us, event | category | flops | bytes accessed | tf_op | source)
XLA Modules:
  0.0 119.6 jit_solution(14742222924723886379)
XLA Ops:
  0.8 1.7 %copy-done = bf16[512,2048]{1,0:T(8,128)(2,1)S(1)} copy-done((bf16[512,2048]{1,0:T(8,128)(2,1)S(1)}, bf16[512,2048]{1,0:T(8,128)(2,1)}, u32[]{:S(2)}) %copy-start) | copy-done | bytes 2097176
  3.2 5.7 %dispatch.1 = bf16[8,128,2048]{2,1,0:T(8,128)(2,1)} custom-call(s32[512,1]{1,0:T(8,128)S(1)} %copy.33.named, s32[1,512]{1,0:T(1,128)S(1)} %bitcast.40, bf16[512,2048]{1,0:T(8,128)(2,1)S(1)} %copy-done), custom_call_target="tpu_custom_call" | custom-call | flops 2147483648 | bytes 6291456 | tf_op jit(solution)/shard_map/dispatch/pallas_call | solution.py:85
  8.9 7.8 %all-to-all-start = ((bf16[8,128,2048]{2,1,0:T(8,128)(2,1)}), bf16[8,128,2048]{2,1,0:T(8,128)(2,1)}, u32[]{:S(2)}, u32[]{:S(2)}) async-start(bf16[8,128,2048]{2,1,0:T(8,128)(2,1)} %dispatch.1), calls=%async_computation | async-start | bytes 8388608 | tf_op jit(solution)/shard_map/all_to_all | solution.py:226
  16.8 4.0 %collective-permute-start.1 = (bf16[64,2560]{1,0:T(8,128)(2,1)S(1)}, bf16[64,2560]{1,0:T(8,128)(2,1)}, u32[]{:S(2)}, u32[]{:S(2)}) collective-permute-start(bf16[64,2560]{1,0:T(8,128)(2,1)S(1)} %pad_maximum_fusion.refs_0_.refs_4_), channel_id=1, source_target_pairs={{0,224},{32,0},{64,32},{96,64},{128,96},{160,128},{192,160},{224,1... | collective-permute-start | bytes 983048 | tf_op jit(solution)/shard_map/ppermute | solution.py:216
  20.8 8.0 %collective-permute-done.refs_1_.refs_5_ = bf16[64,2560]{1,0:T(8,128)(2,1)S(1)} collective-permute-done((bf16[64,2560]{1,0:T(8,128)(2,1)S(1)}, bf16[64,2560]{1,0:T(8,128)(2,1)S(1)}, u32[]{:S(2)}, u32[]{:S(2)}) %collective-permute-start) | collective-permute-done | bytes 327712 | tf_op jit(solution)/shard_map/ppermute | solution.py:213
  29.6 2.7 %collective-permute-start.3 = (bf16[64,2560]{1,0:T(8,128)(2,1)}, bf16[64,2560]{1,0:T(8,128)(2,1)}, u32[]{:S(2)}, u32[]{:S(2)}) collective-permute-start(bf16[64,2560]{1,0:T(8,128)(2,1)} %collective-permute-done.1.refs_2_.refs_6_), channel_id=1, source_target_pairs={{0,224},{32,0},{64,32},{96,64},{128,96},{160,128},{192,160},{224,1... | collective-permute-start | bytes 983048 | tf_op jit(solution)/shard_map/ppermute | solution.py:216
  32.3 6.5 %collective-permute-done.2.refs_3_.refs_7_ = bf16[64,2560]{1,0:T(8,128)(2,1)} collective-permute-done((bf16[64,2560]{1,0:T(8,128)(2,1)S(1)}, bf16[64,2560]{1,0:T(8,128)(2,1)}, u32[]{:S(2)}, u32[]{:S(2)}) %collective-permute-start.2) | collective-permute-done | bytes 327712 | tf_op jit(solution)/shard_map/ppermute | solution.py:213
  38.8 1.6 %copy-done.1 = bf16[512,2048]{1,0:T(8,128)(2,1)S(1)} copy-done((bf16[512,2048]{1,0:T(8,128)(2,1)S(1)}, bf16[512,2048]{1,0:T(8,128)(2,1)}, u32[]{:S(2)}) %copy-start.1) | copy-done | bytes 2097176
  40.4 7.4 %base.2 = f32[3,512,512]{2,1,0:T(8,128)S(1)} custom-call(s32[3]{0:T(128)S(1)} %pad_add_fusion.which, bf16[512,2048]{1,0:T(8,128)(2,1)S(1)} %copy-done.1, bf16[2048,2048]{1,0:T(8,128)(2,1)} %weight.3), custom_call_target="tpu_custom_call" | custom-call | flops 3221225472 | bytes 8388608 | tf_op jit(solution)/shard_map/base/pallas_call | solution.py:48
  50.0 1.5 %collective-permute-start.11 = (bf16[256,512]{1,0:T(8,128)(2,1)}, bf16[256,512]{1,0:T(8,128)(2,1)}, u32[]{:S(2)}, u32[]{:S(2)}) collective-permute-start(bf16[256,512]{1,0:T(8,128)(2,1)} %get-tuple-element.7), channel_id=1, source_target_pairs={{0,3},{1,0},{2,1},{3,2},{4,7},{5,4},{6,5},{7,6},{8,11},{9,8},{10,9... | collective-permute-start | bytes 786440 | tf_op jit(solution)/shard_map/ppermute | solution.py:235
  51.6 2.7 %collective-permute-start.5 = (bf16[64,2560]{1,0:T(8,128)(2,1)}, bf16[64,2560]{1,0:T(8,128)(2,1)S(1)}, u32[]{:S(2)}, u32[]{:S(2)}) collective-permute-start(bf16[64,2560]{1,0:T(8,128)(2,1)} %collective-permute-done.3.refs_4_.refs_8_), channel_id=1, source_target_pairs={{0,224},{32,0},{64,32},{96,64},{128,96},{160,128},{192,160},{224,1... | collective-permute-start | bytes 983048 | tf_op jit(solution)/shard_map/ppermute | solution.py:216
  54.4 1.6 %copy-done.2 = bf16[512,2048]{1,0:T(8,128)(2,1)S(1)} copy-done((bf16[512,2048]{1,0:T(8,128)(2,1)S(1)}, bf16[512,2048]{1,0:T(8,128)(2,1)}, u32[]{:S(2)}) %copy-start.2) | copy-done | bytes 2097176
  55.9 2.7 %base.3 = bf16[1,512,512]{2,1,0:T(8,128)(2,1)S(1)} custom-call(s32[1]{0:T(128)} %bitcast.21.which, bf16[512,2048]{1,0:T(8,128)(2,1)S(1)} %copy-done.2, bf16[2048,2048]{1,0:T(8,128)(2,1)} %weight.3), custom_call_target="tpu_custom_call" | custom-call | flops 1073741824 | bytes 4194304 | tf_op jit(solution)/shard_map/base/pallas_call | solution.py:48
  60.3 2.2 %collective-permute-done.6.refs_7_.refs_11_ = bf16[64,2560]{1,0:T(8,128)(2,1)S(1)} collective-permute-done((bf16[64,2560]{1,0:T(8,128)(2,1)}, bf16[64,2560]{1,0:T(8,128)(2,1)S(1)}, u32[]{:S(2)}, u32[]{:S(2)}) %collective-permute-start.6) | collective-permute-done | bytes 327712 | tf_op jit(solution)/shard_map/ppermute | solution.py:213
  63.3 2.3 %all-to-all-done.rows = bf16[8,128,2048]{2,1,0:T(8,128)(2,1)} async-done(((bf16[8,128,2048]{2,1,0:T(8,128)(2,1)}), bf16[8,128,2048]{2,1,0:T(8,128)(2,1)}, u32[]{:S(2)}, u32[]{:S(2)}) %all-to-all-start) | async-done | bytes 4194336 | tf_op jit(solution)/shard_map/all_to_all | solution.py:226
  68.5 7.4 %down.1.refs_0_ = bf16[8,64,128]{2,1,0:T(8,128)(2,1)S(1)} custom-call(s32[8]{0:T(128)S(1)} %stack.47.order, bf16[8,128,2048]{2,1,0:T(8,128)(2,1)} %all-to-all-done.rows, bf16[64,2560]{1,0:T(8,128)(2,1)S(1)} %pad_maximum_fusion.refs_0_.refs_4_, bf16[64,2560]{1,0:T(8,128)(2,1)S(1)} %copy-done.6, bf16[64,2560]{1,0:T(8,128)(2,1)} %collective-permute-done.1.refs_2_.refs_6_, ...), custom_call_target="tpu_custom_call" | custom-call | flops 268435456 | bytes 6291456 | tf_op jit(solution)/shard_map/down/pallas_call | solution.py:124
  76.0 1.9 %collective-permute-start.8 = (bf16[8,64,128]{2,1,0:T(8,128)(2,1)S(1)}, bf16[8,64,128]{2,1,0:T(8,128)(2,1)S(1)}, u32[]{:S(2)}, u32[]{:S(2)}) collective-permute-start(bf16[8,64,128]{2,1,0:T(8,128)(2,1)S(1)} %down.1.refs_0_), channel_id=1, source_target_pairs={{0,2},{1,3},{2,0},{3,1},{4,6},{5,7},{6,4},{7,5},{8,10},{9,11},{10,... | collective-permute-start | bytes 393224 | tf_op jit(solution)/shard_map/ppermute | solution.py:246
  79.1 4.2 %collective-permute-done.7.refs_1_ = bf16[8,64,128]{2,1,0:T(8,128)(2,1)S(1)} collective-permute-done((bf16[8,64,128]{2,1,0:T(8,128)(2,1)S(1)}, bf16[8,64,128]{2,1,0:T(8,128)(2,1)S(1)}, u32[]{:S(2)}, u32[]{:S(2)}) %collective-permute-start.7) | collective-permute-done | bytes 131104 | tf_op jit(solution)/shard_map/ppermute | solution.py:246
  84.8 4.2 %up.1 = bf16[8,128,512]{2,1,0:T(8,128)(2,1)S(1)} custom-call(s32[8]{0:T(128)S(1)} %stack.47.order, bf16[8,64,128]{2,1,0:T(8,128)(2,1)S(1)} %down.1.refs_0_, bf16[8,64,128]{2,1,0:T(8,128)(2,1)S(1)} %collective-permute-done.7.refs_1_, bf16[8,64,128]{2,1,0:T(8,128)(2,1)S(1)} %collective-permute-done.8.refs_2_, ...), custom_call_target="tpu_custom_call" | custom-call | flops 67108864 | bytes 1572864 | tf_op jit(solution)/shard_map/up/pallas_call | solution.py:158
  89.9 7.3 %all-to-all-start.1 = ((bf16[8,128,512]{2,1,0:T(8,128)(2,1)}), bf16[8,128,512]{2,1,0:T(8,128)(2,1)}, u32[]{:S(2)}, u32[]{:S(2)}) async-start(bf16[8,128,512]{2,1,0:T(8,128)(2,1)} %copy-done.3), calls=%async_computation.1 | async-start | bytes 2097152 | tf_op jit(solution)/shard_map/all_to_all | solution.py:248
  97.9 1.9 %fusion.7.place = s32[512,1]{1,0:T(8,128)} fusion(s32[512,1]{1,0:T(8,128)S(1)} %copy.40, pred[512,1]{1,0:T(8,128)(4,1)S(1)} %copy.36, s32[512,1]{1,0:T(8,128)} %copy-done.14), kind=kLoop, calls=%fused_computation.18 | loop fusion | flops 11264 | bytes 6656 | tf_op jit(solution)/shard_map/add | solution.py:243
  101.4 2.3 %collective-permute-start.15 = (bf16[256,512]{1,0:T(8,128)(2,1)S(1)}, bf16[256,512]{1,0:T(8,128)(2,1)S(1)}, u32[]{:S(2)}, u32[]{:S(2)}) collective-permute-start(bf16[256,512]{1,0:T(8,128)(2,1)S(1)} %get-tuple-element.5), channel_id=1, source_target_pairs={{0,3},{1,0},{2,1},{3,2},{4,7},{5,4},{6,5},{7,6},{8,11},{9,8},{10,9... | collective-permute-start | bytes 786440 | tf_op jit(solution)/shard_map/ppermute | solution.py:237
  104.8 5.2 %collective-permute-done.13.fore_b = bf16[256,512]{1,0:T(8,128)(2,1)S(1)} collective-permute-done((bf16[256,512]{1,0:T(8,128)(2,1)S(1)}, bf16[256,512]{1,0:T(8,128)(2,1)S(1)}, u32[]{:S(2)}, u32[]{:S(2)}) %collective-permute-start.13) | collective-permute-done | bytes 262176 | tf_op jit(solution)/shard_map/ppermute | solution.py:236
  116.6 3.1 %final.1 = bf16[512,512]{1,0:T(8,128)(2,1)} custom-call(s32[512,1]{1,0:T(8,128)S(1)} %copy-done.15, bf16[1024,512]{1,0:T(8,128)(2,1)} %bitcast.13.delta, f32[512,512]{1,0:T(8,128)S(1)} %copy-done.4, bf16[256,512]{1,0:T(8,128)(2,1)} %collective-permute-done.10.fore_a, bf16[256,512]{1,0:T(8,128)(2,1)} %collective-permute-done.11.back_a, ...), custom_call_target="tpu_custom_call" | custom-call | flops 536870912 | bytes 3145728 | tf_op jit(solution)/shard_map/final/pallas_call | solution.py:189
  (80 shorter events, 23.5 us)
Async XLA Ops:
  0.8 8.0 %copy-start.14 = (s32[512,1]{1,0:T(8,128)}, s32[512,1]{1,0:T(8,128)S(1)}, u32[]{:S(2)}) copy-start(s32[512,1]{1,0:T(8,128)S(1)} %copy.33.named) | copy-start | bytes 6148
  8.9 7.8 %copy-start.23 = (bf16[1,64,512]{2,1,0:T(8,128)(2,1)S(1)}, bf16[1,64,512]{2,1,0:T(8,128)(2,1)}, u32[]{:S(2)}) copy-start(bf16[1,64,512]{2,1,0:T(8,128)(2,1)} %param.9) | copy-start | bytes 196612
  8.9 56.7 %all-to-all-start = ((bf16[8,128,2048]{2,1,0:T(8,128)(2,1)}), bf16[8,128,2048]{2,1,0:T(8,128)(2,1)}, u32[]{:S(2)}, u32[]{:S(2)}) async-start(bf16[8,128,2048]{2,1,0:T(8,128)(2,1)} %dispatch.1), calls=%async_computation | async-start | bytes 8388608 | tf_op jit(solution)/shard_map/all_to_all | solution.py:226
  16.7 12.0 %collective-permute-start = (bf16[64,2560]{1,0:T(8,128)(2,1)S(1)}, bf16[64,2560]{1,0:T(8,128)(2,1)S(1)}, u32[]{:S(2)}, u32[]{:S(2)}) collective-permute-start(bf16[64,2560]{1,0:T(8,128)(2,1)S(1)} %pad_maximum_fusion.refs_0_.refs_4_), channel_id=1, source_target_pairs={{0,32},{32,64},{64,96},{96,128},{128,160},{160,192},{192,224},{224... | collective-permute-start | bytes 983048 | tf_op jit(solution)/shard_map/ppermute | solution.py:213
  16.8 12.8 %collective-permute-start.1 = (bf16[64,2560]{1,0:T(8,128)(2,1)S(1)}, bf16[64,2560]{1,0:T(8,128)(2,1)}, u32[]{:S(2)}, u32[]{:S(2)}) collective-permute-start(bf16[64,2560]{1,0:T(8,128)(2,1)S(1)} %pad_maximum_fusion.refs_0_.refs_4_), channel_id=1, source_target_pairs={{0,224},{32,0},{64,32},{96,64},{128,96},{160,128},{192,160},{224,1... | collective-permute-start | bytes 983048 | tf_op jit(solution)/shard_map/ppermute | solution.py:216
  28.8 10.0 %collective-permute-start.2 = (bf16[64,2560]{1,0:T(8,128)(2,1)S(1)}, bf16[64,2560]{1,0:T(8,128)(2,1)}, u32[]{:S(2)}, u32[]{:S(2)}) collective-permute-start(bf16[64,2560]{1,0:T(8,128)(2,1)S(1)} %collective-permute-done.refs_1_.refs_5_), channel_id=1, source_target_pairs={{0,32},{32,64},{64,96},{96,128},{128,160},{160,192},{192,224},{224... | collective-permute-start | bytes 983048 | tf_op jit(solution)/shard_map/ppermute | solution.py:213
  29.6 22.0 %collective-permute-start.3 = (bf16[64,2560]{1,0:T(8,128)(2,1)}, bf16[64,2560]{1,0:T(8,128)(2,1)}, u32[]{:S(2)}, u32[]{:S(2)}) collective-permute-start(bf16[64,2560]{1,0:T(8,128)(2,1)} %collective-permute-done.1.refs_2_.refs_6_), channel_id=1, source_target_pairs={{0,224},{32,0},{64,32},{96,64},{128,96},{160,128},{192,160},{224,1... | collective-permute-start | bytes 983048 | tf_op jit(solution)/shard_map/ppermute | solution.py:216
  38.8 15.6 %collective-permute-start.4 = (bf16[64,2560]{1,0:T(8,128)(2,1)}, bf16[64,2560]{1,0:T(8,128)(2,1)}, u32[]{:S(2)}, u32[]{:S(2)}) collective-permute-start(bf16[64,2560]{1,0:T(8,128)(2,1)} %collective-permute-done.2.refs_3_.refs_7_), channel_id=1, source_target_pairs={{0,32},{32,64},{64,96},{96,128},{128,160},{160,192},{192,224},{224... | collective-permute-start | bytes 983048 | tf_op jit(solution)/shard_map/ppermute | solution.py:213
  48.8 56.0 %collective-permute-start.10 = (bf16[256,512]{1,0:T(8,128)(2,1)}, bf16[256,512]{1,0:T(8,128)(2,1)}, u32[]{:S(2)}, u32[]{:S(2)}) collective-permute-start(bf16[256,512]{1,0:T(8,128)(2,1)} %get-tuple-element.8), channel_id=1, source_target_pairs={{0,1},{1,2},{2,3},{3,0},{4,5},{5,6},{6,7},{7,4},{8,9},{9,10},{10,1... | collective-permute-start | bytes 786440 | tf_op jit(solution)/shard_map/ppermute | solution.py:234
  50.0 54.8 %collective-permute-start.11 = (bf16[256,512]{1,0:T(8,128)(2,1)}, bf16[256,512]{1,0:T(8,128)(2,1)}, u32[]{:S(2)}, u32[]{:S(2)}) collective-permute-start(bf16[256,512]{1,0:T(8,128)(2,1)} %get-tuple-element.7), channel_id=1, source_target_pairs={{0,3},{1,0},{2,1},{3,2},{4,7},{5,4},{6,5},{7,6},{8,11},{9,8},{10,9... | collective-permute-start | bytes 786440 | tf_op jit(solution)/shard_map/ppermute | solution.py:235
  51.6 7.9 %collective-permute-start.5 = (bf16[64,2560]{1,0:T(8,128)(2,1)}, bf16[64,2560]{1,0:T(8,128)(2,1)S(1)}, u32[]{:S(2)}, u32[]{:S(2)}) collective-permute-start(bf16[64,2560]{1,0:T(8,128)(2,1)} %collective-permute-done.3.refs_4_.refs_8_), channel_id=1, source_target_pairs={{0,224},{32,0},{64,32},{96,64},{128,96},{160,128},{192,160},{224,1... | collective-permute-start | bytes 983048 | tf_op jit(solution)/shard_map/ppermute | solution.py:216
  54.4 8.2 %collective-permute-start.6 = (bf16[64,2560]{1,0:T(8,128)(2,1)}, bf16[64,2560]{1,0:T(8,128)(2,1)S(1)}, u32[]{:S(2)}, u32[]{:S(2)}) collective-permute-start(bf16[64,2560]{1,0:T(8,128)(2,1)} %collective-permute-done.4.refs_5_.refs_9_), channel_id=1, source_target_pairs={{0,32},{32,64},{64,96},{96,128},{128,160},{160,192},{192,224},{224... | collective-permute-start | bytes 983048 | tf_op jit(solution)/shard_map/ppermute | solution.py:213
  58.7 20.5 %copy-start.21 = (s32[512,1]{0,1:T(1,128)S(1)}, s32[512,1]{0,1:T(1,128)}, u32[]{:S(2)}) copy-start(s32[512,1]{0,1:T(1,128)} %param.6) | copy-start | bytes 6148
  68.5 16.3 %copy-start.7 = (bf16[64,2560]{1,0:T(8,128)(2,1)S(1)}, bf16[64,2560]{1,0:T(8,128)(2,1)}, u32[]{:S(2)}) copy-start(bf16[64,2560]{1,0:T(8,128)(2,1)} %copy-done.5) | copy-start | bytes 983044
  68.5 16.3 %copy-start.10 = (bf16[64,2560]{1,0:T(8,128)(2,1)S(1)}, bf16[64,2560]{1,0:T(8,128)(2,1)}, u32[]{:S(2)}) copy-start(bf16[64,2560]{1,0:T(8,128)(2,1)} %copy-done.8) | copy-start | bytes 983044
  68.5 16.3 %copy-start.13 = (bf16[64,2560]{1,0:T(8,128)(2,1)S(1)}, bf16[64,2560]{1,0:T(8,128)(2,1)}, u32[]{:S(2)}) copy-start(bf16[64,2560]{1,0:T(8,128)(2,1)} %copy-done.11) | copy-start | bytes 983044
  75.9 7.4 %collective-permute-start.7 = (bf16[8,64,128]{2,1,0:T(8,128)(2,1)S(1)}, bf16[8,64,128]{2,1,0:T(8,128)(2,1)S(1)}, u32[]{:S(2)}, u32[]{:S(2)}) collective-permute-start(bf16[8,64,128]{2,1,0:T(8,128)(2,1)S(1)} %down.1.refs_0_), channel_id=1, source_target_pairs={{0,1},{1,2},{2,3},{3,0},{4,5},{5,6},{6,7},{7,4},{8,9},{9,10},{10,1... | collective-permute-start | bytes 393224 | tf_op jit(solution)/shard_map/ppermute | solution.py:246
  76.0 7.3 %collective-permute-start.8 = (bf16[8,64,128]{2,1,0:T(8,128)(2,1)S(1)}, bf16[8,64,128]{2,1,0:T(8,128)(2,1)S(1)}, u32[]{:S(2)}, u32[]{:S(2)}) collective-permute-start(bf16[8,64,128]{2,1,0:T(8,128)(2,1)S(1)} %down.1.refs_0_), channel_id=1, source_target_pairs={{0,2},{1,3},{2,0},{3,1},{4,6},{5,7},{6,4},{7,5},{8,10},{9,11},{10,... | collective-permute-start | bytes 393224 | tf_op jit(solution)/shard_map/ppermute | solution.py:246
  78.0 6.8 %collective-permute-start.9 = (bf16[8,64,128]{2,1,0:T(8,128)(2,1)S(1)}, bf16[8,64,128]{2,1,0:T(8,128)(2,1)S(1)}, u32[]{:S(2)}, u32[]{:S(2)}) collective-permute-start(bf16[8,64,128]{2,1,0:T(8,128)(2,1)S(1)} %down.1.refs_0_), channel_id=1, source_target_pairs={{0,3},{1,0},{2,1},{3,2},{4,7},{5,4},{6,5},{7,6},{8,11},{9,8},{10,9... | collective-permute-start | bytes 393224 | tf_op jit(solution)/shard_map/ppermute | solution.py:246
  83.3 16.5 %collective-permute-start.14 = (bf16[256,512]{1,0:T(8,128)(2,1)}, bf16[256,512]{1,0:T(8,128)(2,1)}, u32[]{:S(2)}, u32[]{:S(2)}) collective-permute-start(bf16[256,512]{1,0:T(8,128)(2,1)} %get-tuple-element.9), channel_id=1, source_target_pairs={{0,3},{1,0},{2,1},{3,2},{4,7},{5,4},{6,5},{7,6},{8,11},{9,8},{10,9... | collective-permute-start | bytes 786440 | tf_op jit(solution)/shard_map/ppermute | solution.py:233
  83.3 16.5 %collective-permute-start.12 = (bf16[256,512]{1,0:T(8,128)(2,1)}, bf16[256,512]{1,0:T(8,128)(2,1)}, u32[]{:S(2)}, u32[]{:S(2)}) collective-permute-start(bf16[256,512]{1,0:T(8,128)(2,1)} %get-tuple-element.10), channel_id=1, source_target_pairs={{0,1},{1,2},{2,3},{3,0},{4,5},{5,6},{6,7},{7,4},{8,9},{9,10},{10,1... | collective-permute-start | bytes 786440 | tf_op jit(solution)/shard_map/ppermute | solution.py:232
  89.9 22.5 %all-to-all-start.1 = ((bf16[8,128,512]{2,1,0:T(8,128)(2,1)}), bf16[8,128,512]{2,1,0:T(8,128)(2,1)}, u32[]{:S(2)}, u32[]{:S(2)}) async-start(bf16[8,128,512]{2,1,0:T(8,128)(2,1)} %copy-done.3), calls=%async_computation.1 | async-start | bytes 2097152 | tf_op jit(solution)/shard_map/all_to_all | solution.py:248
  101.0 9.1 %collective-permute-start.13 = (bf16[256,512]{1,0:T(8,128)(2,1)S(1)}, bf16[256,512]{1,0:T(8,128)(2,1)S(1)}, u32[]{:S(2)}, u32[]{:S(2)}) collective-permute-start(bf16[256,512]{1,0:T(8,128)(2,1)S(1)} %get-tuple-element.6), channel_id=1, source_target_pairs={{0,1},{1,2},{2,3},{3,0},{4,5},{5,6},{6,7},{7,4},{8,9},{9,10},{10,1... | collective-permute-start | bytes 786440 | tf_op jit(solution)/shard_map/ppermute | solution.py:236
  101.4 9.4 %collective-permute-start.15 = (bf16[256,512]{1,0:T(8,128)(2,1)S(1)}, bf16[256,512]{1,0:T(8,128)(2,1)S(1)}, u32[]{:S(2)}, u32[]{:S(2)}) collective-permute-start(bf16[256,512]{1,0:T(8,128)(2,1)S(1)} %get-tuple-element.5), channel_id=1, source_target_pairs={{0,3},{1,0},{2,1},{3,2},{4,7},{5,4},{6,5},{7,6},{8,11},{9,8},{10,9... | collective-permute-start | bytes 786440 | tf_op jit(solution)/shard_map/ppermute | solution.py:237
  (18 other events, 25.0 us)

commit v3 on v2

v3 whole, which is shorter than its diff:
```python
import jax
import jax.numpy as jnp
from jax import lax
from jax.experimental import pallas as pl
from jax.experimental.pallas import tpu as pltpu
from jax.sharding import Mesh, PartitionSpec as P

F32 = jnp.float32
BF16 = jnp.bfloat16
NZ, NY, NC, NX = 8, 4, 2, 4
COLUMNS = NY * NC
CAP = 16
GROUP = ("y", "core")
WHOLE, PART = 60, 16
ROUTES = ((2, 0), (2, 1), (1, 0), (3, 0), (1, 1), (3, 1), (0, 1))
RELATIVE_Z = (0, -1, 1, -2, 2, -3, 3, -4)


def ring(size, step):
    return [(place, (place + step) % size) for place in range(size)]


def call(kernel, name, out, grid, ins, outs, flops, moved, limit, prefetch=0, scratch=()):
    return pl.pallas_call(
        kernel,
        out_shape=out,
        grid_spec=pltpu.PrefetchScalarGridSpec(
            num_scalar_prefetch=prefetch,
            grid=grid,
            in_specs=ins,
            out_specs=outs,
            scratch_shapes=scratch,
        ),
        compiler_params=pltpu.CompilerParams(vmem_limit_bytes=limit * 1024 * 1024),
        cost_estimate=pl.CostEstimate(flops=flops, bytes_accessed=moved, transcendentals=0),
        name=name,
    )


def base_kernel(which, tokens, weight, *outs):
    product = jnp.dot(tokens[...], weight[...], preferred_element_type=F32)
    half = product.shape[0] // 2
    for j in range(2):

        @pl.when(pl.program_id(0) == j)
        def _():
            top, bottom = outs[2 * j : 2 * j + 2]
            top[...] = product[:half].astype(top.dtype)
            bottom[...] = product[half:].astype(bottom.dtype)


def base_pair(tokens, weight, which, types, tile=256):
    count, inner = tokens.shape
    width = weight.shape[1] // NX
    tiles = width // tile
    first = pl.BlockSpec((count // 2, tile), lambda j, n, w: (0, n + j * (tiles - 1 - n)))
    second = pl.BlockSpec((count // 2, tile), lambda j, n, w: (0, n * j))
    return call(
        base_kernel,
        "base",
        [jax.ShapeDtypeStruct((count // 2, width), kind) for kind in types],
        (2, tiles),
        [
            pl.BlockSpec((count, inner), lambda j, n, w: (0, 0)),
            pl.BlockSpec((inner, tile), lambda j, n, w: (0, w[j] * tiles + n)),
        ],
        [first, first, second, second],
        4 * count * inner * width,
        2 * (count + 2 * width) * inner,
        WHOLE,
        prefetch=1,
    )(jnp.stack(which), tokens, weight)


def dispatch_kernel(owner, tokens, out, chosen, held, made, taken, given):
    count = held.shape[0]
    slots = chosen.shape[0]
    fetch = pltpu.make_async_copy(tokens, held, taken)
    fetch.start()
    mine = owner[...]
    adapter = lax.broadcasted_iota(jnp.int32, (NZ * COLUMNS, count), 0)
    member = (adapter == mine).astype(F32)
    above = lax.broadcasted_iota(jnp.int32, (count, count), 0)
    below = lax.broadcasted_iota(jnp.int32, (count, count), 1)
    before = (above < below).astype(F32).astype(BF16)
    earlier = jnp.dot(member.astype(BF16), before, preferred_element_type=F32)
    position = jnp.sum(earlier * member, axis=0, keepdims=True).astype(jnp.int32)
    place = (mine % COLUMNS) * (NZ * CAP) + (mine // COLUMNS) * CAP + position
    slot = lax.broadcasted_iota(jnp.int32, (slots, count), 0)
    chosen[...] = (slot == place).astype(F32).astype(BF16)
    fetch.wait()
    copies = []
    rows = slots // 4
    for part in range(4):
        block = made.at[pl.ds(2 * part, 2)]
        product = jnp.dot(
            chosen[part * rows : (part + 1) * rows], held[...], preferred_element_type=F32
        )
        block[...] = product.astype(BF16).reshape(block.shape)
        copy = pltpu.make_async_copy(block, out.at[pl.ds(2 * part, 2)], given.at[part])
        copy.start()
        copies.append(copy)
    for copy in copies:
        copy.wait()


def dispatch(tokens, owner):
    count, inner = tokens.shape
    rows = NZ * CAP
    whole = pl.BlockSpec(memory_space=pl.ANY)
    return call(
        dispatch_kernel,
        "dispatch",
        jax.ShapeDtypeStruct((COLUMNS, rows, inner), BF16),
        (1,),
        [pl.BlockSpec((1, count), lambda n: (0, 0)), whole],
        whole,
        2 * COLUMNS * rows * count * inner,
        2 * (count + COLUMNS * rows) * inner,
        WHOLE,
        scratch=[
            pltpu.VMEM((COLUMNS * rows, count), BF16),
            pltpu.VMEM((count, inner), BF16),
            pltpu.VMEM((COLUMNS, rows, inner), BF16),
            pltpu.SemaphoreType.DMA,
            pltpu.SemaphoreType.DMA((4,)),
        ],
    )(owner.reshape(1, count), tokens)


def down_kernel(order, rows, *refs):
    panels, (out, held, kept, first, second) = refs[:NZ], refs[NZ:]
    inner = rows.shape[2]
    copies = []
    for i in range(NZ):
        start = pl.multiple_of(order[i] * CAP, CAP)
        pair = (
            pltpu.make_async_copy(rows.at[:, pl.ds(start, CAP), :], held.at[i], first.at[i]),
            pltpu.make_async_copy(panels[i].at[:, pl.ds(0, inner)], kept.at[i], second.at[i]),
        )
        for copy in pair:
            copy.start()
        copies.append(pair)
    many, rank = 4, kept.shape[1]
    lines = COLUMNS * CAP
    for start in range(0, NZ, many):
        for pair in copies[start : start + many]:
            for copy in pair:
                copy.wait()
        product = lax.dot_general(
            held[start : start + many].reshape(many * lines, inner),
            kept[start : start + many].reshape(many * rank, inner),
            (((1,), (1,)), ((), ())),
            preferred_element_type=F32,
        )
        for i in range(many):
            block = product[i * lines : (i + 1) * lines, i * rank : (i + 1) * rank]
            half = lines // 2
            out[start + i] = jnp.concatenate([block[:half], block[half:]], axis=1).astype(BF16)


def down_step(order, rows, panels):
    inner = rows.shape[2]
    rank = panels[0].shape[0]
    lines = COLUMNS * CAP // 2
    whole = pl.BlockSpec(memory_space=pl.ANY)
    return call(
        down_kernel,
        "down",
        jax.ShapeDtypeStruct((NZ, lines, 2 * rank), BF16),
        (1,),
        [whole] * (1 + NZ),
        pl.BlockSpec((NZ, lines, 2 * rank), lambda i, o: (0, 0, 0)),
        4 * NZ * lines * inner * rank,
        2 * NZ * (2 * lines + rank) * inner,
        WHOLE,
        prefetch=1,
        scratch=[
            pltpu.VMEM((NZ, COLUMNS, CAP, inner), BF16),
            pltpu.VMEM((NZ, rank, inner), BF16),
            pltpu.SemaphoreType.DMA((NZ,)),
            pltpu.SemaphoreType.DMA((NZ,)),
        ],
    )(order, rows, *panels)


def up_kernel(order, homes, *refs):
    parts, panels, outs, low = refs[:NX], refs[NX : NX + NZ], refs[NX + NZ : -1], refs[-1]
    for i in range(NZ):
        total = parts[0][i].astype(F32)
        for part in parts[1:]:
            total = total + part[i].astype(F32)
        rank = total.shape[1] // 2
        low[...] = jnp.concatenate([total[:, :rank], total[:, rank:]], axis=0)
        picked = [
            low[pl.ds(pl.multiple_of(homes[r] * CAP, CAP), CAP), :] for r in range(COLUMNS)
        ]
        delta = jnp.dot(
            jnp.concatenate(picked, axis=0).astype(BF16),
            panels[i][...],
            preferred_element_type=F32,
        ).astype(BF16)
        start = pl.multiple_of(order[i] * CAP, CAP)
        for r in range(COLUMNS):
            outs[r][pl.ds(start, CAP), :] = delta[r * CAP : (r + 1) * CAP]


def up_step(order, homes, parts, panels, width):
    rank, wide = panels[0].shape
    lines = COLUMNS * CAP // 2
    last = wide // width - 1
    return call(
        up_kernel,
        "up",
        [jax.ShapeDtypeStruct((NZ * CAP, width), BF16)] * COLUMNS,
        (1,),
        [pl.BlockSpec((NZ, lines, 2 * rank), lambda i, o, h: (0, 0, 0))] * NX
        + [pl.BlockSpec((rank, width), lambda i, o, h: (0, last))] * NZ,
        [pl.BlockSpec((NZ * CAP, width), lambda i, o, h: (0, 0))] * COLUMNS,
        4 * NZ * lines * rank * width,
        2 * NZ * (2 * lines + rank) * width,
        WHOLE,
        prefetch=2,
        scratch=[pltpu.VMEM((2 * lines, rank), F32)],
    )(order, homes, *parts, *panels)


def final_kernel(handlers, place, base, *refs):
    pieces, (out, held, kept, arrived) = refs[:COLUMNS], refs[COLUMNS:]
    rows = pieces[0].shape[0]
    copies = [pltpu.make_async_copy(base, kept, arrived.at[COLUMNS])]
    for r in range(COLUMNS):
        start = pl.multiple_of(handlers[r] * rows, rows)
        copies.append(
            pltpu.make_async_copy(pieces[r], held.at[pl.ds(start, rows)], arrived.at[r])
        )
    for copy in copies:
        copy.start()
    count = out.shape[0]
    slots = held.shape[0]
    slot = lax.broadcasted_iota(jnp.int32, (count, slots), 1)
    chosen = (slot == place[...]).astype(F32).astype(BF16)
    for copy in copies:
        copy.wait()
    mine = jnp.dot(chosen, held[...], preferred_element_type=F32)
    out[...] = (kept[...] + mine).astype(out.dtype)


def final_step(handlers, place, pieces, base):
    count = place.shape[0]
    rows, width = pieces[0].shape
    slots = COLUMNS * rows
    whole = pl.BlockSpec(memory_space=pl.ANY)
    return call(
        final_kernel,
        "final",
        jax.ShapeDtypeStruct((count, width), BF16),
        (1,),
        [pl.BlockSpec((count, 1), lambda n, h: (0, 0)), whole] + [whole] * COLUMNS,
        pl.BlockSpec((count, width), lambda n, h: (0, 0)),
        2 * count * slots * width,
        2 * (slots + 4 * count) * width,
        PART,
        prefetch=1,
        scratch=[
            pltpu.VMEM((slots, width), BF16),
            pltpu.VMEM((count, width), F32),
            pltpu.SemaphoreType.DMA((COLUMNS + 1,)),
        ],
    )(handlers, place, base, *pieces)


def group_shift(dy, dc):
    return [
        (y * NC + core, (y + dy) % NY * NC + (core + dc) % NC)
        for y in range(NY)
        for core in range(NC)
    ]


def z_ring(chunk):
    fore = back = chunk
    found = [chunk]
    for step in range(1, 5):
        fore = lax.ppermute(fore, "z", ring(NZ, 1))
        found.append(fore)
        if step < 4:
            back = lax.ppermute(back, "z", ring(NZ, -1))
            found.append(back)
    return found


def on_device(tokens, owner, weight, down, up):
    z, x = lax.axis_index("z"), lax.axis_index("x")
    count = tokens.shape[0]

    rows = lax.all_to_all(dispatch(tokens, owner), GROUP, 0, 0, tiled=True)
    panels = z_ring(jnp.concatenate([down[0], up[0]], axis=1))
    order = jnp.stack([(z + dz) % NZ for dz in RELATIVE_Z])

    fore, back, ahead, sent = base_pair(
        tokens, weight, [(x + 2) % NX, (x + 1) % NX], (BF16, BF16, F32, BF16)
    )
    tokens, fore = lax.optimization_barrier((tokens, fore))
    given, behind, top, bottom = base_pair(
        tokens, weight, [(x + 3) % NX, x], (BF16, F32, F32, F32)
    )
    fore = lax.ppermute(fore, "x", ring(NX, 1))
    back = lax.ppermute(back, "x", ring(NX, -1))
    fore_a = lax.ppermute(sent, "x", ring(NX, 1))
    back_a = lax.ppermute(given, "x", ring(NX, -1))
    fore_b = lax.ppermute((ahead + fore.astype(F32)).astype(BF16), "x", ring(NX, 1))
    back_b = lax.ppermute((behind + back.astype(F32)).astype(BF16), "x", ring(NX, -1))
    base = jnp.concatenate(
        [
            top + fore_b.astype(F32) + back_a.astype(F32),
            bottom + fore_a.astype(F32) + back_b.astype(F32),
        ],
        axis=0,
    )

    named = owner[:, 0]
    turn = jnp.arange(count, dtype=jnp.int32)
    earlier = (named[None, :] == named[:, None]) & (turn[None, :] < turn[:, None])
    position = jnp.sum(earlier.astype(jnp.int32), axis=1)
    place = (named % COLUMNS) * (NZ * CAP) + (named // COLUMNS) * CAP + position

    rows, base = lax.optimization_barrier((rows, base))
    part = down_step(order, rows, panels)
    parts = [part] + [lax.ppermute(part, "x", ring(NX, step)) for step in (1, 2, 3)]
    routes = ROUTES + ((0, 0),)
    y, core = lax.axis_index("y"), lax.axis_index("core")
    homes = jnp.stack([(y + dy) % NY * NC + (core + dc) % NC for dy, dc in routes])
    handlers = jnp.stack([(y - dy) % NY * NC + (core - dc) % NC for dy, dc in routes])
    pieces = up_step(order, homes, parts, panels, up.shape[2])
    pieces = [
        lax.ppermute(piece, GROUP, group_shift(*route)) for piece, route in zip(pieces, ROUTES)
    ] + [pieces[-1]]
    return final_step(handlers, place[:, None], pieces, base)


def solution(mesh):
    fine = Mesh(mesh.devices.reshape(NZ, NY, NC, NX), ("z", "y", "core", "x"))
    dp = ("z", "y", "core")
    placed = (P(dp, "x"), P(dp, None), P("x", None), P(dp, None, "x"), P(dp, None, "x"))
    return jax.shard_map(
        on_device, mesh=fine, in_specs=placed, out_specs=P(dp, "x"), check_vma=False
    )
```

time: 121 us -> 105 us (0.87)
  local copies, waits for them, and re-layouts: 21.1 us -> 4.88 us
  waiting for transfers between devices: 29.5 us -> 19.3 us
  starting transfers between devices: 34.7 us -> 41.4 us
  Pallas kernels: 30.4 us -> 33.5 us
  other arithmetic: 3.68 us -> 5.07 us
    ppermute x4, waiting for transfers between devices: 16.7 us -> 0.01 us  [z_ring(): fore = lax.ppermute(fore, 'z', ring(NZ, 1))]
    unnamed x49 -> x35, local copies, waits for them, and re-layouts: 18 us -> 3.14 us
    ppermute x6 -> x13, starting transfers between devices: 6.9 us -> 20.2 us  [the longest x7 14 us: on_device(): lax.ppermute(piece, GROUP, group_shift(*route))]
    all_to_all x1 -> x0, starting transfers between devices: 7.32 us -> none  [on_device(): delta = lax.all_to_all(delta, GROUP, 0, 0, tiled=True)]
    all_to_all x1, waiting for transfers between devices: 2.33 us -> 8.06 us  [on_device(): rows = lax.all_to_all(dispatch(tokens, owner), GROUP, 0, 0, tiled=True)]
    pallas_call x3, Pallas kernels: 14.3 us -> 17.9 us  [the longest x2 14.5 us: base_pair(): call(base_kernel, 'base', [jax.ShapeDtypeStruct((count // 2, width), kind...]
    ppermute x3, waiting for transfers between devices: 0.01 us -> 3.61 us  [z_ring(): back = lax.ppermute(back, 'z', ring(NZ, -1))]
    add x1, other arithmetic: 1.93 us -> 0.28 us  [on_device(): place = named % COLUMNS * (NZ * CAP) + named // COLUMNS * CAP + position]
  transfers between devices with their start and end apart: 18 -> 24, of which waited for: 7 -> 7; matrix products, arithmetic and copies ran while one was open for 6% -> 7% of each run, Pallas kernels for 18% -> 14%
where the time goes in v3:
time: 105 us
  starting transfers between devices  41.4 us (39%)
  Pallas kernels  33.5 us (32%)
  waiting for transfers between devices  19.3 us (18%)
  other arithmetic  5.07 us (5%)
  local copies, waits for them, and re-layouts  4.88 us (5%)
    pallas_call x2, Pallas kernels, base_pair(): call(base_kernel, 'base', [jax.ShapeDtypeStruct((count // 2, width), kind...  14.5 us
    ppermute x7, starting transfers between devices, on_device(): lax.ppermute(piece, GROUP, group_shift(*route))  14 us
    ppermute x3, starting transfers between devices, z_ring(): back = lax.ppermute(back, 'z', ring(NZ, -1))  10 us
    all_to_all x1, waiting for transfers between devices, on_device(): rows = lax.all_to_all(dispatch(tokens, owner), GROUP, 0, 0, tiled=True)  8.06 us
    all_to_all x1, starting transfers between devices, on_device(): rows = lax.all_to_all(dispatch(tokens, owner), GROUP, 0, 0, tiled=True)  7.79 us
    pallas_call x1, Pallas kernels, down_step(): call(down_kernel, 'down', jax.ShapeDtypeStruct((NZ, lines, 2 * rank), BF1...  5.92 us
    pallas_call x1, Pallas kernels, dispatch(): call(dispatch_kernel, 'dispatch', jax.ShapeDtypeStruct((COLUMNS, rows, in...  5.76 us
    pallas_call x1, Pallas kernels, final_step(): call(final_kernel, 'final', jax.ShapeDtypeStruct((count, width), BF16), (...  3.91 us
  transfers between devices with their start and end apart: 24, of which 7 were waited for; matrix products, arithmetic and copies ran while one was open for 7% of the time, Pallas kernels for 14%

profile of v3, /device:TPU:1, one launch (start us, length us, event | category | flops | bytes accessed | tf_op | source)
XLA Modules:
  0.0 104.8 jit_solution(4761147523175440355)
XLA Ops:
  0.0 5.8 %dispatch.1 = bf16[8,128,2048]{2,1,0:T(8,128)(2,1)} custom-call(s32[1,512]{1,0:T(1,128)} %bitcast.34, bf16[512,2048]{1,0:T(8,128)(2,1)} %tokens.4), custom_call_target="tpu_custom_call" | custom-call | flops 2147483648 | bytes 6291456 | tf_op jit(solution)/shard_map/dispatch/pallas_call | solution.py:111
  5.8 7.8 %all-to-all-start = ((bf16[8,128,2048]{2,1,0:T(8,128)(2,1)}), bf16[8,128,2048]{2,1,0:T(8,128)(2,1)}, u32[]{:S(2)}, u32[]{:S(2)}) async-start(bf16[8,128,2048]{2,1,0:T(8,128)(2,1)} %dispatch.1), calls=%async_computation | async-start | bytes 8388608 | tf_op jit(solution)/shard_map/all_to_all | solution.py:297
  13.7 4.0 %collective-permute-start.7 = (bf16[64,2560]{1,0:T(8,128)(2,1)S(1)}, bf16[64,2560]{1,0:T(8,128)(2,1)S(1)}, u32[]{:S(2)}, u32[]{:S(2)}) collective-permute-start(bf16[64,2560]{1,0:T(8,128)(2,1)S(1)} %pad_maximum_fusion.1.refs_0_.refs_4_), channel_id=1, source_target_pairs={{0,224},{32,0},{64,32},{96,64},{128,96},{160,128},{192,160},{224,1... | collective-permute-start | bytes 983048 | tf_op jit(solution)/shard_map/ppermute | solution.py:288
  18.4 7.2 %base.2 = (bf16[256,512]{1,0:T(8,128)(2,1)}, bf16[256,512]{1,0:T(8,128)(2,1)}, f32[256,512]{1,0:T(8,128)}, bf16[256,512]{1,0:T(8,128)(2,1)}) custom-call(s32[2]{0:T(128)} %pad_add_fusion.1.which, bf16[512,2048]{1,0:T(8,128)(2,1)} %tokens.4, bf16[2048,2048]{1,0:T(8,128)(2,1)} %weight.3), custom_call_target="tpu_custom_call" | custom-call | flops 2147483648 | bytes 6291456 | tf_op jit(solution)/shard_map/base/pallas_call | solution.py:58
  25.5 2.5 %collective-permute-start.4 = (bf16[256,512]{1,0:T(8,128)(2,1)}, bf16[256,512]{1,0:T(8,128)(2,1)S(1)}, u32[]{:S(2)}, u32[]{:S(2)}) collective-permute-start(bf16[256,512]{1,0:T(8,128)(2,1)} %get-tuple-element.34), channel_id=1, source_target_pairs={{0,3},{1,0},{2,1},{3,2},{4,7},{5,4},{6,5},{7,6},{8,11},{9,8},{10,9... | collective-permute-start | bytes 786440 | tf_op jit(solution)/shard_map/ppermute | solution.py:309
  29.0 7.4 %base.3 = (bf16[256,512]{1,0:T(8,128)(2,1)}, f32[256,512]{1,0:T(8,128)}, f32[256,512]{1,0:T(8,128)}, f32[256,512]{1,0:T(8,128)}) custom-call(s32[2]{0:T(128)} %pad_add_fusion.which, bf16[512,2048]{1,0:T(8,128)(2,1)} %tokens.4, bf16[2048,2048]{1,0:T(8,128)(2,1)} %weight.3), custom_call_target="tpu_custom_call" | custom-call | flops 2147483648 | bytes 6291456 | tf_op jit(solution)/shard_map/base/pallas_call | solution.py:58
  36.4 1.8 %add_convert_fusion = bf16[256,512]{1,0:T(8,128)(2,1)} fusion(f32[256,512]{1,0:T(8,128)} %get-tuple-element.33, bf16[256,512]{1,0:T(8,128)(2,1)S(1)} %collective-permute-done.4), kind=kLoop, calls=%fused_computation.5 | loop fusion | flops 393216 | bytes 1048576 | tf_op jit(solution)/shard_map/convert_element_type | solution.py:313
  38.3 2.5 %collective-permute-start.5 = (bf16[256,512]{1,0:T(8,128)(2,1)}, bf16[256,512]{1,0:T(8,128)(2,1)S(1)}, u32[]{:S(2)}, u32[]{:S(2)}) collective-permute-start(bf16[256,512]{1,0:T(8,128)(2,1)} %add_convert_fusion), channel_id=1, source_target_pairs={{0,3},{1,0},{2,1},{3,2},{4,7},{5,4},{6,5},{7,6},{8,11},{9,8},{10,9... | collective-permute-start | bytes 786440 | tf_op jit(solution)/shard_map/ppermute | solution.py:313
  43.2 2.5 %collective-permute-start.9 = (bf16[64,2560]{1,0:T(8,128)(2,1)S(1)}, bf16[64,2560]{1,0:T(8,128)(2,1)S(1)}, u32[]{:S(2)}, u32[]{:S(2)}) collective-permute-start(bf16[64,2560]{1,0:T(8,128)(2,1)S(1)} %collective-permute-done.7.refs_2_.refs_6_), channel_id=1, source_target_pairs={{0,224},{32,0},{64,32},{96,64},{128,96},{160,128},{192,160},{224,1... | collective-permute-start | bytes 983048 | tf_op jit(solution)/shard_map/ppermute | solution.py:288
  46.0 1.1 %convert_add_fusion = f32[256,512]{1,0:T(8,128)S(1)} fusion(bf16[256,512]{1,0:T(8,128)(2,1)S(1)} %collective-permute-done.5, f32[256,512]{1,0:T(8,128)} %get-tuple-element.31, bf16[256,512]{1,0:T(8,128)(2,1)S(1)} %collective-permute-done.3), kind=kLoop, calls=%fused_computation.4 | loop fusion | flops 524288 | bytes 1572864 | tf_op jit(solution)/shard_map/add | solution.py:317
  47.1 3.6 %collective-permute-done.9.refs_4_.refs_8_ = bf16[64,2560]{1,0:T(8,128)(2,1)S(1)} collective-permute-done((bf16[64,2560]{1,0:T(8,128)(2,1)S(1)}, bf16[64,2560]{1,0:T(8,128)(2,1)S(1)}, u32[]{:S(2)}, u32[]{:S(2)}) %collective-permute-start.9) | collective-permute-done | bytes 327712 | tf_op jit(solution)/shard_map/ppermute | solution.py:288
  50.7 3.5 %collective-permute-start.11 = (bf16[64,2560]{1,0:T(8,128)(2,1)S(1)}, bf16[64,2560]{1,0:T(8,128)(2,1)S(1)}, u32[]{:S(2)}, u32[]{:S(2)}) collective-permute-start(bf16[64,2560]{1,0:T(8,128)(2,1)S(1)} %collective-permute-done.9.refs_4_.refs_8_), channel_id=1, source_target_pairs={{0,224},{32,0},{64,32},{96,64},{128,96},{160,128},{192,160},{224,1... | collective-permute-start | bytes 983048 | tf_op jit(solution)/shard_map/ppermute | solution.py:288
  54.5 8.1 %all-to-all-done.rows = bf16[8,128,2048]{2,1,0:T(8,128)(2,1)} async-done(((bf16[8,128,2048]{2,1,0:T(8,128)(2,1)}), bf16[8,128,2048]{2,1,0:T(8,128)(2,1)}, u32[]{:S(2)}, u32[]{:S(2)}) %all-to-all-start) | async-done | bytes 4194336 | tf_op jit(solution)/shard_map/all_to_all | solution.py:297
  64.0 5.9 %down.1.refs_0_ = bf16[8,64,128]{2,1,0:T(8,128)(2,1)} custom-call(s32[8]{0:T(128)} %stack.120.order, bf16[8,128,2048]{2,1,0:T(8,128)(2,1)} %all-to-all-done.rows, bf16[64,2560]{1,0:T(8,128)(2,1)} %copy-done.1, bf16[64,2560]{1,0:T(8,128)(2,1)} %copy-done.2, bf16[64,2560]{1,0:T(8,128)(2,1)} %copy-done.3, bf16[64,2560]{1,0:T(8,128)(2,1)} %copy-done.4, ...), custom_call_target="tpu_custom_call" | custom-call | flops 268435456 | bytes 6291456 | tf_op jit(solution)/shard_map/down/pallas_call | solution.py:167
  70.0 2.0 %collective-permute-start.14 = (bf16[8,64,128]{2,1,0:T(8,128)(2,1)}, bf16[8,64,128]{2,1,0:T(8,128)(2,1)S(1)}, u32[]{:S(2)}, u32[]{:S(2)}) collective-permute-start(bf16[8,64,128]{2,1,0:T(8,128)(2,1)} %down.1.refs_0_), channel_id=1, source_target_pairs={{0,2},{1,3},{2,0},{3,1},{4,6},{5,7},{6,4},{7,5},{8,10},{9,11},{10,... | collective-permute-start | bytes 393224 | tf_op jit(solution)/shard_map/ppermute | solution.py:330
  71.9 1.2 %collective-permute-start.15 = (bf16[8,64,128]{2,1,0:T(8,128)(2,1)}, bf16[8,64,128]{2,1,0:T(8,128)(2,1)S(1)}, u32[]{:S(2)}, u32[]{:S(2)}) collective-permute-start(bf16[8,64,128]{2,1,0:T(8,128)(2,1)} %down.1.refs_0_), channel_id=1, source_target_pairs={{0,3},{1,0},{2,1},{3,2},{4,7},{5,4},{6,5},{7,6},{8,11},{9,8},{10,9... | collective-permute-start | bytes 393224 | tf_op jit(solution)/shard_map/ppermute | solution.py:330
  74.1 2.5 %collective-permute-done.13.refs_1_ = bf16[8,64,128]{2,1,0:T(8,128)(2,1)S(1)} collective-permute-done((bf16[8,64,128]{2,1,0:T(8,128)(2,1)}, bf16[8,64,128]{2,1,0:T(8,128)(2,1)S(1)}, u32[]{:S(2)}, u32[]{:S(2)}) %collective-permute-start.13) | collective-permute-done | bytes 131104 | tf_op jit(solution)/shard_map/ppermute | solution.py:330
  78.1 3.4 %up.1 = (bf16[128,512]{1,0:T(8,128)(2,1)}, bf16[128,512]{1,0:T(8,128)(2,1)}, bf16[128,512]{1,0:T(8,128)(2,1)}, bf16[128,512]{1,0:T(8,128)(2,1)}, bf16[128,512]{1...) custom-call(s32[8]{0:T(128)} %stack.120.order, s32[8]{0:T(128)} %stack.128.homes, ...), custom_call_target="tpu_custom_call" | custom-call | flops 67108864 | bytes 1572864 | tf_op jit(solution)/shard_map/up/pallas_call | solution.py:212
  82.0 6.3 %collective-permute-start.17 = (bf16[128,512]{1,0:T(8,128)(2,1)}, bf16[128,512]{1,0:T(8,128)(2,1)S(1)}, u32[]{:S(2)}, u32[]{:S(2)}) collective-permute-start(bf16[128,512]{1,0:T(8,128)(2,1)} %get-tuple-element.38), channel_id=1, source_target_pairs={{0,20},{4,16},{8,28},{12,24},{16,4},{20,0},{24,12},{28,8},{1,21},{... | collective-permute-start | bytes 393224 | tf_op jit(solution)/shard_map/ppermute | solution.py:337
  88.6 1.4 %collective-permute-start.18 = (bf16[128,512]{1,0:T(8,128)(2,1)}, bf16[128,512]{1,0:T(8,128)(2,1)S(1)}, u32[]{:S(2)}, u32[]{:S(2)}) collective-permute-start(bf16[128,512]{1,0:T(8,128)(2,1)} %get-tuple-element.39), channel_id=1, source_target_pairs={{0,8},{4,12},{8,16},{12,20},{16,24},{20,28},{24,0},{28,4},{1,9},{5... | collective-permute-start | bytes 393224 | tf_op jit(solution)/shard_map/ppermute | solution.py:337
  90.0 1.3 %collective-permute-start.19 = (bf16[128,512]{1,0:T(8,128)(2,1)}, bf16[128,512]{1,0:T(8,128)(2,1)S(1)}, u32[]{:S(2)}, u32[]{:S(2)}) collective-permute-start(bf16[128,512]{1,0:T(8,128)(2,1)} %get-tuple-element.40), channel_id=1, source_target_pairs={{0,24},{4,28},{8,0},{12,4},{16,8},{20,12},{24,16},{28,20},{1,25},{... | collective-permute-start | bytes 393224 | tf_op jit(solution)/shard_map/ppermute | solution.py:337
  91.3 3.6 %collective-permute-start.21 = (bf16[128,512]{1,0:T(8,128)(2,1)}, bf16[128,512]{1,0:T(8,128)(2,1)S(1)}, u32[]{:S(2)}, u32[]{:S(2)}) collective-permute-start(bf16[128,512]{1,0:T(8,128)(2,1)} %get-tuple-element.42), channel_id=1, source_target_pairs={{0,28},{4,24},{8,4},{12,0},{16,12},{20,8},{24,20},{28,16},{1,29},{... | collective-permute-start | bytes 393224 | tf_op jit(solution)/shard_map/ppermute | solution.py:337
  97.0 2.8 %collective-permute-done.20.refs_4_ = bf16[128,512]{1,0:T(8,128)(2,1)S(1)} collective-permute-done((bf16[128,512]{1,0:T(8,128)(2,1)}, bf16[128,512]{1,0:T(8,128)(2,1)S(1)}, u32[]{:S(2)}, u32[]{:S(2)}) %collective-permute-start.20) | collective-permute-done | bytes 131104 | tf_op jit(solution)/shard_map/ppermute | solution.py:337
  100.7 3.9 %final.1 = bf16[512,512]{1,0:T(8,128)(2,1)} custom-call(s32[8]{0:T(128)S(1)} %stack.105.handlers, s32[512,1]{1,0:T(8,128)S(1)} %fusion.3.place, f32[512,512]{1,0:T(8,128)S(1)} %pad_maximum_fusion.base, bf16[128,512]{1,0:T(8,128)(2,1)S(1)} %collective-permute-done.16.refs_0_, bf16[128,512]{1,0:T(8,128)(2,1)S(1)} %collective-permute-done.17.refs_1_, ...), custom_call_target="tpu_custom_call" | custom-call | flops 536870912 | bytes 3145728 | tf_op jit(solution)/shard_map/final/pallas_call | solution.py:254
  (81 shorter events, 12.2 us)
Async XLA Ops:
  5.8 56.7 %all-to-all-start = ((bf16[8,128,2048]{2,1,0:T(8,128)(2,1)}), bf16[8,128,2048]{2,1,0:T(8,128)(2,1)}, u32[]{:S(2)}, u32[]{:S(2)}) async-start(bf16[8,128,2048]{2,1,0:T(8,128)(2,1)} %dispatch.1), calls=%async_computation | async-start | bytes 8388608 | tf_op jit(solution)/shard_map/all_to_all | solution.py:297
  13.6 15.3 %collective-permute-start.6 = (bf16[64,2560]{1,0:T(8,128)(2,1)S(1)}, bf16[64,2560]{1,0:T(8,128)(2,1)S(1)}, u32[]{:S(2)}, u32[]{:S(2)}) collective-permute-start(bf16[64,2560]{1,0:T(8,128)(2,1)S(1)} %pad_maximum_fusion.1.refs_0_.refs_4_), channel_id=1, source_target_pairs={{0,32},{32,64},{64,96},{96,128},{128,160},{160,192},{192,224},{224... | collective-permute-start | bytes 983048 | tf_op jit(solution)/shard_map/ppermute | solution.py:285
  13.7 29.5 %collective-permute-start.7 = (bf16[64,2560]{1,0:T(8,128)(2,1)S(1)}, bf16[64,2560]{1,0:T(8,128)(2,1)S(1)}, u32[]{:S(2)}, u32[]{:S(2)}) collective-permute-start(bf16[64,2560]{1,0:T(8,128)(2,1)S(1)} %pad_maximum_fusion.1.refs_0_.refs_4_), channel_id=1, source_target_pairs={{0,224},{32,0},{64,32},{96,64},{128,96},{160,128},{192,160},{224,1... | collective-permute-start | bytes 983048 | tf_op jit(solution)/shard_map/ppermute | solution.py:288
  25.5 10.9 %collective-permute-start.4 = (bf16[256,512]{1,0:T(8,128)(2,1)}, bf16[256,512]{1,0:T(8,128)(2,1)S(1)}, u32[]{:S(2)}, u32[]{:S(2)}) collective-permute-start(bf16[256,512]{1,0:T(8,128)(2,1)} %get-tuple-element.34), channel_id=1, source_target_pairs={{0,3},{1,0},{2,1},{3,2},{4,7},{5,4},{6,5},{7,6},{8,11},{9,8},{10,9... | collective-permute-start | bytes 786440 | tf_op jit(solution)/shard_map/ppermute | solution.py:309
  28.0 17.8 %collective-permute-start.3 = (bf16[256,512]{1,0:T(8,128)(2,1)}, bf16[256,512]{1,0:T(8,128)(2,1)S(1)}, u32[]{:S(2)}, u32[]{:S(2)}) collective-permute-start(bf16[256,512]{1,0:T(8,128)(2,1)} %get-tuple-element.32), channel_id=1, source_target_pairs={{0,1},{1,2},{2,3},{3,0},{4,5},{5,6},{6,7},{7,4},{8,9},{9,10},{10,1... | collective-permute-start | bytes 786440 | tf_op jit(solution)/shard_map/ppermute | solution.py:310
  28.0 14.4 %collective-permute-start = (bf16[256,512]{1,0:T(8,128)(2,1)}, bf16[256,512]{1,0:T(8,128)(2,1)S(1)}, u32[]{:S(2)}, u32[]{:S(2)}) collective-permute-start(bf16[256,512]{1,0:T(8,128)(2,1)} %get-tuple-element.29), channel_id=1, source_target_pairs={{0,1},{1,2},{2,3},{3,0},{4,5},{5,6},{6,7},{7,4},{8,9},{9,10},{10,1... | collective-permute-start | bytes 786440 | tf_op jit(solution)/shard_map/ppermute | solution.py:308
  28.9 16.9 %collective-permute-start.8 = (bf16[64,2560]{1,0:T(8,128)(2,1)S(1)}, bf16[64,2560]{1,0:T(8,128)(2,1)S(1)}, u32[]{:S(2)}, u32[]{:S(2)}) collective-permute-start(bf16[64,2560]{1,0:T(8,128)(2,1)S(1)} %collective-permute-done.6.refs_1_.refs_5_), channel_id=1, source_target_pairs={{0,32},{32,64},{64,96},{96,128},{128,160},{160,192},{192,224},{224... | collective-permute-start | bytes 983048 | tf_op jit(solution)/shard_map/ppermute | solution.py:285
  38.3 7.7 %collective-permute-start.5 = (bf16[256,512]{1,0:T(8,128)(2,1)}, bf16[256,512]{1,0:T(8,128)(2,1)S(1)}, u32[]{:S(2)}, u32[]{:S(2)}) collective-permute-start(bf16[256,512]{1,0:T(8,128)(2,1)} %add_convert_fusion), channel_id=1, source_target_pairs={{0,3},{1,0},{2,1},{3,2},{4,7},{5,4},{6,5},{7,6},{8,11},{9,8},{10,9... | collective-permute-start | bytes 786440 | tf_op jit(solution)/shard_map/ppermute | solution.py:313
  42.4 11.8 %collective-permute-start.2 = (bf16[256,512]{1,0:T(8,128)(2,1)}, bf16[256,512]{1,0:T(8,128)(2,1)S(1)}, u32[]{:S(2)}, u32[]{:S(2)}) collective-permute-start(bf16[256,512]{1,0:T(8,128)(2,1)} %get-tuple-element.30), channel_id=1, source_target_pairs={{0,3},{1,0},{2,1},{3,2},{4,7},{5,4},{6,5},{7,6},{8,11},{9,8},{10,9... | collective-permute-start | bytes 786440 | tf_op jit(solution)/shard_map/ppermute | solution.py:311
  43.2 7.5 %collective-permute-start.9 = (bf16[64,2560]{1,0:T(8,128)(2,1)S(1)}, bf16[64,2560]{1,0:T(8,128)(2,1)S(1)}, u32[]{:S(2)}, u32[]{:S(2)}) collective-permute-start(bf16[64,2560]{1,0:T(8,128)(2,1)S(1)} %collective-permute-done.7.refs_2_.refs_6_), channel_id=1, source_target_pairs={{0,224},{32,0},{64,32},{96,64},{128,96},{160,128},{192,160},{224,1... | collective-permute-start | bytes 983048 | tf_op jit(solution)/shard_map/ppermute | solution.py:288
  45.8 8.5 %collective-permute-start.10 = (bf16[64,2560]{1,0:T(8,128)(2,1)S(1)}, bf16[64,2560]{1,0:T(8,128)(2,1)S(1)}, u32[]{:S(2)}, u32[]{:S(2)}) collective-permute-start(bf16[64,2560]{1,0:T(8,128)(2,1)S(1)} %collective-permute-done.8.refs_3_.refs_7_), channel_id=1, source_target_pairs={{0,32},{32,64},{64,96},{96,128},{128,160},{160,192},{192,224},{224... | collective-permute-start | bytes 983048 | tf_op jit(solution)/shard_map/ppermute | solution.py:285
  45.9 8.4 %collective-permute-start.1 = (bf16[256,512]{1,0:T(8,128)(2,1)S(1)}, bf16[256,512]{1,0:T(8,128)(2,1)S(1)}, u32[]{:S(2)}, u32[]{:S(2)}) collective-permute-start(bf16[256,512]{1,0:T(8,128)(2,1)S(1)} %add_convert_fusion.1), channel_id=1, source_target_pairs={{0,1},{1,2},{2,3},{3,0},{4,5},{5,6},{6,7},{7,4},{8,9},{9,10},{10,1... | collective-permute-start | bytes 786440 | tf_op jit(solution)/shard_map/ppermute | solution.py:312
  50.7 11.8 %collective-permute-start.11 = (bf16[64,2560]{1,0:T(8,128)(2,1)S(1)}, bf16[64,2560]{1,0:T(8,128)(2,1)S(1)}, u32[]{:S(2)}, u32[]{:S(2)}) collective-permute-start(bf16[64,2560]{1,0:T(8,128)(2,1)S(1)} %collective-permute-done.9.refs_4_.refs_8_), channel_id=1, source_target_pairs={{0,224},{32,0},{64,32},{96,64},{128,96},{160,128},{192,160},{224,1... | collective-permute-start | bytes 983048 | tf_op jit(solution)/shard_map/ppermute | solution.py:288
  54.2 8.3 %collective-permute-start.12 = (bf16[64,2560]{1,0:T(8,128)(2,1)S(1)}, bf16[64,2560]{1,0:T(8,128)(2,1)S(1)}, u32[]{:S(2)}, u32[]{:S(2)}) collective-permute-start(bf16[64,2560]{1,0:T(8,128)(2,1)S(1)} %collective-permute-done.10.refs_5_.refs_9_), channel_id=1, source_target_pairs={{0,32},{32,64},{64,96},{96,128},{128,160},{160,192},{192,224},{224... | collective-permute-start | bytes 983048 | tf_op jit(solution)/shard_map/ppermute | solution.py:285
  69.9 6.7 %collective-permute-start.13 = (bf16[8,64,128]{2,1,0:T(8,128)(2,1)}, bf16[8,64,128]{2,1,0:T(8,128)(2,1)S(1)}, u32[]{:S(2)}, u32[]{:S(2)}) collective-permute-start(bf16[8,64,128]{2,1,0:T(8,128)(2,1)} %down.1.refs_0_), channel_id=1, source_target_pairs={{0,1},{1,2},{2,3},{3,0},{4,5},{5,6},{6,7},{7,4},{8,9},{9,10},{10,1... | collective-permute-start | bytes 393224 | tf_op jit(solution)/shard_map/ppermute | solution.py:330
  70.0 6.6 %collective-permute-start.14 = (bf16[8,64,128]{2,1,0:T(8,128)(2,1)}, bf16[8,64,128]{2,1,0:T(8,128)(2,1)S(1)}, u32[]{:S(2)}, u32[]{:S(2)}) collective-permute-start(bf16[8,64,128]{2,1,0:T(8,128)(2,1)} %down.1.refs_0_), channel_id=1, source_target_pairs={{0,2},{1,3},{2,0},{3,1},{4,6},{5,7},{6,4},{7,5},{8,10},{9,11},{10,... | collective-permute-start | bytes 393224 | tf_op jit(solution)/shard_map/ppermute | solution.py:330
  71.9 5.6 %collective-permute-start.15 = (bf16[8,64,128]{2,1,0:T(8,128)(2,1)}, bf16[8,64,128]{2,1,0:T(8,128)(2,1)S(1)}, u32[]{:S(2)}, u32[]{:S(2)}) collective-permute-start(bf16[8,64,128]{2,1,0:T(8,128)(2,1)} %down.1.refs_0_), channel_id=1, source_target_pairs={{0,3},{1,0},{2,1},{3,2},{4,7},{5,4},{6,5},{7,6},{8,11},{9,8},{10,9... | collective-permute-start | bytes 393224 | tf_op jit(solution)/shard_map/ppermute | solution.py:330
  81.6 9.8 %collective-permute-start.16 = (bf16[128,512]{1,0:T(8,128)(2,1)}, bf16[128,512]{1,0:T(8,128)(2,1)S(1)}, u32[]{:S(2)}, u32[]{:S(2)}) collective-permute-start(bf16[128,512]{1,0:T(8,128)(2,1)} %get-tuple-element.37), channel_id=1, source_target_pairs={{0,16},{4,20},{8,24},{12,28},{16,0},{20,4},{24,8},{28,12},{1,17},{... | collective-permute-start | bytes 393224 | tf_op jit(solution)/shard_map/ppermute | solution.py:337
  82.0 12.8 %collective-permute-start.17 = (bf16[128,512]{1,0:T(8,128)(2,1)}, bf16[128,512]{1,0:T(8,128)(2,1)S(1)}, u32[]{:S(2)}, u32[]{:S(2)}) collective-permute-start(bf16[128,512]{1,0:T(8,128)(2,1)} %get-tuple-element.38), channel_id=1, source_target_pairs={{0,20},{4,16},{8,28},{12,24},{16,4},{20,0},{24,12},{28,8},{1,21},{... | collective-permute-start | bytes 393224 | tf_op jit(solution)/shard_map/ppermute | solution.py:337
  88.6 8.4 %collective-permute-start.18 = (bf16[128,512]{1,0:T(8,128)(2,1)}, bf16[128,512]{1,0:T(8,128)(2,1)S(1)}, u32[]{:S(2)}, u32[]{:S(2)}) collective-permute-start(bf16[128,512]{1,0:T(8,128)(2,1)} %get-tuple-element.39), channel_id=1, source_target_pairs={{0,8},{4,12},{8,16},{12,20},{16,24},{20,28},{24,0},{28,4},{1,9},{5... | collective-permute-start | bytes 393224 | tf_op jit(solution)/shard_map/ppermute | solution.py:337
  90.0 7.0 %collective-permute-start.19 = (bf16[128,512]{1,0:T(8,128)(2,1)}, bf16[128,512]{1,0:T(8,128)(2,1)S(1)}, u32[]{:S(2)}, u32[]{:S(2)}) collective-permute-start(bf16[128,512]{1,0:T(8,128)(2,1)} %get-tuple-element.40), channel_id=1, source_target_pairs={{0,24},{4,28},{8,0},{12,4},{16,8},{20,12},{24,16},{28,20},{1,25},{... | collective-permute-start | bytes 393224 | tf_op jit(solution)/shard_map/ppermute | solution.py:337
  91.3 8.5 %collective-permute-start.20 = (bf16[128,512]{1,0:T(8,128)(2,1)}, bf16[128,512]{1,0:T(8,128)(2,1)S(1)}, u32[]{:S(2)}, u32[]{:S(2)}) collective-permute-start(bf16[128,512]{1,0:T(8,128)(2,1)} %get-tuple-element.41), channel_id=1, source_target_pairs={{0,12},{4,8},{8,20},{12,16},{16,28},{20,24},{24,4},{28,0},{1,13},{... | collective-permute-start | bytes 393224 | tf_op jit(solution)/shard_map/ppermute | solution.py:337
  91.3 8.5 %collective-permute-start.21 = (bf16[128,512]{1,0:T(8,128)(2,1)}, bf16[128,512]{1,0:T(8,128)(2,1)S(1)}, u32[]{:S(2)}, u32[]{:S(2)}) collective-permute-start(bf16[128,512]{1,0:T(8,128)(2,1)} %get-tuple-element.42), channel_id=1, source_target_pairs={{0,28},{4,24},{8,4},{12,0},{16,12},{20,8},{24,20},{28,16},{1,29},{... | collective-permute-start | bytes 393224 | tf_op jit(solution)/shard_map/ppermute | solution.py:337
  94.9 4.9 %collective-permute-start.22 = (bf16[128,512]{1,0:T(8,128)(2,1)}, bf16[128,512]{1,0:T(8,128)(2,1)S(1)}, u32[]{:S(2)}, u32[]{:S(2)}) collective-permute-start(bf16[128,512]{1,0:T(8,128)(2,1)} %get-tuple-element.43), channel_id=1, source_target_pairs={{0,4},{4,0},{8,12},{12,8},{16,20},{20,16},{24,28},{28,24},{1,5},{5... | collective-permute-start | bytes 393224 | tf_op jit(solution)/shard_map/ppermute | solution.py:337
  (17 other events, 142.7 us)

commit v4 on v3

v4 whole, which is shorter than its diff:
```python
import jax
import jax.numpy as jnp
from jax import lax
from jax.experimental import pallas as pl
from jax.experimental.pallas import tpu as pltpu
from jax.sharding import Mesh, PartitionSpec as P

F32 = jnp.float32
BF16 = jnp.bfloat16
NZ, NY, NC, NX = 8, 4, 2, 4
COLUMNS = NY * NC
CAP = 16
GROUP = ("y", "core")
WHOLE, PART = 60, 16
ROUTES = ((2, 0), (2, 1), (1, 0), (3, 0), (1, 1), (3, 1), (0, 1))
RELATIVE_Z = (0, -1, 1, -2, 2, -3, 3, -4)
ORDER, HOMES, HANDLERS = 4, 12, 20


def ring(size, step):
    return [(place, (place + step) % size) for place in range(size)]


def call(kernel, name, out, grid, ins, outs, flops, moved, limit, prefetch=0, scratch=()):
    return pl.pallas_call(
        kernel,
        out_shape=out,
        grid_spec=pltpu.PrefetchScalarGridSpec(
            num_scalar_prefetch=prefetch,
            grid=grid,
            in_specs=ins,
            out_specs=outs,
            scratch_shapes=scratch,
        ),
        compiler_params=pltpu.CompilerParams(vmem_limit_bytes=limit * 1024 * 1024),
        cost_estimate=pl.CostEstimate(flops=flops, bytes_accessed=moved, transcendentals=0),
        name=name,
    )


def base_kernel(table, tokens, weight, *outs):
    product = jnp.dot(tokens[...], weight[...], preferred_element_type=F32)
    half = product.shape[0] // 2
    for j in range(2):

        @pl.when(pl.program_id(0) == j)
        def _():
            top, bottom = outs[2 * j : 2 * j + 2]
            top[...] = product[:half].astype(top.dtype)
            bottom[...] = product[half:].astype(bottom.dtype)


def base_pair(tokens, weight, table, start, types, tile=256):
    count, inner = tokens.shape
    width = weight.shape[1] // NX
    tiles = width // tile
    first = pl.BlockSpec((count // 2, tile), lambda j, n, w: (0, n + j * (tiles - 1 - n)))
    second = pl.BlockSpec((count // 2, tile), lambda j, n, w: (0, n * j))
    return call(
        base_kernel,
        "base",
        [jax.ShapeDtypeStruct((count // 2, width), kind) for kind in types],
        (2, tiles),
        [
            pl.BlockSpec((count, inner), lambda j, n, w: (0, 0)),
            pl.BlockSpec((inner, tile), lambda j, n, w: (0, w[start + j] * tiles + n)),
        ],
        [first, first, second, second],
        4 * count * inner * width,
        2 * (count + 2 * width) * inner,
        WHOLE,
        prefetch=1,
    )(table, tokens, weight)


def dispatch_kernel(owner, tokens, out, chosen, held, made, taken, given):
    count = held.shape[0]
    slots = chosen.shape[0]
    width = held.shape[1] // taken.shape[0]
    blocks = [pl.ds(part * width, width) for part in range(taken.shape[0])]
    fetches = [
        pltpu.make_async_copy(tokens.at[:, block], held.at[:, block], taken.at[part])
        for part, block in enumerate(blocks)
    ]
    for fetch in fetches:
        fetch.start()
    mine = owner[...]
    adapter = lax.broadcasted_iota(jnp.int32, (NZ * COLUMNS, count), 0)
    member = (adapter == mine).astype(F32)
    above = lax.broadcasted_iota(jnp.int32, (count, count), 0)
    below = lax.broadcasted_iota(jnp.int32, (count, count), 1)
    before = (above < below).astype(F32).astype(BF16)
    earlier = jnp.dot(member.astype(BF16), before, preferred_element_type=F32)
    position = jnp.sum(earlier * member, axis=0, keepdims=True).astype(jnp.int32)
    place = (mine % COLUMNS) * (NZ * CAP) + (mine // COLUMNS) * CAP + position
    slot = lax.broadcasted_iota(jnp.int32, (slots, count), 0)
    chosen[...] = (slot == place).astype(F32).astype(BF16)
    copies = []
    for part, block in enumerate(blocks):
        fetches[part].wait()
        product = jnp.dot(chosen[...], held[:, block], preferred_element_type=F32)
        made[:, :, block] = product.astype(BF16).reshape(made.shape[0], made.shape[1], width)
        copy = pltpu.make_async_copy(made.at[:, :, block], out.at[:, :, block], given.at[part])
        copy.start()
        copies.append(copy)
    for copy in copies:
        copy.wait()


def dispatch(tokens, owner):
    count, inner = tokens.shape
    rows = NZ * CAP
    whole = pl.BlockSpec(memory_space=pl.ANY)
    return call(
        dispatch_kernel,
        "dispatch",
        jax.ShapeDtypeStruct((COLUMNS, rows, inner), BF16),
        (1,),
        [pl.BlockSpec((1, count), lambda n: (0, 0)), whole],
        whole,
        2 * COLUMNS * rows * count * inner,
        2 * (count + COLUMNS * rows) * inner,
        WHOLE,
        scratch=[
            pltpu.VMEM((COLUMNS * rows, count), BF16),
            pltpu.VMEM((count, inner), BF16),
            pltpu.VMEM((COLUMNS, rows, inner), BF16),
            pltpu.SemaphoreType.DMA((4,)),
            pltpu.SemaphoreType.DMA((4,)),
        ],
    )(owner.reshape(1, count), tokens)


def down_kernel(table, rows, *refs):
    panels, (out, held, kept, first, second) = refs[:NZ], refs[NZ:]
    inner = rows.shape[2]
    copies = []
    for i in range(NZ):
        start = pl.multiple_of(table[ORDER + i] * CAP, CAP)
        pair = (
            pltpu.make_async_copy(rows.at[:, pl.ds(start, CAP), :], held.at[i], first.at[i]),
            pltpu.make_async_copy(panels[i].at[:, pl.ds(0, inner)], kept.at[i], second.at[i]),
        )
        for copy in pair:
            copy.start()
        copies.append(pair)
    many, rank = 4, kept.shape[1]
    lines = COLUMNS * CAP
    for start in range(0, NZ, many):
        for pair in copies[start : start + many]:
            for copy in pair:
                copy.wait()
        product = lax.dot_general(
            kept[start : start + many].reshape(many * rank, inner),
            held[start : start + many].reshape(many * lines, inner),
            (((1,), (1,)), ((), ())),
            preferred_element_type=F32,
        )
        for i in range(many):
            block = product[i * rank : (i + 1) * rank, i * lines : (i + 1) * lines]
            out[start + i] = block.astype(BF16)


def down_step(table, rows, panels):
    inner = rows.shape[2]
    rank = panels[0].shape[0]
    lines = COLUMNS * CAP
    whole = pl.BlockSpec(memory_space=pl.ANY)
    return call(
        down_kernel,
        "down",
        jax.ShapeDtypeStruct((NZ, rank, lines), BF16),
        (1,),
        [whole] * (1 + NZ),
        pl.BlockSpec(memory_space=pltpu.VMEM),
        2 * NZ * lines * inner * rank,
        2 * NZ * (lines + rank) * inner,
        PART,
        prefetch=1,
        scratch=[
            pltpu.VMEM((NZ, COLUMNS, CAP, inner), BF16),
            pltpu.VMEM((NZ, rank, inner), BF16),
            pltpu.SemaphoreType.DMA((NZ,)),
            pltpu.SemaphoreType.DMA((NZ,)),
        ],
    )(table, rows, *panels)


def collect_kernel(*refs):
    panels, (out, arrived) = refs[:NZ], refs[NZ:]
    width = out.shape[2]
    copies = [
        pltpu.make_async_copy(
            panels[i].at[:, pl.ds(panels[i].shape[1] - width, width)], out.at[i], arrived.at[i]
        )
        for i in range(NZ)
    ]
    for copy in copies:
        copy.start()
    for copy in copies:
        copy.wait()


def collect(panels, width):
    rank = panels[0].shape[0]
    return call(
        collect_kernel,
        "collect",
        jax.ShapeDtypeStruct((NZ, rank, width), BF16),
        (1,),
        [pl.BlockSpec(memory_space=pl.ANY)] * NZ,
        pl.BlockSpec(memory_space=pltpu.VMEM),
        0,
        4 * NZ * rank * width,
        PART,
        scratch=[pltpu.SemaphoreType.DMA((NZ,))],
    )(*panels)


def up_kernel(table, *refs):
    parts, panels, outs, low = refs[:NX], refs[NX], refs[NX + 1 : -1], refs[-1]
    for i in range(NZ):
        total = parts[0][i].astype(F32)
        for part in parts[1:]:
            total = total + part[i].astype(F32)
        low[i] = total.T
        picked = [
            low[i, pl.ds(pl.multiple_of(table[HOMES + r] * CAP, CAP), CAP), :]
            for r in range(COLUMNS)
        ]
        delta = jnp.dot(
            jnp.concatenate(picked, axis=0).astype(BF16), panels[i], preferred_element_type=F32
        ).astype(BF16)
        start = pl.multiple_of(table[ORDER + i] * CAP, CAP)
        for r in range(COLUMNS):
            outs[r][pl.ds(start, CAP), :] = delta[r * CAP : (r + 1) * CAP]


def up_step(table, parts, panels):
    _, rank, width = panels.shape
    lines = COLUMNS * CAP
    near = pl.BlockSpec(memory_space=pltpu.VMEM)
    return call(
        up_kernel,
        "up",
        [jax.ShapeDtypeStruct((NZ * CAP, width), BF16)] * COLUMNS,
        (1,),
        [near] * (NX + 1),
        [near] * COLUMNS,
        2 * NZ * lines * rank * width,
        2 * NZ * (lines + rank) * width,
        PART,
        prefetch=1,
        scratch=[pltpu.VMEM((NZ, lines, rank), F32)],
    )(table, *parts, panels)


def final_kernel(table, place, base, *refs):
    pieces, (out, held, made, taken, sent) = refs[:COLUMNS], refs[COLUMNS:]
    fetch = pltpu.make_async_copy(pieces[-1], held, taken)
    fetch.start()
    rows, width = pieces[0].shape
    count = made.shape[0]
    turn = lax.broadcasted_iota(jnp.int32, (count, rows), 1)
    named = place[...]
    chosen = jnp.concatenate(
        [
            (turn + table[HANDLERS + r] * rows == named).astype(F32).astype(BF16)
            for r in range(COLUMNS)
        ],
        axis=1,
    )
    fetch.wait()
    delta = jnp.concatenate([piece[...] for piece in pieces[:-1]] + [held[...]], axis=0)
    copies = []
    parts = sent.shape[0]
    tall = count // parts
    for part in range(parts):
        some = pl.ds(part * tall, tall)
        mine = jnp.dot(
            chosen[part * tall : (part + 1) * tall], delta, preferred_element_type=F32
        )
        made[some] = (base[some] + mine).astype(made.dtype)
        copy = pltpu.make_async_copy(made.at[some], out.at[some], sent.at[part])
        copy.start()
        copies.append(copy)
    for copy in copies:
        copy.wait()


def final_step(table, place, pieces, base):
    count = place.shape[0]
    rows, width = pieces[0].shape
    slots = COLUMNS * rows
    near = pl.BlockSpec(memory_space=pltpu.VMEM)
    return call(
        final_kernel,
        "final",
        jax.ShapeDtypeStruct((count, width), BF16),
        (1,),
        [pl.BlockSpec((count, 1), lambda n, t: (0, 0))] + [near] * COLUMNS + [pl.BlockSpec(memory_space=pltpu.HBM)],
        pl.BlockSpec(memory_space=pltpu.HBM),
        2 * count * slots * width,
        2 * (slots + 4 * count) * width,
        PART,
        prefetch=1,
        scratch=[
            pltpu.VMEM((rows, width), BF16),
            pltpu.VMEM((count, width), BF16),
            pltpu.SemaphoreType.DMA,
            pltpu.SemaphoreType.DMA((2,)),
        ],
    )(table, place, base, *pieces)


def group_shift(dy, dc):
    return [
        (y * NC + core, (y + dy) % NY * NC + (core + dc) % NC)
        for y in range(NY)
        for core in range(NC)
    ]


def z_ring(chunk):
    fore = back = chunk
    found = [chunk]
    for step in range(1, 5):
        fore = lax.ppermute(fore, "z", ring(NZ, 1))
        found.append(fore)
        if step < 4:
            back = lax.ppermute(back, "z", ring(NZ, -1))
            found.append(back)
    return found


def on_device(tokens, owner, weight, down, up):
    z, y, core, x = (lax.axis_index(name) for name in ("z", "y", "core", "x"))
    count = tokens.shape[0]
    routes = ROUTES + ((0, 0),)
    table = jnp.stack(
        [(x + 2) % NX, (x + 1) % NX, (x + 3) % NX, x]
        + [(z + dz) % NZ for dz in RELATIVE_Z]
        + [(y + dy) % NY * NC + (core + dc) % NC for dy, dc in routes]
        + [(y - dy) % NY * NC + (core - dc) % NC for dy, dc in routes]
    )

    rows = lax.all_to_all(dispatch(tokens, owner), GROUP, 0, 0, tiled=True)
    panels = z_ring(jnp.concatenate([down[0], up[0]], axis=1))

    fore, back, ahead, sent = base_pair(tokens, weight, table, 0, (BF16, BF16, F32, BF16))
    tokens, fore = lax.optimization_barrier((tokens, fore))
    given, behind, top, bottom = base_pair(tokens, weight, table, 2, (BF16, F32, F32, F32))
    fore = lax.ppermute(fore, "x", ring(NX, 1))
    back = lax.ppermute(back, "x", ring(NX, -1))
    fore_a = lax.ppermute(sent, "x", ring(NX, 1))
    back_a = lax.ppermute(given, "x", ring(NX, -1))
    fore_b = lax.ppermute((ahead + fore.astype(F32)).astype(BF16), "x", ring(NX, 1))
    back_b = lax.ppermute((behind + back.astype(F32)).astype(BF16), "x", ring(NX, -1))
    base = jnp.concatenate(
        [
            top + fore_b.astype(F32) + back_a.astype(F32),
            bottom + fore_a.astype(F32) + back_b.astype(F32),
        ],
        axis=0,
    )

    named = owner[:, 0]
    turn = jnp.arange(count, dtype=jnp.int32)
    earlier = (named[None, :] == named[:, None]) & (turn[None, :] < turn[:, None])
    position = jnp.sum(earlier.astype(jnp.int32), axis=1)
    place = (named % COLUMNS) * (NZ * CAP) + (named // COLUMNS) * CAP + position

    rows, base = lax.optimization_barrier((rows, base))
    part = down_step(table, rows, panels)
    parts = [part] + [lax.ppermute(part, "x", ring(NX, step)) for step in (1, 2, 3)]
    pieces = up_step(table, parts, collect(panels, up.shape[2]))
    pieces = [
        lax.ppermute(piece, GROUP, group_shift(*route)) for piece, route in zip(pieces, ROUTES)
    ] + [pieces[-1]]
    return final_step(table, place[:, None], pieces, base)


def solution(mesh):
    fine = Mesh(mesh.devices.reshape(NZ, NY, NC, NX), ("z", "y", "core", "x"))
    dp = ("z", "y", "core")
    placed = (P(dp, "x"), P(dp, None), P("x", None), P(dp, None, "x"), P(dp, None, "x"))
    return jax.shard_map(
        on_device, mesh=fine, in_specs=placed, out_specs=P(dp, "x"), check_vma=False
    )
```

time: 105 us -> 96.9 us (0.923)
  Pallas kernels: 33.5 us -> 29.2 us
  local copies, waits for them, and re-layouts: 4.88 us -> 2.67 us
    unnamed x35 -> x13, local copies, waits for them, and re-layouts: 3.14 us -> 0.9 us
    pallas_call x1, Pallas kernels: 3.91 us -> 2.3 us  [final_step(): call(final_kernel, 'final', jax.ShapeDtypeStruct((count, width), BF16), (...]
    pallas_call x1, Pallas kernels: 3.41 us -> 2.09 us  [up_step(): call(up_kernel, 'up', [jax.ShapeDtypeStruct((NZ * CAP, width), BF16)] * C...]
    another operation x2 -> x0, other arithmetic: 1.3 us -> none  [base_pair(): jnp.stack(which)]
    pallas_call x1 -> x2, Pallas kernels: 5.92 us -> 4.7 us  [the longest x1 3.73 us: down_step(): call(down_kernel, 'down', jax.ShapeDtypeStruct((NZ, rank, lines), BF16),...]
    ppermute x3, waiting for transfers between devices: 3.35 us -> 2.22 us  [on_device(): lax.ppermute(part, 'x', ring(NX, step))]
    ppermute x7, waiting for transfers between devices: 3.62 us -> 2.56 us  [on_device(): lax.ppermute(piece, GROUP, group_shift(*route))]
  transfers between devices with their start and end apart: 24 -> 24, of which waited for: 7 -> 6; matrix products, arithmetic and copies ran while one was open for 7% -> 8% of each run, Pallas kernels for 14% -> 16%
where the time goes in v4:
time: 96.9 us; the launch traced here: 96.5 us
  starting transfers between devices  40.8 us (42%)
  Pallas kernels  29.2 us (30%)
  waiting for transfers between devices  18.3 us (19%)
  other arithmetic  4.9 us (5%)
  local copies, waits for them, and re-layouts  2.67 us (3%)
    pallas_call x2, Pallas kernels, base_pair(): call(base_kernel, 'base', [jax.ShapeDtypeStruct((count // 2, width), kind...  14.4 us
    ppermute x7, starting transfers between devices, on_device(): lax.ppermute(piece, GROUP, group_shift(*route))  14.1 us
    ppermute x3, starting transfers between devices, z_ring(): back = lax.ppermute(back, 'z', ring(NZ, -1))  10.1 us
    all_to_all x1, waiting for transfers between devices, on_device(): rows = lax.all_to_all(dispatch(tokens, owner), GROUP, 0, 0, tiled=True)  8.82 us
    all_to_all x1, starting transfers between devices, on_device(): rows = lax.all_to_all(dispatch(tokens, owner), GROUP, 0, 0, tiled=True)  7.82 us
    pallas_call x1, Pallas kernels, dispatch(): call(dispatch_kernel, 'dispatch', jax.ShapeDtypeStruct((COLUMNS, rows, in...  5.66 us
    pallas_call x1, Pallas kernels, down_step(): call(down_kernel, 'down', jax.ShapeDtypeStruct((NZ, rank, lines), BF16),...  3.73 us
    ppermute x3, waiting for transfers between devices, z_ring(): back = lax.ppermute(back, 'z', ring(NZ, -1))  3.29 us
  transfers between devices with their start and end apart: 24, of which 6 were waited for; matrix products, arithmetic and copies ran while one was open for 8% of the time, Pallas kernels for 16%

profile of v4, /device:TPU:1, one launch (start us, length us, event | category | flops | bytes accessed | tf_op | source)
XLA Modules:
  0.0 96.5 jit_solution(10827408034272750565)
XLA Ops:
  0.0 5.7 %dispatch.1 = bf16[8,128,2048]{2,1,0:T(8,128)(2,1)} custom-call(s32[1,512]{1,0:T(1,128)} %bitcast.34, bf16[512,2048]{1,0:T(8,128)(2,1)} %tokens.4), custom_call_target="tpu_custom_call" | custom-call | flops 2147483648 | bytes 6291456 | tf_op jit(solution)/shard_map/dispatch/pallas_call | solution.py:114
  5.7 7.8 %all-to-all-start = ((bf16[8,128,2048]{2,1,0:T(8,128)(2,1)}), bf16[8,128,2048]{2,1,0:T(8,128)(2,1)}, u32[]{:S(2)}, u32[]{:S(2)}) async-start(bf16[8,128,2048]{2,1,0:T(8,128)(2,1)} %dispatch.1), calls=%async_computation | async-start | bytes 8388608 | tf_op jit(solution)/shard_map/all_to_all | solution.py:347
  14.7 7.2 %base.2 = (bf16[256,512]{1,0:T(8,128)(2,1)}, bf16[256,512]{1,0:T(8,128)(2,1)}, f32[256,512]{1,0:T(8,128)}, bf16[256,512]{1,0:T(8,128)(2,1)}) custom-call(s32[28]{0:T(128)} %stack.112.table, bf16[512,2048]{1,0:T(8,128)(2,1)} %tokens.4, bf16[2048,2048]{1,0:T(8,128)(2,1)} %weight.3), custom_call_target="tpu_custom_call" | custom-call | flops 2147483648 | bytes 6291456 | tf_op jit(solution)/shard_map/base/pallas_call | solution.py:59
  21.8 2.1 %collective-permute-start.4 = (bf16[256,512]{1,0:T(8,128)(2,1)}, bf16[256,512]{1,0:T(8,128)(2,1)S(1)}, u32[]{:S(2)}, u32[]{:S(2)}) collective-permute-start(bf16[256,512]{1,0:T(8,128)(2,1)} %get-tuple-element.34), channel_id=1, source_target_pairs={{0,3},{1,0},{2,1},{3,2},{4,7},{5,4},{6,5},{7,6},{8,11},{9,8},{10,9... | collective-permute-start | bytes 786440 | tf_op jit(solution)/shard_map/ppermute | solution.py:354
  23.9 4.3 %collective-permute-start.7 = (bf16[64,2560]{1,0:T(8,128)(2,1)S(1)}, bf16[64,2560]{1,0:T(8,128)(2,1)S(1)}, u32[]{:S(2)}, u32[]{:S(2)}) collective-permute-start(bf16[64,2560]{1,0:T(8,128)(2,1)S(1)} %pad_maximum_fusion.1.refs_0_), channel_id=1, source_target_pairs={{0,224},{32,0},{64,32},{96,64},{128,96},{160,128},{192,160},{224,1... | collective-permute-start | bytes 983048 | tf_op jit(solution)/shard_map/ppermute | solution.py:331
  28.4 7.2 %base.3 = (bf16[256,512]{1,0:T(8,128)(2,1)}, f32[256,512]{1,0:T(8,128)}, f32[256,512]{1,0:T(8,128)}, f32[256,512]{1,0:T(8,128)}) custom-call(s32[28]{0:T(128)} %stack.112.table, bf16[512,2048]{1,0:T(8,128)(2,1)} %tokens.4, bf16[2048,2048]{1,0:T(8,128)(2,1)} %weight.3), custom_call_target="tpu_custom_call" | custom-call | flops 2147483648 | bytes 6291456 | tf_op jit(solution)/shard_map/base/pallas_call | solution.py:59
  35.6 1.9 %add_convert_fusion = bf16[256,512]{1,0:T(8,128)(2,1)} fusion(f32[256,512]{1,0:T(8,128)} %get-tuple-element.33, bf16[256,512]{1,0:T(8,128)(2,1)S(1)} %collective-permute-done.4), kind=kLoop, calls=%fused_computation.5 | loop fusion | flops 393216 | bytes 1048576 | tf_op jit(solution)/shard_map/convert_element_type | solution.py:358
  37.5 2.7 %collective-permute-start.5 = (bf16[256,512]{1,0:T(8,128)(2,1)}, bf16[256,512]{1,0:T(8,128)(2,1)}, u32[]{:S(2)}, u32[]{:S(2)}) collective-permute-start(bf16[256,512]{1,0:T(8,128)(2,1)} %add_convert_fusion), channel_id=1, source_target_pairs={{0,3},{1,0},{2,1},{3,2},{4,7},{5,4},{6,5},{7,6},{8,11},{9,8},{10,9... | collective-permute-start | bytes 786440 | tf_op jit(solution)/shard_map/ppermute | solution.py:358
  41.1 1.4 %collective-permute-done = bf16[256,512]{1,0:T(8,128)(2,1)S(1)} collective-permute-done((bf16[256,512]{1,0:T(8,128)(2,1)}, bf16[256,512]{1,0:T(8,128)(2,1)S(1)}, u32[]{:S(2)}, u32[]{:S(2)}) %collective-permute-start) | collective-permute-done | bytes 262176 | tf_op jit(solution)/shard_map/ppermute | solution.py:353
  42.5 2.5 %collective-permute-start.9 = (bf16[64,2560]{1,0:T(8,128)(2,1)S(1)}, bf16[64,2560]{1,0:T(8,128)(2,1)S(1)}, u32[]{:S(2)}, u32[]{:S(2)}) collective-permute-start(bf16[64,2560]{1,0:T(8,128)(2,1)S(1)} %collective-permute-done.7.refs_2_), channel_id=1, source_target_pairs={{0,224},{32,0},{64,32},{96,64},{128,96},{160,128},{192,160},{224,1... | collective-permute-start | bytes 983048 | tf_op jit(solution)/shard_map/ppermute | solution.py:331
  46.8 3.3 %collective-permute-done.9.refs_4_ = bf16[64,2560]{1,0:T(8,128)(2,1)S(1)} collective-permute-done((bf16[64,2560]{1,0:T(8,128)(2,1)S(1)}, bf16[64,2560]{1,0:T(8,128)(2,1)S(1)}, u32[]{:S(2)}, u32[]{:S(2)}) %collective-permute-start.9) | collective-permute-done | bytes 327712 | tf_op jit(solution)/shard_map/ppermute | solution.py:331
  50.1 3.3 %collective-permute-start.11 = (bf16[64,2560]{1,0:T(8,128)(2,1)S(1)}, bf16[64,2560]{1,0:T(8,128)(2,1)S(1)}, u32[]{:S(2)}, u32[]{:S(2)}) collective-permute-start(bf16[64,2560]{1,0:T(8,128)(2,1)S(1)} %collective-permute-done.9.refs_4_), channel_id=1, source_target_pairs={{0,224},{32,0},{64,32},{96,64},{128,96},{160,128},{192,160},{224,1... | collective-permute-start | bytes 983048 | tf_op jit(solution)/shard_map/ppermute | solution.py:331
  53.6 8.8 %all-to-all-done.rows = bf16[8,128,2048]{2,1,0:T(8,128)(2,1)} async-done(((bf16[8,128,2048]{2,1,0:T(8,128)(2,1)}), bf16[8,128,2048]{2,1,0:T(8,128)(2,1)}, u32[]{:S(2)}, u32[]{:S(2)}) %all-to-all-start) | async-done | bytes 4194336 | tf_op jit(solution)/shard_map/all_to_all | solution.py:347
  62.5 3.7 %down.1.refs_0_ = bf16[8,64,128]{2,1,0:T(8,128)(2,1)S(1)} custom-call(s32[28]{0:T(128)S(1)} %copy-done, bf16[8,128,2048]{2,1,0:T(8,128)(2,1)} %all-to-all-done.rows, bf16[64,2560]{1,0:T(8,128)(2,1)S(1)} %pad_maximum_fusion.1.refs_0_, bf16[64,2560]{1,0:T(8,128)(2,1)S(1)} %collective-permute-done.6.refs_1_, ...), custom_call_target="tpu_custom_call" | custom-call | flops 268435456 | bytes 6291456 | tf_op jit(solution)/shard_map/down/pallas_call | solution.py:169
  66.3 1.9 %collective-permute-start.14 = (bf16[8,64,128]{2,1,0:T(8,128)(2,1)S(1)}, bf16[8,64,128]{2,1,0:T(8,128)(2,1)}, u32[]{:S(2)}, u32[]{:S(2)}) collective-permute-start(bf16[8,64,128]{2,1,0:T(8,128)(2,1)S(1)} %down.1.refs_0_), channel_id=1, source_target_pairs={{0,2},{1,3},{2,0},{3,1},{4,6},{5,7},{6,4},{7,5},{8,10},{9,11},{10,... | collective-permute-start | bytes 393224 | tf_op jit(solution)/shard_map/ppermute | solution.py:375
  71.5 1.4 %collective-permute-done.13.refs_1_ = bf16[8,64,128]{2,1,0:T(8,128)(2,1)} collective-permute-done((bf16[8,64,128]{2,1,0:T(8,128)(2,1)S(1)}, bf16[8,64,128]{2,1,0:T(8,128)(2,1)}, u32[]{:S(2)}, u32[]{:S(2)}) %collective-permute-start.13) | collective-permute-done | bytes 131104 | tf_op jit(solution)/shard_map/ppermute | solution.py:375
  73.7 2.1 %up.1 = (bf16[128,512]{1,0:T(8,128)(2,1)S(1)}, bf16[128,512]{1,0:T(8,128)(2,1)S(1)}, bf16[128,512]{1,0:T(8,128)(2,1)S(1)}, bf16[128,512]{1,0:T(8,128)(2,1)S(1)},...) custom-call(s32[28]{0:T(128)S(1)} %copy-done, ...), custom_call_target="tpu_custom_call" | custom-call | flops 67108864 | bytes 1572864 | tf_op jit(solution)/shard_map/up/pallas_call | solution.py:243
  76.4 6.3 %collective-permute-start.17 = (bf16[128,512]{1,0:T(8,128)(2,1)S(1)}, bf16[128,512]{1,0:T(8,128)(2,1)S(1)}, u32[]{:S(2)}, u32[]{:S(2)}) collective-permute-start(bf16[128,512]{1,0:T(8,128)(2,1)S(1)} %get-tuple-element.38), channel_id=1, source_target_pairs={{0,20},{4,16},{8,28},{12,24},{16,4},{20,0},{24,12},{28,8},{1,21},{... | collective-permute-start | bytes 393224 | tf_op jit(solution)/shard_map/ppermute | solution.py:378
  82.9 1.5 %collective-permute-start.18 = (bf16[128,512]{1,0:T(8,128)(2,1)S(1)}, bf16[128,512]{1,0:T(8,128)(2,1)S(1)}, u32[]{:S(2)}, u32[]{:S(2)}) collective-permute-start(bf16[128,512]{1,0:T(8,128)(2,1)S(1)} %get-tuple-element.39), channel_id=1, source_target_pairs={{0,8},{4,12},{8,16},{12,20},{16,24},{20,28},{24,0},{28,4},{1,9},{5... | collective-permute-start | bytes 393224 | tf_op jit(solution)/shard_map/ppermute | solution.py:378
  84.4 1.3 %collective-permute-start.19 = (bf16[128,512]{1,0:T(8,128)(2,1)S(1)}, bf16[128,512]{1,0:T(8,128)(2,1)S(1)}, u32[]{:S(2)}, u32[]{:S(2)}) collective-permute-start(bf16[128,512]{1,0:T(8,128)(2,1)S(1)} %get-tuple-element.40), channel_id=1, source_target_pairs={{0,24},{4,28},{8,0},{12,4},{16,8},{20,12},{24,16},{28,20},{1,25},{... | collective-permute-start | bytes 393224 | tf_op jit(solution)/shard_map/ppermute | solution.py:378
  85.7 3.4 %collective-permute-start.21 = (bf16[128,512]{1,0:T(8,128)(2,1)S(1)}, bf16[128,512]{1,0:T(8,128)(2,1)S(1)}, u32[]{:S(2)}, u32[]{:S(2)}) collective-permute-start(bf16[128,512]{1,0:T(8,128)(2,1)S(1)} %get-tuple-element.42), channel_id=1, source_target_pairs={{0,28},{4,24},{8,4},{12,0},{16,12},{20,8},{24,20},{28,16},{1,29},{... | collective-permute-start | bytes 393224 | tf_op jit(solution)/shard_map/ppermute | solution.py:378
  90.1 1.3 %fusion.3.place = s32[512,1]{1,0:T(8,128)S(1)} fusion(s32[512,1]{1,0:T(8,128)} %copy.37, pred[512,1]{1,0:T(8,128)(4,1)S(1)} %copy.33, s32[512,1]{1,0:T(8,128)} %copy.30), kind=kLoop, calls=%fused_computation.16 | loop fusion | flops 11264 | bytes 6656 | tf_op jit(solution)/shard_map/add | solution.py:371
  91.5 2.5 %collective-permute-done.20.refs_4_ = bf16[128,512]{1,0:T(8,128)(2,1)S(1)} collective-permute-done((bf16[128,512]{1,0:T(8,128)(2,1)S(1)}, bf16[128,512]{1,0:T(8,128)(2,1)S(1)}, u32[]{:S(2)}, u32[]{:S(2)}) %collective-permute-start.20) | collective-permute-done | bytes 131104 | tf_op jit(solution)/shard_map/ppermute | solution.py:378
  94.0 2.3 %final.1 = bf16[512,512]{1,0:T(8,128)(2,1)} custom-call(s32[28]{0:T(128)S(1)} %copy-done, s32[512,1]{1,0:T(8,128)S(1)} %fusion.3.place, f32[512,512]{1,0:T(8,128)S(1)} %pad_maximum_fusion.base, bf16[128,512]{1,0:T(8,128)(2,1)S(1)} %collective-permute-done.16.refs_0_, bf16[128,512]{1,0:T(8,128)(2,1)S(1)} %collective-permute-done.17.refs_1_, ...), custom_call_target="tpu_custom_call" | custom-call | flops 536870912 | bytes 3145728 | tf_op jit(solution)/shard_map/final/pallas_call | solution.py:296
  (56 shorter events, 10.0 us)
Async XLA Ops:
  5.7 56.8 %all-to-all-start = ((bf16[8,128,2048]{2,1,0:T(8,128)(2,1)}), bf16[8,128,2048]{2,1,0:T(8,128)(2,1)}, u32[]{:S(2)}, u32[]{:S(2)}) async-start(bf16[8,128,2048]{2,1,0:T(8,128)(2,1)} %dispatch.1), calls=%async_computation | async-start | bytes 8388608 | tf_op jit(solution)/shard_map/all_to_all | solution.py:347
  13.6 14.8 %collective-permute-start.6 = (bf16[64,2560]{1,0:T(8,128)(2,1)S(1)}, bf16[64,2560]{1,0:T(8,128)(2,1)S(1)}, u32[]{:S(2)}, u32[]{:S(2)}) collective-permute-start(bf16[64,2560]{1,0:T(8,128)(2,1)S(1)} %pad_maximum_fusion.1.refs_0_), channel_id=1, source_target_pairs={{0,32},{32,64},{64,96},{96,128},{128,160},{160,192},{192,224},{224... | collective-permute-start | bytes 983048 | tf_op jit(solution)/shard_map/ppermute | solution.py:328
  21.8 13.8 %collective-permute-start.4 = (bf16[256,512]{1,0:T(8,128)(2,1)}, bf16[256,512]{1,0:T(8,128)(2,1)S(1)}, u32[]{:S(2)}, u32[]{:S(2)}) collective-permute-start(bf16[256,512]{1,0:T(8,128)(2,1)} %get-tuple-element.34), channel_id=1, source_target_pairs={{0,3},{1,0},{2,1},{3,2},{4,7},{5,4},{6,5},{7,6},{8,11},{9,8},{10,9... | collective-permute-start | bytes 786440 | tf_op jit(solution)/shard_map/ppermute | solution.py:354
  23.9 18.6 %collective-permute-start.7 = (bf16[64,2560]{1,0:T(8,128)(2,1)S(1)}, bf16[64,2560]{1,0:T(8,128)(2,1)S(1)}, u32[]{:S(2)}, u32[]{:S(2)}) collective-permute-start(bf16[64,2560]{1,0:T(8,128)(2,1)S(1)} %pad_maximum_fusion.1.refs_0_), channel_id=1, source_target_pairs={{0,224},{32,0},{64,32},{96,64},{128,96},{160,128},{192,160},{224,1... | collective-permute-start | bytes 983048 | tf_op jit(solution)/shard_map/ppermute | solution.py:331
  28.2 16.9 %collective-permute-start.3 = (bf16[256,512]{1,0:T(8,128)(2,1)}, bf16[256,512]{1,0:T(8,128)(2,1)S(1)}, u32[]{:S(2)}, u32[]{:S(2)}) collective-permute-start(bf16[256,512]{1,0:T(8,128)(2,1)} %get-tuple-element.32), channel_id=1, source_target_pairs={{0,1},{1,2},{2,3},{3,0},{4,5},{5,6},{6,7},{7,4},{8,9},{9,10},{10,1... | collective-permute-start | bytes 786440 | tf_op jit(solution)/shard_map/ppermute | solution.py:355
  28.2 14.3 %collective-permute-start = (bf16[256,512]{1,0:T(8,128)(2,1)}, bf16[256,512]{1,0:T(8,128)(2,1)S(1)}, u32[]{:S(2)}, u32[]{:S(2)}) collective-permute-start(bf16[256,512]{1,0:T(8,128)(2,1)} %get-tuple-element.29), channel_id=1, source_target_pairs={{0,1},{1,2},{2,3},{3,0},{4,5},{5,6},{6,7},{7,4},{8,9},{9,10},{10,1... | collective-permute-start | bytes 786440 | tf_op jit(solution)/shard_map/ppermute | solution.py:353
  28.4 16.6 %collective-permute-start.8 = (bf16[64,2560]{1,0:T(8,128)(2,1)S(1)}, bf16[64,2560]{1,0:T(8,128)(2,1)S(1)}, u32[]{:S(2)}, u32[]{:S(2)}) collective-permute-start(bf16[64,2560]{1,0:T(8,128)(2,1)S(1)} %collective-permute-done.6.refs_1_), channel_id=1, source_target_pairs={{0,32},{32,64},{64,96},{96,128},{128,160},{160,192},{192,224},{224... | collective-permute-start | bytes 983048 | tf_op jit(solution)/shard_map/ppermute | solution.py:328
  37.5 8.1 %collective-permute-start.5 = (bf16[256,512]{1,0:T(8,128)(2,1)}, bf16[256,512]{1,0:T(8,128)(2,1)}, u32[]{:S(2)}, u32[]{:S(2)}) collective-permute-start(bf16[256,512]{1,0:T(8,128)(2,1)} %add_convert_fusion), channel_id=1, source_target_pairs={{0,3},{1,0},{2,1},{3,2},{4,7},{5,4},{6,5},{7,6},{8,11},{9,8},{10,9... | collective-permute-start | bytes 786440 | tf_op jit(solution)/shard_map/ppermute | solution.py:358
  42.5 11.0 %collective-permute-start.2 = (bf16[256,512]{1,0:T(8,128)(2,1)}, bf16[256,512]{1,0:T(8,128)(2,1)S(1)}, u32[]{:S(2)}, u32[]{:S(2)}) collective-permute-start(bf16[256,512]{1,0:T(8,128)(2,1)} %get-tuple-element.30), channel_id=1, source_target_pairs={{0,3},{1,0},{2,1},{3,2},{4,7},{5,4},{6,5},{7,6},{8,11},{9,8},{10,9... | collective-permute-start | bytes 786440 | tf_op jit(solution)/shard_map/ppermute | solution.py:356
  42.5 7.6 %collective-permute-start.9 = (bf16[64,2560]{1,0:T(8,128)(2,1)S(1)}, bf16[64,2560]{1,0:T(8,128)(2,1)S(1)}, u32[]{:S(2)}, u32[]{:S(2)}) collective-permute-start(bf16[64,2560]{1,0:T(8,128)(2,1)S(1)} %collective-permute-done.7.refs_2_), channel_id=1, source_target_pairs={{0,224},{32,0},{64,32},{96,64},{128,96},{160,128},{192,160},{224,1... | collective-permute-start | bytes 983048 | tf_op jit(solution)/shard_map/ppermute | solution.py:331
  45.0 8.4 %collective-permute-start.10 = (bf16[64,2560]{1,0:T(8,128)(2,1)S(1)}, bf16[64,2560]{1,0:T(8,128)(2,1)S(1)}, u32[]{:S(2)}, u32[]{:S(2)}) collective-permute-start(bf16[64,2560]{1,0:T(8,128)(2,1)S(1)} %collective-permute-done.8.refs_3_), channel_id=1, source_target_pairs={{0,32},{32,64},{64,96},{96,128},{128,160},{160,192},{192,224},{224... | collective-permute-start | bytes 983048 | tf_op jit(solution)/shard_map/ppermute | solution.py:328
  45.1 8.3 %collective-permute-start.1 = (bf16[256,512]{1,0:T(8,128)(2,1)S(1)}, bf16[256,512]{1,0:T(8,128)(2,1)S(1)}, u32[]{:S(2)}, u32[]{:S(2)}) collective-permute-start(bf16[256,512]{1,0:T(8,128)(2,1)S(1)} %add_convert_fusion.1), channel_id=1, source_target_pairs={{0,1},{1,2},{2,3},{3,0},{4,5},{5,6},{6,7},{7,4},{8,9},{9,10},{10,1... | collective-permute-start | bytes 786440 | tf_op jit(solution)/shard_map/ppermute | solution.py:357
  50.1 12.4 %collective-permute-start.11 = (bf16[64,2560]{1,0:T(8,128)(2,1)S(1)}, bf16[64,2560]{1,0:T(8,128)(2,1)S(1)}, u32[]{:S(2)}, u32[]{:S(2)}) collective-permute-start(bf16[64,2560]{1,0:T(8,128)(2,1)S(1)} %collective-permute-done.9.refs_4_), channel_id=1, source_target_pairs={{0,224},{32,0},{64,32},{96,64},{128,96},{160,128},{192,160},{224,1... | collective-permute-start | bytes 983048 | tf_op jit(solution)/shard_map/ppermute | solution.py:331
  53.4 9.0 %collective-permute-start.12 = (bf16[64,2560]{1,0:T(8,128)(2,1)S(1)}, bf16[64,2560]{1,0:T(8,128)(2,1)}, u32[]{:S(2)}, u32[]{:S(2)}) collective-permute-start(bf16[64,2560]{1,0:T(8,128)(2,1)S(1)} %collective-permute-done.10.refs_5_), channel_id=1, source_target_pairs={{0,32},{32,64},{64,96},{96,128},{128,160},{160,192},{192,224},{224... | collective-permute-start | bytes 983048 | tf_op jit(solution)/shard_map/ppermute | solution.py:328
  66.2 6.6 %collective-permute-start.13 = (bf16[8,64,128]{2,1,0:T(8,128)(2,1)S(1)}, bf16[8,64,128]{2,1,0:T(8,128)(2,1)}, u32[]{:S(2)}, u32[]{:S(2)}) collective-permute-start(bf16[8,64,128]{2,1,0:T(8,128)(2,1)S(1)} %down.1.refs_0_), channel_id=1, source_target_pairs={{0,1},{1,2},{2,3},{3,0},{4,5},{5,6},{6,7},{7,4},{8,9},{9,10},{10,1... | collective-permute-start | bytes 393224 | tf_op jit(solution)/shard_map/ppermute | solution.py:375
  66.3 6.5 %collective-permute-start.14 = (bf16[8,64,128]{2,1,0:T(8,128)(2,1)S(1)}, bf16[8,64,128]{2,1,0:T(8,128)(2,1)}, u32[]{:S(2)}, u32[]{:S(2)}) collective-permute-start(bf16[8,64,128]{2,1,0:T(8,128)(2,1)S(1)} %down.1.refs_0_), channel_id=1, source_target_pairs={{0,2},{1,3},{2,0},{3,1},{4,6},{5,7},{6,4},{7,5},{8,10},{9,11},{10,... | collective-permute-start | bytes 393224 | tf_op jit(solution)/shard_map/ppermute | solution.py:375
  68.2 5.5 %collective-permute-start.15 = (bf16[8,64,128]{2,1,0:T(8,128)(2,1)S(1)}, bf16[8,64,128]{2,1,0:T(8,128)(2,1)}, u32[]{:S(2)}, u32[]{:S(2)}) collective-permute-start(bf16[8,64,128]{2,1,0:T(8,128)(2,1)S(1)} %down.1.refs_0_), channel_id=1, source_target_pairs={{0,3},{1,0},{2,1},{3,2},{4,7},{5,4},{6,5},{7,6},{8,11},{9,8},{10,9... | collective-permute-start | bytes 393224 | tf_op jit(solution)/shard_map/ppermute | solution.py:375
  75.8 9.9 %collective-permute-start.16 = (bf16[128,512]{1,0:T(8,128)(2,1)S(1)}, bf16[128,512]{1,0:T(8,128)(2,1)S(1)}, u32[]{:S(2)}, u32[]{:S(2)}) collective-permute-start(bf16[128,512]{1,0:T(8,128)(2,1)S(1)} %get-tuple-element.37), channel_id=1, source_target_pairs={{0,16},{4,20},{8,24},{12,28},{16,0},{20,4},{24,8},{28,12},{1,17},{... | collective-permute-start | bytes 393224 | tf_op jit(solution)/shard_map/ppermute | solution.py:378
  76.4 12.7 %collective-permute-start.17 = (bf16[128,512]{1,0:T(8,128)(2,1)S(1)}, bf16[128,512]{1,0:T(8,128)(2,1)S(1)}, u32[]{:S(2)}, u32[]{:S(2)}) collective-permute-start(bf16[128,512]{1,0:T(8,128)(2,1)S(1)} %get-tuple-element.38), channel_id=1, source_target_pairs={{0,20},{4,16},{8,28},{12,24},{16,4},{20,0},{24,12},{28,8},{1,21},{... | collective-permute-start | bytes 393224 | tf_op jit(solution)/shard_map/ppermute | solution.py:378
  82.9 8.5 %collective-permute-start.18 = (bf16[128,512]{1,0:T(8,128)(2,1)S(1)}, bf16[128,512]{1,0:T(8,128)(2,1)S(1)}, u32[]{:S(2)}, u32[]{:S(2)}) collective-permute-start(bf16[128,512]{1,0:T(8,128)(2,1)S(1)} %get-tuple-element.39), channel_id=1, source_target_pairs={{0,8},{4,12},{8,16},{12,20},{16,24},{20,28},{24,0},{28,4},{1,9},{5... | collective-permute-start | bytes 393224 | tf_op jit(solution)/shard_map/ppermute | solution.py:378
  84.4 7.0 %collective-permute-start.19 = (bf16[128,512]{1,0:T(8,128)(2,1)S(1)}, bf16[128,512]{1,0:T(8,128)(2,1)S(1)}, u32[]{:S(2)}, u32[]{:S(2)}) collective-permute-start(bf16[128,512]{1,0:T(8,128)(2,1)S(1)} %get-tuple-element.40), channel_id=1, source_target_pairs={{0,24},{4,28},{8,0},{12,4},{16,8},{20,12},{24,16},{28,20},{1,25},{... | collective-permute-start | bytes 393224 | tf_op jit(solution)/shard_map/ppermute | solution.py:378
  85.7 8.3 %collective-permute-start.20 = (bf16[128,512]{1,0:T(8,128)(2,1)S(1)}, bf16[128,512]{1,0:T(8,128)(2,1)S(1)}, u32[]{:S(2)}, u32[]{:S(2)}) collective-permute-start(bf16[128,512]{1,0:T(8,128)(2,1)S(1)} %get-tuple-element.41), channel_id=1, source_target_pairs={{0,12},{4,8},{8,20},{12,16},{16,28},{20,24},{24,4},{28,0},{1,13},{... | collective-permute-start | bytes 393224 | tf_op jit(solution)/shard_map/ppermute | solution.py:378
  85.7 8.3 %collective-permute-start.21 = (bf16[128,512]{1,0:T(8,128)(2,1)S(1)}, bf16[128,512]{1,0:T(8,128)(2,1)S(1)}, u32[]{:S(2)}, u32[]{:S(2)}) collective-permute-start(bf16[128,512]{1,0:T(8,128)(2,1)S(1)} %get-tuple-element.42), channel_id=1, source_target_pairs={{0,28},{4,24},{8,4},{12,0},{16,12},{20,8},{24,20},{28,16},{1,29},{... | collective-permute-start | bytes 393224 | tf_op jit(solution)/shard_map/ppermute | solution.py:378
  89.1 4.9 %collective-permute-start.22 = (bf16[128,512]{1,0:T(8,128)(2,1)S(1)}, bf16[128,512]{1,0:T(8,128)(2,1)S(1)}, u32[]{:S(2)}, u32[]{:S(2)}) collective-permute-start(bf16[128,512]{1,0:T(8,128)(2,1)S(1)} %get-tuple-element.43), channel_id=1, source_target_pairs={{0,4},{4,0},{8,12},{12,8},{16,20},{20,16},{24,28},{28,24},{1,5},{5... | collective-permute-start | bytes 393224 | tf_op jit(solution)/shard_map/ppermute | solution.py:378
  (6 other events, 89.2 us)

commit v5 on v4

--- a/solution.py
+++ b/solution.py
@@ -1,3 +1,5 @@
+import functools
+
 import jax
 import jax.numpy as jnp
 from jax import lax
@@ -10,6 +12,7 @@
 NZ, NY, NC, NX = 8, 4, 2, 4
 COLUMNS = NY * NC
 CAP = 16
+EARLY = 5
 GROUP = ("y", "core")
 WHOLE, PART = 60, 16
 ROUTES = ((2, 0), (2, 1), (1, 0), (3, 0), (1, 1), (3, 1), (0, 1))
@@ -255,31 +258,52 @@
     )(table, *parts, panels)
 
 
-def final_kernel(table, place, base, *refs):
-    pieces, (out, held, made, taken, sent) = refs[:COLUMNS], refs[COLUMNS:]
-    fetch = pltpu.make_async_copy(pieces[-1], held, taken)
-    fetch.start()
-    rows, width = pieces[0].shape
-    count = made.shape[0]
-    turn = lax.broadcasted_iota(jnp.int32, (count, rows), 1)
-    named = place[...]
+def place_pieces(table, start, named, pieces):
+    rows = pieces[0].shape[0]
+    turn = lax.broadcasted_iota(jnp.int32, (named.shape[0], rows), 1)
     chosen = jnp.concatenate(
         [
-            (turn + table[HANDLERS + r] * rows == named).astype(F32).astype(BF16)
-            for r in range(COLUMNS)
+            (turn + table[HANDLERS + start + r] * rows == named).astype(F32).astype(BF16)
+            for r in range(len(pieces))
         ],
         axis=1,
     )
-    fetch.wait()
-    delta = jnp.concatenate([piece[...] for piece in pieces[:-1]] + [held[...]], axis=0)
+    delta = jnp.concatenate([piece[...] for piece in pieces], axis=0)
+    return jnp.dot(chosen, delta, preferred_element_type=F32)
+
+
+def early_kernel(start, table, place, base, *refs):
+    pieces, out = refs[:-1], refs[-1]
+    out[...] = base[...] + place_pieces(table, start, place[...], pieces)
+
+
+def early_step(table, start, place, pieces, base):
+    count = place.shape[0]
+    rows, width = pieces[0].shape
+    near = pl.BlockSpec(memory_space=pltpu.VMEM)
+    return call(
+        functools.partial(early_kernel, start),
+        "early",
+        jax.ShapeDtypeStruct((count, width), F32),
+        (1,),
+        [pl.BlockSpec((count, 1), lambda n, t: (0, 0))] + [near] * (1 + len(pieces)),
+        near,
+        2 * count * rows * len(pieces) * width,
+        4 * count * width,
+        PART,
+        prefetch=1,
+    )(table, place, base, *pieces)
+
+
+def final_kernel(start, table, place, base, *refs):
+    pieces, (out, made, sent) = refs[:-3], refs[-3:]
+    count = made.shape[0]
     copies = []
     parts = sent.shape[0]
     tall = count // parts
     for part in range(parts):
         some = pl.ds(part * tall, tall)
-        mine = jnp.dot(
-            chosen[part * tall : (part + 1) * tall], delta, preferred_element_type=F32
-        )
+        mine = place_pieces(table, start, place[some], pieces)
         made[some] = (base[some] + mine).astype(made.dtype)
         copy = pltpu.make_async_copy(made.at[some], out.at[some], sent.at[part])
         copy.start()
@@ -288,28 +312,22 @@
         copy.wait()
 
 
-def final_step(table, place, pieces, base):
+def final_step(table, start, place, pieces, base):
     count = place.shape[0]
     rows, width = pieces[0].shape
-    slots = COLUMNS * rows
     near = pl.BlockSpec(memory_space=pltpu.VMEM)
     return call(
-        final_kernel,
+        functools.partial(final_kernel, start),
         "final",
         jax.ShapeDtypeStruct((count, width), BF16),
         (1,),
-        [pl.BlockSpec((count, 1), lambda n, t: (0, 0))] + [near] * COLUMNS + [pl.BlockSpec(memory_space=pltpu.HBM)],
+        [near] * (2 + len(pieces)),
         pl.BlockSpec(memory_space=pltpu.HBM),
-        2 * count * slots * width,
-        2 * (slots + 4 * count) * width,
+        2 * count * rows * len(pieces) * width,
+        4 * count * width,
         PART,
         prefetch=1,
-        scratch=[
-            pltpu.VMEM((rows, width), BF16),
-            pltpu.VMEM((count, width), BF16),
-            pltpu.SemaphoreType.DMA,
-            pltpu.SemaphoreType.DMA((2,)),
-        ],
+        scratch=[pltpu.VMEM((count, width), BF16), pltpu.SemaphoreType.DMA((2,))],
     )(table, place, base, *pieces)
 
 
@@ -336,7 +354,7 @@
 def on_device(tokens, owner, weight, down, up):
     z, y, core, x = (lax.axis_index(name) for name in ("z", "y", "core", "x"))
     count = tokens.shape[0]
-    routes = ROUTES + ((0, 0),)
+    routes = ((0, 0),) + ROUTES
     table = jnp.stack(
         [(x + 2) % NX, (x + 1) % NX, (x + 3) % NX, x]
         + [(z + dz) % NZ for dz in RELATIVE_Z]
@@ -372,12 +390,14 @@
 
     rows, base = lax.optimization_barrier((rows, base))
     part = down_step(table, rows, panels)
-    parts = [part] + [lax.ppermute(part, "x", ring(NX, step)) for step in (1, 2, 3)]
+    parts = [part] + [lax.ppermute(part, "x", ring(NX, step)) for step in (2, 1, 3)]
     pieces = up_step(table, parts, collect(panels, up.shape[2]))
-    pieces = [
-        lax.ppermute(piece, GROUP, group_shift(*route)) for piece, route in zip(pieces, ROUTES)
-    ] + [pieces[-1]]
-    return final_step(table, place[:, None], pieces, base)
+    pieces = [pieces[0]] + [
+        lax.ppermute(piece, GROUP, group_shift(*route)) for piece, route in zip(pieces[1:], ROUTES)
+    ]
+    place = place[:, None]
+    base = early_step(table, 0, place, pieces[:EARLY], base)
+    return final_step(table, EARLY, place, pieces[EARLY:], base)
 
 
 def solution(mesh):

time: 96.9 us -> 95.8 us (0.989)
  waiting for transfers between devices: 18.3 us -> 16 us
    ppermute x7, waiting for transfers between devices: 2.56 us -> 1.39 us  [on_device(): lax.ppermute(piece, GROUP, group_shift(*route))]
    ppermute x3, waiting for transfers between devices: 2.22 us -> 1.12 us  [on_device(): lax.ppermute(part, 'x', ring(NX, step))]
    pallas_call x1 -> x2, Pallas kernels: 2.3 us -> 2.91 us  [the longest x1 1.75 us: final_step(): call(functools.partial(final_kernel, start), 'final', jax.ShapeDtypeStruc...]
  transfers between devices with their start and end apart: 24 -> 24, of which waited for: 6 -> 6; matrix products, arithmetic and copies ran while one was open for 8% -> 8% of each run, Pallas kernels for 16% -> 17%
where the time goes in v5:
time: 95.8 us; the launch traced here: 95.3 us
  starting transfers between devices  41.3 us (43%)
  Pallas kernels  29.8 us (31%)
  waiting for transfers between devices  16 us (17%)
  other arithmetic  4.9 us (5%)
  local copies, waits for them, and re-layouts  2.67 us (3%)
    pallas_call x2, Pallas kernels, base_pair(): call(base_kernel, 'base', [jax.ShapeDtypeStruct((count // 2, width), kind...  14.4 us
    ppermute x7, starting transfers between devices, on_device(): lax.ppermute(piece, GROUP, group_shift(*route))  14 us
    ppermute x3, starting transfers between devices, z_ring(): back = lax.ppermute(back, 'z', ring(NZ, -1))  10.1 us
    all_to_all x1, waiting for transfers between devices, on_device(): rows = lax.all_to_all(dispatch(tokens, owner), GROUP, 0, 0, tiled=True)  8.82 us
    all_to_all x1, starting transfers between devices, on_device(): rows = lax.all_to_all(dispatch(tokens, owner), GROUP, 0, 0, tiled=True)  7.82 us
    pallas_call x1, Pallas kernels, dispatch(): call(dispatch_kernel, 'dispatch', jax.ShapeDtypeStruct((COLUMNS, rows, in...  5.66 us
    ppermute x3, starting transfers between devices, on_device(): lax.ppermute(part, 'x', ring(NX, step))  3.78 us
    pallas_call x1, Pallas kernels, down_step(): call(down_kernel, 'down', jax.ShapeDtypeStruct((NZ, rank, lines), BF16),...  3.73 us
  transfers between devices with their start and end apart: 24, of which 6 were waited for; matrix products, arithmetic and copies ran while one was open for 8% of the time, Pallas kernels for 17%

profile of v5, /device:TPU:1, one launch (start us, length us, event | category | flops | bytes accessed | tf_op | source)
XLA Modules:
  0.0 95.3 jit_solution(4096218363444987088)
XLA Ops:
  0.0 5.7 %dispatch.1 = bf16[8,128,2048]{2,1,0:T(8,128)(2,1)} custom-call(s32[1,512]{1,0:T(1,128)} %bitcast.34, bf16[512,2048]{1,0:T(8,128)(2,1)} %tokens.4), custom_call_target="tpu_custom_call" | custom-call | flops 2147483648 | bytes 6291456 | tf_op jit(solution)/shard_map/dispatch/pallas_call | solution.py:117
  5.7 7.8 %all-to-all-start = ((bf16[8,128,2048]{2,1,0:T(8,128)(2,1)}), bf16[8,128,2048]{2,1,0:T(8,128)(2,1)}, u32[]{:S(2)}, u32[]{:S(2)}) async-start(bf16[8,128,2048]{2,1,0:T(8,128)(2,1)} %dispatch.1), calls=%async_computation | async-start | bytes 8388608 | tf_op jit(solution)/shard_map/all_to_all | solution.py:365
  14.7 7.2 %base.2 = (bf16[256,512]{1,0:T(8,128)(2,1)}, bf16[256,512]{1,0:T(8,128)(2,1)}, f32[256,512]{1,0:T(8,128)}, bf16[256,512]{1,0:T(8,128)(2,1)}) custom-call(s32[28]{0:T(128)} %stack.112.table, bf16[512,2048]{1,0:T(8,128)(2,1)} %tokens.4, bf16[2048,2048]{1,0:T(8,128)(2,1)} %weight.3), custom_call_target="tpu_custom_call" | custom-call | flops 2147483648 | bytes 6291456 | tf_op jit(solution)/shard_map/base/pallas_call | solution.py:62
  21.8 2.1 %collective-permute-start.4 = (bf16[256,512]{1,0:T(8,128)(2,1)}, bf16[256,512]{1,0:T(8,128)(2,1)S(1)}, u32[]{:S(2)}, u32[]{:S(2)}) collective-permute-start(bf16[256,512]{1,0:T(8,128)(2,1)} %get-tuple-element.34), channel_id=1, source_target_pairs={{0,3},{1,0},{2,1},{3,2},{4,7},{5,4},{6,5},{7,6},{8,11},{9,8},{10,9... | collective-permute-start | bytes 786440 | tf_op jit(solution)/shard_map/ppermute | solution.py:372
  23.9 4.3 %collective-permute-start.7 = (bf16[64,2560]{1,0:T(8,128)(2,1)S(1)}, bf16[64,2560]{1,0:T(8,128)(2,1)S(1)}, u32[]{:S(2)}, u32[]{:S(2)}) collective-permute-start(bf16[64,2560]{1,0:T(8,128)(2,1)S(1)} %pad_maximum_fusion.1.refs_0_), channel_id=1, source_target_pairs={{0,224},{32,0},{64,32},{96,64},{128,96},{160,128},{192,160},{224,1... | collective-permute-start | bytes 983048 | tf_op jit(solution)/shard_map/ppermute | solution.py:349
  28.4 7.2 %base.3 = (bf16[256,512]{1,0:T(8,128)(2,1)}, f32[256,512]{1,0:T(8,128)}, f32[256,512]{1,0:T(8,128)}, f32[256,512]{1,0:T(8,128)}) custom-call(s32[28]{0:T(128)} %stack.112.table, bf16[512,2048]{1,0:T(8,128)(2,1)} %tokens.4, bf16[2048,2048]{1,0:T(8,128)(2,1)} %weight.3), custom_call_target="tpu_custom_call" | custom-call | flops 2147483648 | bytes 6291456 | tf_op jit(solution)/shard_map/base/pallas_call | solution.py:62
  35.6 1.9 %add_convert_fusion = bf16[256,512]{1,0:T(8,128)(2,1)} fusion(f32[256,512]{1,0:T(8,128)} %get-tuple-element.33, bf16[256,512]{1,0:T(8,128)(2,1)S(1)} %collective-permute-done.4), kind=kLoop, calls=%fused_computation.5 | loop fusion | flops 393216 | bytes 1048576 | tf_op jit(solution)/shard_map/convert_element_type | solution.py:376
  37.5 2.7 %collective-permute-start.5 = (bf16[256,512]{1,0:T(8,128)(2,1)}, bf16[256,512]{1,0:T(8,128)(2,1)}, u32[]{:S(2)}, u32[]{:S(2)}) collective-permute-start(bf16[256,512]{1,0:T(8,128)(2,1)} %add_convert_fusion), channel_id=1, source_target_pairs={{0,3},{1,0},{2,1},{3,2},{4,7},{5,4},{6,5},{7,6},{8,11},{9,8},{10,9... | collective-permute-start | bytes 786440 | tf_op jit(solution)/shard_map/ppermute | solution.py:376
  41.1 1.4 %collective-permute-done = bf16[256,512]{1,0:T(8,128)(2,1)S(1)} collective-permute-done((bf16[256,512]{1,0:T(8,128)(2,1)}, bf16[256,512]{1,0:T(8,128)(2,1)S(1)}, u32[]{:S(2)}, u32[]{:S(2)}) %collective-permute-start) | collective-permute-done | bytes 262176 | tf_op jit(solution)/shard_map/ppermute | solution.py:371
  42.5 2.5 %collective-permute-start.9 = (bf16[64,2560]{1,0:T(8,128)(2,1)S(1)}, bf16[64,2560]{1,0:T(8,128)(2,1)S(1)}, u32[]{:S(2)}, u32[]{:S(2)}) collective-permute-start(bf16[64,2560]{1,0:T(8,128)(2,1)S(1)} %collective-permute-done.7.refs_2_), channel_id=1, source_target_pairs={{0,224},{32,0},{64,32},{96,64},{128,96},{160,128},{192,160},{224,1... | collective-permute-start | bytes 983048 | tf_op jit(solution)/shard_map/ppermute | solution.py:349
  45.6 1.2 %convert_add_fusion = f32[256,512]{1,0:T(8,128)S(1)} fusion(bf16[256,512]{1,0:T(8,128)(2,1)} %collective-permute-done.5, f32[256,512]{1,0:T(8,128)} %get-tuple-element.31, bf16[256,512]{1,0:T(8,128)(2,1)S(1)} %collective-permute-done.3), kind=kLoop, calls=%fused_computation.4 | loop fusion | flops 524288 | bytes 1572864 | tf_op jit(solution)/shard_map/add | solution.py:380
  46.8 3.3 %collective-permute-done.9.refs_4_ = bf16[64,2560]{1,0:T(8,128)(2,1)S(1)} collective-permute-done((bf16[64,2560]{1,0:T(8,128)(2,1)S(1)}, bf16[64,2560]{1,0:T(8,128)(2,1)S(1)}, u32[]{:S(2)}, u32[]{:S(2)}) %collective-permute-start.9) | collective-permute-done | bytes 327712 | tf_op jit(solution)/shard_map/ppermute | solution.py:349
  50.1 3.3 %collective-permute-start.11 = (bf16[64,2560]{1,0:T(8,128)(2,1)S(1)}, bf16[64,2560]{1,0:T(8,128)(2,1)S(1)}, u32[]{:S(2)}, u32[]{:S(2)}) collective-permute-start(bf16[64,2560]{1,0:T(8,128)(2,1)S(1)} %collective-permute-done.9.refs_4_), channel_id=1, source_target_pairs={{0,224},{32,0},{64,32},{96,64},{128,96},{160,128},{192,160},{224,1... | collective-permute-start | bytes 983048 | tf_op jit(solution)/shard_map/ppermute | solution.py:349
  53.6 8.8 %all-to-all-done.rows = bf16[8,128,2048]{2,1,0:T(8,128)(2,1)} async-done(((bf16[8,128,2048]{2,1,0:T(8,128)(2,1)}), bf16[8,128,2048]{2,1,0:T(8,128)(2,1)}, u32[]{:S(2)}, u32[]{:S(2)}) %all-to-all-start) | async-done | bytes 4194336 | tf_op jit(solution)/shard_map/all_to_all | solution.py:365
  62.5 3.7 %down.1.refs_0_ = bf16[8,64,128]{2,1,0:T(8,128)(2,1)S(1)} custom-call(s32[28]{0:T(128)S(1)} %copy-done, bf16[8,128,2048]{2,1,0:T(8,128)(2,1)} %all-to-all-done.rows, bf16[64,2560]{1,0:T(8,128)(2,1)S(1)} %pad_maximum_fusion.1.refs_0_, bf16[64,2560]{1,0:T(8,128)(2,1)S(1)} %collective-permute-done.6.refs_1_, ...), custom_call_target="tpu_custom_call" | custom-call | flops 268435456 | bytes 6291456 | tf_op jit(solution)/shard_map/down/pallas_call | solution.py:172
  67.6 2.4 %collective-permute-start.15 = (bf16[8,64,128]{2,1,0:T(8,128)(2,1)S(1)}, bf16[8,64,128]{2,1,0:T(8,128)(2,1)}, u32[]{:S(2)}, u32[]{:S(2)}) collective-permute-start(bf16[8,64,128]{2,1,0:T(8,128)(2,1)S(1)} %down.1.refs_0_), channel_id=1, source_target_pairs={{0,3},{1,0},{2,1},{3,2},{4,7},{5,4},{6,5},{7,6},{8,11},{9,8},{10,9... | collective-permute-start | bytes 393224 | tf_op jit(solution)/shard_map/ppermute | solution.py:393
  73.2 2.1 %up.1 = (bf16[128,512]{1,0:T(8,128)(2,1)S(1)}, bf16[128,512]{1,0:T(8,128)(2,1)S(1)}, bf16[128,512]{1,0:T(8,128)(2,1)S(1)}, bf16[128,512]{1,0:T(8,128)(2,1)S(1)},...) custom-call(s32[28]{0:T(128)S(1)} %copy-done, ...), custom_call_target="tpu_custom_call" | custom-call | flops 67108864 | bytes 1572864 | tf_op jit(solution)/shard_map/up/pallas_call | solution.py:246
  76.1 6.1 %collective-permute-start.17 = (bf16[128,512]{1,0:T(8,128)(2,1)S(1)}, bf16[128,512]{1,0:T(8,128)(2,1)S(1)}, u32[]{:S(2)}, u32[]{:S(2)}) collective-permute-start(bf16[128,512]{1,0:T(8,128)(2,1)S(1)} %get-tuple-element.39), channel_id=1, source_target_pairs={{0,20},{4,16},{8,28},{12,24},{16,4},{20,0},{24,12},{28,8},{1,21},{... | collective-permute-start | bytes 393224 | tf_op jit(solution)/shard_map/ppermute | solution.py:396
  82.4 1.5 %collective-permute-start.18 = (bf16[128,512]{1,0:T(8,128)(2,1)S(1)}, bf16[128,512]{1,0:T(8,128)(2,1)S(1)}, u32[]{:S(2)}, u32[]{:S(2)}) collective-permute-start(bf16[128,512]{1,0:T(8,128)(2,1)S(1)} %get-tuple-element.40), channel_id=1, source_target_pairs={{0,8},{4,12},{8,16},{12,20},{16,24},{20,28},{24,0},{28,4},{1,9},{5... | collective-permute-start | bytes 393224 | tf_op jit(solution)/shard_map/ppermute | solution.py:396
  83.8 1.3 %collective-permute-start.19 = (bf16[128,512]{1,0:T(8,128)(2,1)S(1)}, bf16[128,512]{1,0:T(8,128)(2,1)S(1)}, u32[]{:S(2)}, u32[]{:S(2)}) collective-permute-start(bf16[128,512]{1,0:T(8,128)(2,1)S(1)} %get-tuple-element.41), channel_id=1, source_target_pairs={{0,24},{4,28},{8,0},{12,4},{16,8},{20,12},{24,16},{28,20},{1,25},{... | collective-permute-start | bytes 393224 | tf_op jit(solution)/shard_map/ppermute | solution.py:396
  85.1 3.4 %collective-permute-start.21 = (bf16[128,512]{1,0:T(8,128)(2,1)S(1)}, bf16[128,512]{1,0:T(8,128)(2,1)S(1)}, u32[]{:S(2)}, u32[]{:S(2)}) collective-permute-start(bf16[128,512]{1,0:T(8,128)(2,1)S(1)} %get-tuple-element.43), channel_id=1, source_target_pairs={{0,28},{4,24},{8,4},{12,0},{16,12},{20,8},{24,20},{28,16},{1,29},{... | collective-permute-start | bytes 393224 | tf_op jit(solution)/shard_map/ppermute | solution.py:396
  89.5 1.3 %fusion.3.place = s32[512,1]{1,0:T(8,128)S(1)} fusion(s32[512,1]{1,0:T(8,128)} %copy.37, pred[512,1]{1,0:T(8,128)(4,1)S(1)} %copy.33, s32[512,1]{1,0:T(8,128)} %copy.30), kind=kLoop, calls=%fused_computation.16 | loop fusion | flops 11264 | bytes 6656 | tf_op jit(solution)/shard_map/add | solution.py:389
  92.0 1.4 %collective-permute-done.20.refs_0_ = bf16[128,512]{1,0:T(8,128)(2,1)S(1)} collective-permute-done((bf16[128,512]{1,0:T(8,128)(2,1)S(1)}, bf16[128,512]{1,0:T(8,128)(2,1)S(1)}, u32[]{:S(2)}, u32[]{:S(2)}) %collective-permute-start.20) | collective-permute-done | bytes 131104 | tf_op jit(solution)/shard_map/ppermute | solution.py:396
  93.4 1.8 %final.1 = bf16[512,512]{1,0:T(8,128)(2,1)} custom-call(s32[28]{0:T(128)S(1)} %copy-done, s32[512,1]{1,0:T(8,128)S(1)} %fusion.3.place, f32[512,512]{1,0:T(8,128)S(1)} %early.1.base, bf16[128,512]{1,0:T(8,128)(2,1)S(1)} %collective-permute-done.20.refs_0_, bf16[128,512]{1,0:T(8,128)(2,1)S(1)} %collective-permute-done.21.refs_1_, ...), custom_call_target="tpu_custom_call" | custom-call | flops 201326592 | bytes 1048576 | tf_op jit(solution)/shard_map/final/pallas_call | solution.py:319
  (57 shorter events, 10.5 us)
Async XLA Ops:
  5.7 56.8 %all-to-all-start = ((bf16[8,128,2048]{2,1,0:T(8,128)(2,1)}), bf16[8,128,2048]{2,1,0:T(8,128)(2,1)}, u32[]{:S(2)}, u32[]{:S(2)}) async-start(bf16[8,128,2048]{2,1,0:T(8,128)(2,1)} %dispatch.1), calls=%async_computation | async-start | bytes 8388608 | tf_op jit(solution)/shard_map/all_to_all | solution.py:365
  13.6 14.8 %collective-permute-start.6 = (bf16[64,2560]{1,0:T(8,128)(2,1)S(1)}, bf16[64,2560]{1,0:T(8,128)(2,1)S(1)}, u32[]{:S(2)}, u32[]{:S(2)}) collective-permute-start(bf16[64,2560]{1,0:T(8,128)(2,1)S(1)} %pad_maximum_fusion.1.refs_0_), channel_id=1, source_target_pairs={{0,32},{32,64},{64,96},{96,128},{128,160},{160,192},{192,224},{224... | collective-permute-start | bytes 983048 | tf_op jit(solution)/shard_map/ppermute | solution.py:346
  21.8 13.8 %collective-permute-start.4 = (bf16[256,512]{1,0:T(8,128)(2,1)}, bf16[256,512]{1,0:T(8,128)(2,1)S(1)}, u32[]{:S(2)}, u32[]{:S(2)}) collective-permute-start(bf16[256,512]{1,0:T(8,128)(2,1)} %get-tuple-element.34), channel_id=1, source_target_pairs={{0,3},{1,0},{2,1},{3,2},{4,7},{5,4},{6,5},{7,6},{8,11},{9,8},{10,9... | collective-permute-start | bytes 786440 | tf_op jit(solution)/shard_map/ppermute | solution.py:372
  23.9 18.6 %collective-permute-start.7 = (bf16[64,2560]{1,0:T(8,128)(2,1)S(1)}, bf16[64,2560]{1,0:T(8,128)(2,1)S(1)}, u32[]{:S(2)}, u32[]{:S(2)}) collective-permute-start(bf16[64,2560]{1,0:T(8,128)(2,1)S(1)} %pad_maximum_fusion.1.refs_0_), channel_id=1, source_target_pairs={{0,224},{32,0},{64,32},{96,64},{128,96},{160,128},{192,160},{224,1... | collective-permute-start | bytes 983048 | tf_op jit(solution)/shard_map/ppermute | solution.py:349
  28.2 16.9 %collective-permute-start.3 = (bf16[256,512]{1,0:T(8,128)(2,1)}, bf16[256,512]{1,0:T(8,128)(2,1)S(1)}, u32[]{:S(2)}, u32[]{:S(2)}) collective-permute-start(bf16[256,512]{1,0:T(8,128)(2,1)} %get-tuple-element.32), channel_id=1, source_target_pairs={{0,1},{1,2},{2,3},{3,0},{4,5},{5,6},{6,7},{7,4},{8,9},{9,10},{10,1... | collective-permute-start | bytes 786440 | tf_op jit(solution)/shard_map/ppermute | solution.py:373
  28.2 14.3 %collective-permute-start = (bf16[256,512]{1,0:T(8,128)(2,1)}, bf16[256,512]{1,0:T(8,128)(2,1)S(1)}, u32[]{:S(2)}, u32[]{:S(2)}) collective-permute-start(bf16[256,512]{1,0:T(8,128)(2,1)} %get-tuple-element.29), channel_id=1, source_target_pairs={{0,1},{1,2},{2,3},{3,0},{4,5},{5,6},{6,7},{7,4},{8,9},{9,10},{10,1... | collective-permute-start | bytes 786440 | tf_op jit(solution)/shard_map/ppermute | solution.py:371
  28.4 16.6 %collective-permute-start.8 = (bf16[64,2560]{1,0:T(8,128)(2,1)S(1)}, bf16[64,2560]{1,0:T(8,128)(2,1)S(1)}, u32[]{:S(2)}, u32[]{:S(2)}) collective-permute-start(bf16[64,2560]{1,0:T(8,128)(2,1)S(1)} %collective-permute-done.6.refs_1_), channel_id=1, source_target_pairs={{0,32},{32,64},{64,96},{96,128},{128,160},{160,192},{192,224},{224... | collective-permute-start | bytes 983048 | tf_op jit(solution)/shard_map/ppermute | solution.py:346
  37.5 8.1 %collective-permute-start.5 = (bf16[256,512]{1,0:T(8,128)(2,1)}, bf16[256,512]{1,0:T(8,128)(2,1)}, u32[]{:S(2)}, u32[]{:S(2)}) collective-permute-start(bf16[256,512]{1,0:T(8,128)(2,1)} %add_convert_fusion), channel_id=1, source_target_pairs={{0,3},{1,0},{2,1},{3,2},{4,7},{5,4},{6,5},{7,6},{8,11},{9,8},{10,9... | collective-permute-start | bytes 786440 | tf_op jit(solution)/shard_map/ppermute | solution.py:376
  42.5 11.0 %collective-permute-start.2 = (bf16[256,512]{1,0:T(8,128)(2,1)}, bf16[256,512]{1,0:T(8,128)(2,1)S(1)}, u32[]{:S(2)}, u32[]{:S(2)}) collective-permute-start(bf16[256,512]{1,0:T(8,128)(2,1)} %get-tuple-element.30), channel_id=1, source_target_pairs={{0,3},{1,0},{2,1},{3,2},{4,7},{5,4},{6,5},{7,6},{8,11},{9,8},{10,9... | collective-permute-start | bytes 786440 | tf_op jit(solution)/shard_map/ppermute | solution.py:374
  42.5 7.6 %collective-permute-start.9 = (bf16[64,2560]{1,0:T(8,128)(2,1)S(1)}, bf16[64,2560]{1,0:T(8,128)(2,1)S(1)}, u32[]{:S(2)}, u32[]{:S(2)}) collective-permute-start(bf16[64,2560]{1,0:T(8,128)(2,1)S(1)} %collective-permute-done.7.refs_2_), channel_id=1, source_target_pairs={{0,224},{32,0},{64,32},{96,64},{128,96},{160,128},{192,160},{224,1... | collective-permute-start | bytes 983048 | tf_op jit(solution)/shard_map/ppermute | solution.py:349
  45.0 8.4 %collective-permute-start.10 = (bf16[64,2560]{1,0:T(8,128)(2,1)S(1)}, bf16[64,2560]{1,0:T(8,128)(2,1)S(1)}, u32[]{:S(2)}, u32[]{:S(2)}) collective-permute-start(bf16[64,2560]{1,0:T(8,128)(2,1)S(1)} %collective-permute-done.8.refs_3_), channel_id=1, source_target_pairs={{0,32},{32,64},{64,96},{96,128},{128,160},{160,192},{192,224},{224... | collective-permute-start | bytes 983048 | tf_op jit(solution)/shard_map/ppermute | solution.py:346
  45.1 8.3 %collective-permute-start.1 = (bf16[256,512]{1,0:T(8,128)(2,1)S(1)}, bf16[256,512]{1,0:T(8,128)(2,1)S(1)}, u32[]{:S(2)}, u32[]{:S(2)}) collective-permute-start(bf16[256,512]{1,0:T(8,128)(2,1)S(1)} %add_convert_fusion.1), channel_id=1, source_target_pairs={{0,1},{1,2},{2,3},{3,0},{4,5},{5,6},{6,7},{7,4},{8,9},{9,10},{10,1... | collective-permute-start | bytes 786440 | tf_op jit(solution)/shard_map/ppermute | solution.py:375
  50.1 12.4 %collective-permute-start.11 = (bf16[64,2560]{1,0:T(8,128)(2,1)S(1)}, bf16[64,2560]{1,0:T(8,128)(2,1)S(1)}, u32[]{:S(2)}, u32[]{:S(2)}) collective-permute-start(bf16[64,2560]{1,0:T(8,128)(2,1)S(1)} %collective-permute-done.9.refs_4_), channel_id=1, source_target_pairs={{0,224},{32,0},{64,32},{96,64},{128,96},{160,128},{192,160},{224,1... | collective-permute-start | bytes 983048 | tf_op jit(solution)/shard_map/ppermute | solution.py:349
  53.4 9.0 %collective-permute-start.12 = (bf16[64,2560]{1,0:T(8,128)(2,1)S(1)}, bf16[64,2560]{1,0:T(8,128)(2,1)}, u32[]{:S(2)}, u32[]{:S(2)}) collective-permute-start(bf16[64,2560]{1,0:T(8,128)(2,1)S(1)} %collective-permute-done.10.refs_5_), channel_id=1, source_target_pairs={{0,32},{32,64},{64,96},{96,128},{128,160},{160,192},{192,224},{224... | collective-permute-start | bytes 983048 | tf_op jit(solution)/shard_map/ppermute | solution.py:346
  66.2 5.9 %collective-permute-start.13 = (bf16[8,64,128]{2,1,0:T(8,128)(2,1)S(1)}, bf16[8,64,128]{2,1,0:T(8,128)(2,1)}, u32[]{:S(2)}, u32[]{:S(2)}) collective-permute-start(bf16[8,64,128]{2,1,0:T(8,128)(2,1)S(1)} %down.1.refs_0_), channel_id=1, source_target_pairs={{0,2},{1,3},{2,0},{3,1},{4,6},{5,7},{6,4},{7,5},{8,10},{9,11},{10,... | collective-permute-start | bytes 393224 | tf_op jit(solution)/shard_map/ppermute | solution.py:393
  67.3 5.8 %collective-permute-start.14 = (bf16[8,64,128]{2,1,0:T(8,128)(2,1)S(1)}, bf16[8,64,128]{2,1,0:T(8,128)(2,1)}, u32[]{:S(2)}, u32[]{:S(2)}) collective-permute-start(bf16[8,64,128]{2,1,0:T(8,128)(2,1)S(1)} %down.1.refs_0_), channel_id=1, source_target_pairs={{0,1},{1,2},{2,3},{3,0},{4,5},{5,6},{6,7},{7,4},{8,9},{9,10},{10,1... | collective-permute-start | bytes 393224 | tf_op jit(solution)/shard_map/ppermute | solution.py:393
  67.6 5.6 %collective-permute-start.15 = (bf16[8,64,128]{2,1,0:T(8,128)(2,1)S(1)}, bf16[8,64,128]{2,1,0:T(8,128)(2,1)}, u32[]{:S(2)}, u32[]{:S(2)}) collective-permute-start(bf16[8,64,128]{2,1,0:T(8,128)(2,1)S(1)} %down.1.refs_0_), channel_id=1, source_target_pairs={{0,3},{1,0},{2,1},{3,2},{4,7},{5,4},{6,5},{7,6},{8,11},{9,8},{10,9... | collective-permute-start | bytes 393224 | tf_op jit(solution)/shard_map/ppermute | solution.py:393
  75.3 9.8 %collective-permute-start.16 = (bf16[128,512]{1,0:T(8,128)(2,1)S(1)}, bf16[128,512]{1,0:T(8,128)(2,1)S(1)}, u32[]{:S(2)}, u32[]{:S(2)}) collective-permute-start(bf16[128,512]{1,0:T(8,128)(2,1)S(1)} %get-tuple-element.38), channel_id=1, source_target_pairs={{0,16},{4,20},{8,24},{12,28},{16,0},{20,4},{24,8},{28,12},{1,17},{... | collective-permute-start | bytes 393224 | tf_op jit(solution)/shard_map/ppermute | solution.py:396
  76.1 12.4 %collective-permute-start.17 = (bf16[128,512]{1,0:T(8,128)(2,1)S(1)}, bf16[128,512]{1,0:T(8,128)(2,1)S(1)}, u32[]{:S(2)}, u32[]{:S(2)}) collective-permute-start(bf16[128,512]{1,0:T(8,128)(2,1)S(1)} %get-tuple-element.39), channel_id=1, source_target_pairs={{0,20},{4,16},{8,28},{12,24},{16,4},{20,0},{24,12},{28,8},{1,21},{... | collective-permute-start | bytes 393224 | tf_op jit(solution)/shard_map/ppermute | solution.py:396
  82.4 8.5 %collective-permute-start.18 = (bf16[128,512]{1,0:T(8,128)(2,1)S(1)}, bf16[128,512]{1,0:T(8,128)(2,1)S(1)}, u32[]{:S(2)}, u32[]{:S(2)}) collective-permute-start(bf16[128,512]{1,0:T(8,128)(2,1)S(1)} %get-tuple-element.40), channel_id=1, source_target_pairs={{0,8},{4,12},{8,16},{12,20},{16,24},{20,28},{24,0},{28,4},{1,9},{5... | collective-permute-start | bytes 393224 | tf_op jit(solution)/shard_map/ppermute | solution.py:396
  83.8 7.0 %collective-permute-start.19 = (bf16[128,512]{1,0:T(8,128)(2,1)S(1)}, bf16[128,512]{1,0:T(8,128)(2,1)S(1)}, u32[]{:S(2)}, u32[]{:S(2)}) collective-permute-start(bf16[128,512]{1,0:T(8,128)(2,1)S(1)} %get-tuple-element.41), channel_id=1, source_target_pairs={{0,24},{4,28},{8,0},{12,4},{16,8},{20,12},{24,16},{28,20},{1,25},{... | collective-permute-start | bytes 393224 | tf_op jit(solution)/shard_map/ppermute | solution.py:396
  85.1 8.3 %collective-permute-start.20 = (bf16[128,512]{1,0:T(8,128)(2,1)S(1)}, bf16[128,512]{1,0:T(8,128)(2,1)S(1)}, u32[]{:S(2)}, u32[]{:S(2)}) collective-permute-start(bf16[128,512]{1,0:T(8,128)(2,1)S(1)} %get-tuple-element.42), channel_id=1, source_target_pairs={{0,12},{4,8},{8,20},{12,16},{16,28},{20,24},{24,4},{28,0},{1,13},{... | collective-permute-start | bytes 393224 | tf_op jit(solution)/shard_map/ppermute | solution.py:396
  85.1 8.3 %collective-permute-start.21 = (bf16[128,512]{1,0:T(8,128)(2,1)S(1)}, bf16[128,512]{1,0:T(8,128)(2,1)S(1)}, u32[]{:S(2)}, u32[]{:S(2)}) collective-permute-start(bf16[128,512]{1,0:T(8,128)(2,1)S(1)} %get-tuple-element.43), channel_id=1, source_target_pairs={{0,28},{4,24},{8,4},{12,0},{16,12},{20,8},{24,20},{28,16},{1,29},{... | collective-permute-start | bytes 393224 | tf_op jit(solution)/shard_map/ppermute | solution.py:396
  88.5 4.9 %collective-permute-start.22 = (bf16[128,512]{1,0:T(8,128)(2,1)S(1)}, bf16[128,512]{1,0:T(8,128)(2,1)S(1)}, u32[]{:S(2)}, u32[]{:S(2)}) collective-permute-start(bf16[128,512]{1,0:T(8,128)(2,1)S(1)} %get-tuple-element.44), channel_id=1, source_target_pairs={{0,4},{4,0},{8,12},{12,8},{16,20},{20,16},{24,28},{28,24},{1,5},{5... | collective-permute-start | bytes 393224 | tf_op jit(solution)/shard_map/ppermute | solution.py:396
  (6 other events, 89.2 us)

commit v6 on v5

--- a/solution.py
+++ b/solution.py
@@ -12,10 +12,10 @@
 NZ, NY, NC, NX = 8, 4, 2, 4
 COLUMNS = NY * NC
 CAP = 16
-EARLY = 5
+EARLY = 6
 GROUP = ("y", "core")
 WHOLE, PART = 60, 16
-ROUTES = ((2, 0), (2, 1), (1, 0), (3, 0), (1, 1), (3, 1), (0, 1))
+ROUTES = ((2, 0), (2, 1), (1, 0), (3, 0), (0, 1), (1, 1), (3, 1))
 RELATIVE_Z = (0, -1, 1, -2, 2, -3, 3, -4)
 ORDER, HOMES, HANDLERS = 4, 12, 20
 
@@ -366,7 +366,9 @@
     panels = z_ring(jnp.concatenate([down[0], up[0]], axis=1))
 
     fore, back, ahead, sent = base_pair(tokens, weight, table, 0, (BF16, BF16, F32, BF16))
-    tokens, fore = lax.optimization_barrier((tokens, fore))
+    tokens, fore, panels[1], panels[2] = lax.optimization_barrier(
+        (tokens, fore, panels[1], panels[2])
+    )
     given, behind, top, bottom = base_pair(tokens, weight, table, 2, (BF16, F32, F32, F32))
     fore = lax.ppermute(fore, "x", ring(NX, 1))
     back = lax.ppermute(back, "x", ring(NX, -1))

time: 95.8 us -> 95.4 us (level)
  starting transfers between devices: 41.3 us -> 43.4 us
  waiting for transfers between devices: 16 us -> 14 us
    ppermute x1, starting transfers between devices: 0.01 us -> 1.36 us  [on_device(): back_a = lax.ppermute(given, 'x', ring(NX, -1))]
    ppermute x1, waiting for transfers between devices: 1.38 us -> 0.04 us  [on_device(): fore = lax.ppermute(fore, 'x', ring(NX, 1))]
  transfers between devices with their start and end apart: 24 -> 24, of which waited for: 6 -> 4; matrix products, arithmetic and copies ran while one was open for 8% -> 8% of each run, Pallas kernels for 17% -> 17%
where the time goes in v6:
time: 95.4 us; the launch traced here: 95 us
  starting transfers between devices  43.4 us (45%)
  Pallas kernels  29.6 us (31%)
  waiting for transfers between devices  14 us (15%)
  other arithmetic  4.9 us (5%)
  local copies, waits for them, and re-layouts  2.66 us (3%)
    ppermute x7, starting transfers between devices, on_device(): lax.ppermute(piece, GROUP, group_shift(*route))  14.8 us
    pallas_call x2, Pallas kernels, base_pair(): call(base_kernel, 'base', [jax.ShapeDtypeStruct((count // 2, width), kind...  14.4 us
    ppermute x3, starting transfers between devices, z_ring(): back = lax.ppermute(back, 'z', ring(NZ, -1))  10.1 us
    all_to_all x1, waiting for transfers between devices, on_device(): rows = lax.all_to_all(dispatch(tokens, owner), GROUP, 0, 0, tiled=True)  8.97 us
    all_to_all x1, starting transfers between devices, on_device(): rows = lax.all_to_all(dispatch(tokens, owner), GROUP, 0, 0, tiled=True)  7.82 us
    pallas_call x1, Pallas kernels, dispatch(): call(dispatch_kernel, 'dispatch', jax.ShapeDtypeStruct((COLUMNS, rows, in...  5.66 us
    ppermute x3, starting transfers between devices, on_device(): lax.ppermute(part, 'x', ring(NX, step))  3.78 us
    pallas_call x1, Pallas kernels, down_step(): call(down_kernel, 'down', jax.ShapeDtypeStruct((NZ, rank, lines), BF16),...  3.73 us
  transfers between devices with their start and end apart: 24, of which 4 were waited for; matrix products, arithmetic and copies ran while one was open for 8% of the time, Pallas kernels for 17%

profile of v6, /device:TPU:1, one launch (start us, length us, event | category | flops | bytes accessed | tf_op | source)
XLA Modules:
  0.0 95.0 jit_solution(4549870005240652939)
XLA Ops:
  0.0 5.7 %dispatch.1 = bf16[8,128,2048]{2,1,0:T(8,128)(2,1)} custom-call(s32[1,512]{1,0:T(1,128)} %bitcast.34, bf16[512,2048]{1,0:T(8,128)(2,1)} %tokens.4), custom_call_target="tpu_custom_call" | custom-call | flops 2147483648 | bytes 6291456 | tf_op jit(solution)/shard_map/dispatch/pallas_call | solution.py:117
  5.7 7.8 %all-to-all-start = ((bf16[8,128,2048]{2,1,0:T(8,128)(2,1)}), bf16[8,128,2048]{2,1,0:T(8,128)(2,1)}, u32[]{:S(2)}, u32[]{:S(2)}) async-start(bf16[8,128,2048]{2,1,0:T(8,128)(2,1)} %dispatch.1), calls=%async_computation | async-start | bytes 8388608 | tf_op jit(solution)/shard_map/all_to_all | solution.py:365
  13.7 3.9 %collective-permute-start.1 = (bf16[64,2560]{1,0:T(8,128)(2,1)S(1)}, bf16[64,2560]{1,0:T(8,128)(2,1)S(1)}, u32[]{:S(2)}, u32[]{:S(2)}) collective-permute-start(bf16[64,2560]{1,0:T(8,128)(2,1)S(1)} %pad_maximum_fusion.1.refs_0_), channel_id=1, source_target_pairs={{0,224},{32,0},{64,32},{96,64},{128,96},{160,128},{192,160},{224,1... | collective-permute-start | bytes 983048 | tf_op jit(solution)/shard_map/ppermute | solution.py:349
  18.3 7.2 %base.2 = (bf16[256,512]{1,0:T(8,128)(2,1)}, bf16[256,512]{1,0:T(8,128)(2,1)}, f32[256,512]{1,0:T(8,128)}, bf16[256,512]{1,0:T(8,128)(2,1)}) custom-call(s32[28]{0:T(128)} %stack.112.table, bf16[512,2048]{1,0:T(8,128)(2,1)} %tokens.4, bf16[2048,2048]{1,0:T(8,128)(2,1)} %weight.3), custom_call_target="tpu_custom_call" | custom-call | flops 2147483648 | bytes 6291456 | tf_op jit(solution)/shard_map/base/pallas_call | solution.py:62
  25.5 2.5 %collective-permute-start.6 = (bf16[256,512]{1,0:T(8,128)(2,1)}, bf16[256,512]{1,0:T(8,128)(2,1)S(1)}, u32[]{:S(2)}, u32[]{:S(2)}) collective-permute-start(bf16[256,512]{1,0:T(8,128)(2,1)} %get-tuple-element.36), channel_id=1, source_target_pairs={{0,3},{1,0},{2,1},{3,2},{4,7},{5,4},{6,5},{7,6},{8,11},{9,8},{10,9... | collective-permute-start | bytes 786440 | tf_op jit(solution)/shard_map/ppermute | solution.py:374
  28.2 7.2 %base.3 = (bf16[256,512]{1,0:T(8,128)(2,1)}, f32[256,512]{1,0:T(8,128)}, f32[256,512]{1,0:T(8,128)}, f32[256,512]{1,0:T(8,128)}) custom-call(s32[28]{0:T(128)} %stack.112.table, bf16[512,2048]{1,0:T(8,128)(2,1)} %tokens.4, bf16[2048,2048]{1,0:T(8,128)(2,1)} %weight.3), custom_call_target="tpu_custom_call" | custom-call | flops 2147483648 | bytes 6291456 | tf_op jit(solution)/shard_map/base/pallas_call | solution.py:62
  35.5 1.9 %add_convert_fusion = bf16[256,512]{1,0:T(8,128)(2,1)} fusion(f32[256,512]{1,0:T(8,128)} %get-tuple-element.35, bf16[256,512]{1,0:T(8,128)(2,1)S(1)} %collective-permute-done.6), kind=kLoop, calls=%fused_computation.5 | loop fusion | flops 393216 | bytes 1048576 | tf_op jit(solution)/shard_map/convert_element_type | solution.py:378
  37.3 2.6 %collective-permute-start.7 = (bf16[256,512]{1,0:T(8,128)(2,1)}, bf16[256,512]{1,0:T(8,128)(2,1)}, u32[]{:S(2)}, u32[]{:S(2)}) collective-permute-start(bf16[256,512]{1,0:T(8,128)(2,1)} %add_convert_fusion), channel_id=1, source_target_pairs={{0,3},{1,0},{2,1},{3,2},{4,7},{5,4},{6,5},{7,6},{8,11},{9,8},{10,9... | collective-permute-start | bytes 786440 | tf_op jit(solution)/shard_map/ppermute | solution.py:378
  40.8 1.4 %collective-permute-start.4 = (bf16[256,512]{1,0:T(8,128)(2,1)}, bf16[256,512]{1,0:T(8,128)(2,1)S(1)}, u32[]{:S(2)}, u32[]{:S(2)}) collective-permute-start(bf16[256,512]{1,0:T(8,128)(2,1)} %get-tuple-element.32), channel_id=1, source_target_pairs={{0,3},{1,0},{2,1},{3,2},{4,7},{5,4},{6,5},{7,6},{8,11},{9,8},{10,9... | collective-permute-start | bytes 786440 | tf_op jit(solution)/shard_map/ppermute | solution.py:376
  42.2 2.6 %collective-permute-start.9 = (bf16[64,2560]{1,0:T(8,128)(2,1)S(1)}, bf16[64,2560]{1,0:T(8,128)(2,1)S(1)}, u32[]{:S(2)}, u32[]{:S(2)}) collective-permute-start(bf16[64,2560]{1,0:T(8,128)(2,1)S(1)} %collective-permute-done.1.refs_2_), channel_id=1, source_target_pairs={{0,224},{32,0},{64,32},{96,64},{128,96},{160,128},{192,160},{224,1... | collective-permute-start | bytes 983048 | tf_op jit(solution)/shard_map/ppermute | solution.py:349
  45.1 1.2 %convert_add_fusion = f32[256,512]{1,0:T(8,128)S(1)} fusion(bf16[256,512]{1,0:T(8,128)(2,1)} %collective-permute-done.7, f32[256,512]{1,0:T(8,128)} %get-tuple-element.33, bf16[256,512]{1,0:T(8,128)(2,1)S(1)} %collective-permute-done.5), kind=kLoop, calls=%fused_computation.4 | loop fusion | flops 524288 | bytes 1572864 | tf_op jit(solution)/shard_map/add | solution.py:382
  46.4 3.4 %collective-permute-done.9.refs_4_ = bf16[64,2560]{1,0:T(8,128)(2,1)S(1)} collective-permute-done((bf16[64,2560]{1,0:T(8,128)(2,1)S(1)}, bf16[64,2560]{1,0:T(8,128)(2,1)S(1)}, u32[]{:S(2)}, u32[]{:S(2)}) %collective-permute-start.9) | collective-permute-done | bytes 327712 | tf_op jit(solution)/shard_map/ppermute | solution.py:349
  49.7 3.5 %collective-permute-start.11 = (bf16[64,2560]{1,0:T(8,128)(2,1)S(1)}, bf16[64,2560]{1,0:T(8,128)(2,1)S(1)}, u32[]{:S(2)}, u32[]{:S(2)}) collective-permute-start(bf16[64,2560]{1,0:T(8,128)(2,1)S(1)} %collective-permute-done.9.refs_4_), channel_id=1, source_target_pairs={{0,224},{32,0},{64,32},{96,64},{128,96},{160,128},{192,160},{224,1... | collective-permute-start | bytes 983048 | tf_op jit(solution)/shard_map/ppermute | solution.py:349
  53.5 9.0 %all-to-all-done.rows = bf16[8,128,2048]{2,1,0:T(8,128)(2,1)} async-done(((bf16[8,128,2048]{2,1,0:T(8,128)(2,1)}), bf16[8,128,2048]{2,1,0:T(8,128)(2,1)}, u32[]{:S(2)}, u32[]{:S(2)}) %all-to-all-start) | async-done | bytes 4194336 | tf_op jit(solution)/shard_map/all_to_all | solution.py:365
  62.5 3.7 %down.1.refs_0_ = bf16[8,64,128]{2,1,0:T(8,128)(2,1)S(1)} custom-call(s32[28]{0:T(128)S(1)} %copy-done, bf16[8,128,2048]{2,1,0:T(8,128)(2,1)} %all-to-all-done.rows, bf16[64,2560]{1,0:T(8,128)(2,1)S(1)} %pad_maximum_fusion.1.refs_0_, bf16[64,2560]{1,0:T(8,128)(2,1)S(1)} %collective-permute-done.refs_1_, bf16[64,2560]{1,0:T(8,128)(2,1)S(1)} %collective-permute-done.1.refs_2_, ...), custom_call_target="tpu_custom_call" | custom-call | flops 268435456 | bytes 6291456 | tf_op jit(solution)/shard_map/down/pallas_call | solution.py:172
  67.6 2.4 %collective-permute-start.15 = (bf16[8,64,128]{2,1,0:T(8,128)(2,1)S(1)}, bf16[8,64,128]{2,1,0:T(8,128)(2,1)}, u32[]{:S(2)}, u32[]{:S(2)}) collective-permute-start(bf16[8,64,128]{2,1,0:T(8,128)(2,1)S(1)} %down.1.refs_0_), channel_id=1, source_target_pairs={{0,3},{1,0},{2,1},{3,2},{4,7},{5,4},{6,5},{7,6},{8,11},{9,8},{10,9... | collective-permute-start | bytes 393224 | tf_op jit(solution)/shard_map/ppermute | solution.py:395
  73.1 2.1 %up.1 = (bf16[128,512]{1,0:T(8,128)(2,1)S(1)}, bf16[128,512]{1,0:T(8,128)(2,1)S(1)}, bf16[128,512]{1,0:T(8,128)(2,1)S(1)}, bf16[128,512]{1,0:T(8,128)(2,1)S(1)},...) custom-call(s32[28]{0:T(128)S(1)} %copy-done, ...), custom_call_target="tpu_custom_call" | custom-call | flops 67108864 | bytes 1572864 | tf_op jit(solution)/shard_map/up/pallas_call | solution.py:246
  75.9 6.0 %collective-permute-start.17 = (bf16[128,512]{1,0:T(8,128)(2,1)S(1)}, bf16[128,512]{1,0:T(8,128)(2,1)S(1)}, u32[]{:S(2)}, u32[]{:S(2)}) collective-permute-start(bf16[128,512]{1,0:T(8,128)(2,1)S(1)} %get-tuple-element.43), channel_id=1, source_target_pairs={{0,20},{4,16},{8,28},{12,24},{16,4},{20,0},{24,12},{28,8},{1,21},{... | collective-permute-start | bytes 393224 | tf_op jit(solution)/shard_map/ppermute | solution.py:398
  82.2 1.5 %collective-permute-start.18 = (bf16[128,512]{1,0:T(8,128)(2,1)S(1)}, bf16[128,512]{1,0:T(8,128)(2,1)S(1)}, u32[]{:S(2)}, u32[]{:S(2)}) collective-permute-start(bf16[128,512]{1,0:T(8,128)(2,1)S(1)} %get-tuple-element.44), channel_id=1, source_target_pairs={{0,8},{4,12},{8,16},{12,20},{16,24},{20,28},{24,0},{28,4},{1,9},{5... | collective-permute-start | bytes 393224 | tf_op jit(solution)/shard_map/ppermute | solution.py:398
  83.7 1.3 %collective-permute-start.19 = (bf16[128,512]{1,0:T(8,128)(2,1)S(1)}, bf16[128,512]{1,0:T(8,128)(2,1)S(1)}, u32[]{:S(2)}, u32[]{:S(2)}) collective-permute-start(bf16[128,512]{1,0:T(8,128)(2,1)S(1)} %get-tuple-element.45), channel_id=1, source_target_pairs={{0,24},{4,28},{8,0},{12,4},{16,8},{20,12},{24,16},{28,20},{1,25},{... | collective-permute-start | bytes 393224 | tf_op jit(solution)/shard_map/ppermute | solution.py:398
  86.7 3.5 %collective-permute-start.22 = (bf16[128,512]{1,0:T(8,128)(2,1)S(1)}, bf16[128,512]{1,0:T(8,128)(2,1)S(1)}, u32[]{:S(2)}, u32[]{:S(2)}) collective-permute-start(bf16[128,512]{1,0:T(8,128)(2,1)S(1)} %get-tuple-element.48), channel_id=1, source_target_pairs={{0,28},{4,24},{8,4},{12,0},{16,12},{20,8},{24,20},{28,16},{1,29},{... | collective-permute-start | bytes 393224 | tf_op jit(solution)/shard_map/ppermute | solution.py:398
  90.2 1.3 %fusion.3.place = s32[512,1]{1,0:T(8,128)S(1)} fusion(s32[512,1]{1,0:T(8,128)} %copy.37, pred[512,1]{1,0:T(8,128)(4,1)S(1)} %copy.33, s32[512,1]{1,0:T(8,128)} %copy.30), kind=kLoop, calls=%fused_computation.16 | loop fusion | flops 11264 | bytes 6656 | tf_op jit(solution)/shard_map/add | solution.py:391
  91.5 1.2 %early.1.base = f32[512,512]{1,0:T(8,128)S(1)} custom-call(s32[28]{0:T(128)S(1)} %copy-done, s32[512,1]{1,0:T(8,128)S(1)} %fusion.3.place, f32[512,512]{1,0:T(8,128)S(1)} %pad_maximum_fusion.base, bf16[128,512]{1,0:T(8,128)(2,1)S(1)} %get-tuple-element.41.refs_0_, bf16[128,512]{1,0:T(8,128)(2,1)S(1)} %collective-permute-done.16.refs_1_, ...), custom_call_target="tpu_custom_call" | custom-call | flops 402653184 | bytes 1048576 | tf_op jit(solution)/shard_map/early/pallas_call | solution.py:284
  93.2 1.6 %final.1 = bf16[512,512]{1,0:T(8,128)(2,1)} custom-call(s32[28]{0:T(128)S(1)} %copy-done, s32[512,1]{1,0:T(8,128)S(1)} %fusion.3.place, f32[512,512]{1,0:T(8,128)S(1)} %early.1.base, bf16[128,512]{1,0:T(8,128)(2,1)S(1)} %collective-permute-done.21.refs_0_, bf16[128,512]{1,0:T(8,128)(2,1)S(1)} %collective-permute-done.22.refs_1_), custom_call_target="tpu_custom_call" | custom-call | flops 134217728 | bytes 1048576 | tf_op jit(solution)/shard_map/final/pallas_call | solution.py:319
  (57 shorter events, 10.1 us)
Async XLA Ops:
  5.7 56.8 %all-to-all-start = ((bf16[8,128,2048]{2,1,0:T(8,128)(2,1)}), bf16[8,128,2048]{2,1,0:T(8,128)(2,1)}, u32[]{:S(2)}, u32[]{:S(2)}) async-start(bf16[8,128,2048]{2,1,0:T(8,128)(2,1)} %dispatch.1), calls=%async_computation | async-start | bytes 8388608 | tf_op jit(solution)/shard_map/all_to_all | solution.py:365
  13.6 14.4 %collective-permute-start = (bf16[64,2560]{1,0:T(8,128)(2,1)S(1)}, bf16[64,2560]{1,0:T(8,128)(2,1)S(1)}, u32[]{:S(2)}, u32[]{:S(2)}) collective-permute-start(bf16[64,2560]{1,0:T(8,128)(2,1)S(1)} %pad_maximum_fusion.1.refs_0_), channel_id=1, source_target_pairs={{0,32},{32,64},{64,96},{96,128},{128,160},{160,192},{192,224},{224... | collective-permute-start | bytes 983048 | tf_op jit(solution)/shard_map/ppermute | solution.py:346
  13.7 14.3 %collective-permute-start.1 = (bf16[64,2560]{1,0:T(8,128)(2,1)S(1)}, bf16[64,2560]{1,0:T(8,128)(2,1)S(1)}, u32[]{:S(2)}, u32[]{:S(2)}) collective-permute-start(bf16[64,2560]{1,0:T(8,128)(2,1)S(1)} %pad_maximum_fusion.1.refs_0_), channel_id=1, source_target_pairs={{0,224},{32,0},{64,32},{96,64},{128,96},{160,128},{192,160},{224,1... | collective-permute-start | bytes 983048 | tf_op jit(solution)/shard_map/ppermute | solution.py:349
  25.5 10.0 %collective-permute-start.6 = (bf16[256,512]{1,0:T(8,128)(2,1)}, bf16[256,512]{1,0:T(8,128)(2,1)S(1)}, u32[]{:S(2)}, u32[]{:S(2)}) collective-permute-start(bf16[256,512]{1,0:T(8,128)(2,1)} %get-tuple-element.36), channel_id=1, source_target_pairs={{0,3},{1,0},{2,1},{3,2},{4,7},{5,4},{6,5},{7,6},{8,11},{9,8},{10,9... | collective-permute-start | bytes 786440 | tf_op jit(solution)/shard_map/ppermute | solution.py:374
  27.9 17.0 %collective-permute-start.5 = (bf16[256,512]{1,0:T(8,128)(2,1)}, bf16[256,512]{1,0:T(8,128)(2,1)S(1)}, u32[]{:S(2)}, u32[]{:S(2)}) collective-permute-start(bf16[256,512]{1,0:T(8,128)(2,1)} %get-tuple-element.34), channel_id=1, source_target_pairs={{0,1},{1,2},{2,3},{3,0},{4,5},{5,6},{6,7},{7,4},{8,9},{9,10},{10,1... | collective-permute-start | bytes 786440 | tf_op jit(solution)/shard_map/ppermute | solution.py:375
  28.0 14.2 %collective-permute-start.2 = (bf16[256,512]{1,0:T(8,128)(2,1)}, bf16[256,512]{1,0:T(8,128)(2,1)S(1)}, u32[]{:S(2)}, u32[]{:S(2)}) collective-permute-start(bf16[256,512]{1,0:T(8,128)(2,1)} %get-tuple-element.31), channel_id=1, source_target_pairs={{0,1},{1,2},{2,3},{3,0},{4,5},{5,6},{6,7},{7,4},{8,9},{9,10},{10,1... | collective-permute-start | bytes 786440 | tf_op jit(solution)/shard_map/ppermute | solution.py:373
  28.2 16.6 %collective-permute-start.8 = (bf16[64,2560]{1,0:T(8,128)(2,1)S(1)}, bf16[64,2560]{1,0:T(8,128)(2,1)S(1)}, u32[]{:S(2)}, u32[]{:S(2)}) collective-permute-start(bf16[64,2560]{1,0:T(8,128)(2,1)S(1)} %collective-permute-done.refs_1_), channel_id=1, source_target_pairs={{0,32},{32,64},{64,96},{96,128},{128,160},{160,192},{192,224},{224... | collective-permute-start | bytes 983048 | tf_op jit(solution)/shard_map/ppermute | solution.py:346
  37.3 7.8 %collective-permute-start.7 = (bf16[256,512]{1,0:T(8,128)(2,1)}, bf16[256,512]{1,0:T(8,128)(2,1)}, u32[]{:S(2)}, u32[]{:S(2)}) collective-permute-start(bf16[256,512]{1,0:T(8,128)(2,1)} %add_convert_fusion), channel_id=1, source_target_pairs={{0,3},{1,0},{2,1},{3,2},{4,7},{5,4},{6,5},{7,6},{8,11},{9,8},{10,9... | collective-permute-start | bytes 786440 | tf_op jit(solution)/shard_map/ppermute | solution.py:378
  40.8 12.5 %collective-permute-start.4 = (bf16[256,512]{1,0:T(8,128)(2,1)}, bf16[256,512]{1,0:T(8,128)(2,1)S(1)}, u32[]{:S(2)}, u32[]{:S(2)}) collective-permute-start(bf16[256,512]{1,0:T(8,128)(2,1)} %get-tuple-element.32), channel_id=1, source_target_pairs={{0,3},{1,0},{2,1},{3,2},{4,7},{5,4},{6,5},{7,6},{8,11},{9,8},{10,9... | collective-permute-start | bytes 786440 | tf_op jit(solution)/shard_map/ppermute | solution.py:376
  42.2 7.5 %collective-permute-start.9 = (bf16[64,2560]{1,0:T(8,128)(2,1)S(1)}, bf16[64,2560]{1,0:T(8,128)(2,1)S(1)}, u32[]{:S(2)}, u32[]{:S(2)}) collective-permute-start(bf16[64,2560]{1,0:T(8,128)(2,1)S(1)} %collective-permute-done.1.refs_2_), channel_id=1, source_target_pairs={{0,224},{32,0},{64,32},{96,64},{128,96},{160,128},{192,160},{224,1... | collective-permute-start | bytes 983048 | tf_op jit(solution)/shard_map/ppermute | solution.py:349
  44.9 8.4 %collective-permute-start.10 = (bf16[64,2560]{1,0:T(8,128)(2,1)S(1)}, bf16[64,2560]{1,0:T(8,128)(2,1)S(1)}, u32[]{:S(2)}, u32[]{:S(2)}) collective-permute-start(bf16[64,2560]{1,0:T(8,128)(2,1)S(1)} %collective-permute-done.8.refs_3_), channel_id=1, source_target_pairs={{0,32},{32,64},{64,96},{96,128},{128,160},{160,192},{192,224},{224... | collective-permute-start | bytes 983048 | tf_op jit(solution)/shard_map/ppermute | solution.py:346
  45.0 8.3 %collective-permute-start.3 = (bf16[256,512]{1,0:T(8,128)(2,1)S(1)}, bf16[256,512]{1,0:T(8,128)(2,1)S(1)}, u32[]{:S(2)}, u32[]{:S(2)}) collective-permute-start(bf16[256,512]{1,0:T(8,128)(2,1)S(1)} %add_convert_fusion.1), channel_id=1, source_target_pairs={{0,1},{1,2},{2,3},{3,0},{4,5},{5,6},{6,7},{7,4},{8,9},{9,10},{10,1... | collective-permute-start | bytes 786440 | tf_op jit(solution)/shard_map/ppermute | solution.py:377
  49.7 12.7 %collective-permute-start.11 = (bf16[64,2560]{1,0:T(8,128)(2,1)S(1)}, bf16[64,2560]{1,0:T(8,128)(2,1)S(1)}, u32[]{:S(2)}, u32[]{:S(2)}) collective-permute-start(bf16[64,2560]{1,0:T(8,128)(2,1)S(1)} %collective-permute-done.9.refs_4_), channel_id=1, source_target_pairs={{0,224},{32,0},{64,32},{96,64},{128,96},{160,128},{192,160},{224,1... | collective-permute-start | bytes 983048 | tf_op jit(solution)/shard_map/ppermute | solution.py:349
  53.3 9.2 %collective-permute-start.12 = (bf16[64,2560]{1,0:T(8,128)(2,1)S(1)}, bf16[64,2560]{1,0:T(8,128)(2,1)}, u32[]{:S(2)}, u32[]{:S(2)}) collective-permute-start(bf16[64,2560]{1,0:T(8,128)(2,1)S(1)} %collective-permute-done.10.refs_5_), channel_id=1, source_target_pairs={{0,32},{32,64},{64,96},{96,128},{128,160},{160,192},{192,224},{224... | collective-permute-start | bytes 983048 | tf_op jit(solution)/shard_map/ppermute | solution.py:346
  66.2 5.9 %collective-permute-start.13 = (bf16[8,64,128]{2,1,0:T(8,128)(2,1)S(1)}, bf16[8,64,128]{2,1,0:T(8,128)(2,1)}, u32[]{:S(2)}, u32[]{:S(2)}) collective-permute-start(bf16[8,64,128]{2,1,0:T(8,128)(2,1)S(1)} %down.1.refs_0_), channel_id=1, source_target_pairs={{0,2},{1,3},{2,0},{3,1},{4,6},{5,7},{6,4},{7,5},{8,10},{9,11},{10,... | collective-permute-start | bytes 393224 | tf_op jit(solution)/shard_map/ppermute | solution.py:395
  67.3 5.8 %collective-permute-start.14 = (bf16[8,64,128]{2,1,0:T(8,128)(2,1)S(1)}, bf16[8,64,128]{2,1,0:T(8,128)(2,1)}, u32[]{:S(2)}, u32[]{:S(2)}) collective-permute-start(bf16[8,64,128]{2,1,0:T(8,128)(2,1)S(1)} %down.1.refs_0_), channel_id=1, source_target_pairs={{0,1},{1,2},{2,3},{3,0},{4,5},{5,6},{6,7},{7,4},{8,9},{9,10},{10,1... | collective-permute-start | bytes 393224 | tf_op jit(solution)/shard_map/ppermute | solution.py:395
  67.6 5.5 %collective-permute-start.15 = (bf16[8,64,128]{2,1,0:T(8,128)(2,1)S(1)}, bf16[8,64,128]{2,1,0:T(8,128)(2,1)}, u32[]{:S(2)}, u32[]{:S(2)}) collective-permute-start(bf16[8,64,128]{2,1,0:T(8,128)(2,1)S(1)} %down.1.refs_0_), channel_id=1, source_target_pairs={{0,3},{1,0},{2,1},{3,2},{4,7},{5,4},{6,5},{7,6},{8,11},{9,8},{10,9... | collective-permute-start | bytes 393224 | tf_op jit(solution)/shard_map/ppermute | solution.py:395
  75.2 10.3 %collective-permute-start.16 = (bf16[128,512]{1,0:T(8,128)(2,1)S(1)}, bf16[128,512]{1,0:T(8,128)(2,1)S(1)}, u32[]{:S(2)}, u32[]{:S(2)}) collective-permute-start(bf16[128,512]{1,0:T(8,128)(2,1)S(1)} %get-tuple-element.42), channel_id=1, source_target_pairs={{0,16},{4,20},{8,24},{12,28},{16,0},{20,4},{24,8},{28,12},{1,17},{... | collective-permute-start | bytes 393224 | tf_op jit(solution)/shard_map/ppermute | solution.py:398
  75.9 10.7 %collective-permute-start.17 = (bf16[128,512]{1,0:T(8,128)(2,1)S(1)}, bf16[128,512]{1,0:T(8,128)(2,1)S(1)}, u32[]{:S(2)}, u32[]{:S(2)}) collective-permute-start(bf16[128,512]{1,0:T(8,128)(2,1)S(1)} %get-tuple-element.43), channel_id=1, source_target_pairs={{0,20},{4,16},{8,28},{12,24},{16,4},{20,0},{24,12},{28,8},{1,21},{... | collective-permute-start | bytes 393224 | tf_op jit(solution)/shard_map/ppermute | solution.py:398
  82.2 9.3 %collective-permute-start.18 = (bf16[128,512]{1,0:T(8,128)(2,1)S(1)}, bf16[128,512]{1,0:T(8,128)(2,1)S(1)}, u32[]{:S(2)}, u32[]{:S(2)}) collective-permute-start(bf16[128,512]{1,0:T(8,128)(2,1)S(1)} %get-tuple-element.44), channel_id=1, source_target_pairs={{0,8},{4,12},{8,16},{12,20},{16,24},{20,28},{24,0},{28,4},{1,9},{5... | collective-permute-start | bytes 393224 | tf_op jit(solution)/shard_map/ppermute | solution.py:398
  83.7 7.8 %collective-permute-start.19 = (bf16[128,512]{1,0:T(8,128)(2,1)S(1)}, bf16[128,512]{1,0:T(8,128)(2,1)S(1)}, u32[]{:S(2)}, u32[]{:S(2)}) collective-permute-start(bf16[128,512]{1,0:T(8,128)(2,1)S(1)} %get-tuple-element.45), channel_id=1, source_target_pairs={{0,24},{4,28},{8,0},{12,4},{16,8},{20,12},{24,16},{28,20},{1,25},{... | collective-permute-start | bytes 393224 | tf_op jit(solution)/shard_map/ppermute | solution.py:398
  85.0 6.5 %collective-permute-start.20 = (bf16[128,512]{1,0:T(8,128)(2,1)S(1)}, bf16[128,512]{1,0:T(8,128)(2,1)S(1)}, u32[]{:S(2)}, u32[]{:S(2)}) collective-permute-start(bf16[128,512]{1,0:T(8,128)(2,1)S(1)} %get-tuple-element.46), channel_id=1, source_target_pairs={{0,4},{4,0},{8,12},{12,8},{16,20},{20,16},{24,28},{28,24},{1,5},{5... | collective-permute-start | bytes 393224 | tf_op jit(solution)/shard_map/ppermute | solution.py:398
  85.6 7.6 %collective-permute-start.21 = (bf16[128,512]{1,0:T(8,128)(2,1)S(1)}, bf16[128,512]{1,0:T(8,128)(2,1)S(1)}, u32[]{:S(2)}, u32[]{:S(2)}) collective-permute-start(bf16[128,512]{1,0:T(8,128)(2,1)S(1)} %get-tuple-element.47), channel_id=1, source_target_pairs={{0,12},{4,8},{8,20},{12,16},{16,28},{20,24},{24,4},{28,0},{1,13},{... | collective-permute-start | bytes 393224 | tf_op jit(solution)/shard_map/ppermute | solution.py:398
  86.7 6.5 %collective-permute-start.22 = (bf16[128,512]{1,0:T(8,128)(2,1)S(1)}, bf16[128,512]{1,0:T(8,128)(2,1)S(1)}, u32[]{:S(2)}, u32[]{:S(2)}) collective-permute-start(bf16[128,512]{1,0:T(8,128)(2,1)S(1)} %get-tuple-element.48), channel_id=1, source_target_pairs={{0,28},{4,24},{8,4},{12,0},{16,12},{20,8},{24,20},{28,16},{1,29},{... | collective-permute-start | bytes 393224 | tf_op jit(solution)/shard_map/ppermute | solution.py:398
  (6 other events, 89.4 us)

commit v7 on v6

--- a/solution.py
+++ b/solution.py
@@ -12,7 +12,7 @@
 NZ, NY, NC, NX = 8, 4, 2, 4
 COLUMNS = NY * NC
 CAP = 16
-EARLY = 6
+EARLY = 7
 GROUP = ("y", "core")
 WHOLE, PART = 60, 16
 ROUTES = ((2, 0), (2, 1), (1, 0), (3, 0), (0, 1), (1, 1), (3, 1))

time: 95.4 us -> 96.7 us (1.014)
  waiting for transfers between devices: 14 us -> 15.2 us
    ppermute x7, waiting for transfers between devices: 0.52 us -> 1.69 us  [on_device(): lax.ppermute(piece, GROUP, group_shift(*route))]
where the time goes in v7:
time: 96.7 us; the launch traced here: 96.3 us
  starting transfers between devices  43.4 us (45%)
  Pallas kernels  29.8 us (31%)
  waiting for transfers between devices  15.2 us (16%)
  other arithmetic  4.9 us (5%)
  local copies, waits for them, and re-layouts  2.66 us (3%)
    ppermute x7, starting transfers between devices, on_device(): lax.ppermute(piece, GROUP, group_shift(*route))  14.8 us
    pallas_call x2, Pallas kernels, base_pair(): call(base_kernel, 'base', [jax.ShapeDtypeStruct((count // 2, width), kind...  14.4 us
    ppermute x3, starting transfers between devices, z_ring(): back = lax.ppermute(back, 'z', ring(NZ, -1))  10.1 us
    all_to_all x1, waiting for transfers between devices, on_device(): rows = lax.all_to_all(dispatch(tokens, owner), GROUP, 0, 0, tiled=True)  8.97 us
    all_to_all x1, starting transfers between devices, on_device(): rows = lax.all_to_all(dispatch(tokens, owner), GROUP, 0, 0, tiled=True)  7.82 us
    pallas_call x1, Pallas kernels, dispatch(): call(dispatch_kernel, 'dispatch', jax.ShapeDtypeStruct((COLUMNS, rows, in...  5.66 us
    ppermute x3, starting transfers between devices, on_device(): lax.ppermute(part, 'x', ring(NX, step))  3.78 us
    pallas_call x1, Pallas kernels, down_step(): call(down_kernel, 'down', jax.ShapeDtypeStruct((NZ, rank, lines), BF16),...  3.73 us
  transfers between devices with their start and end apart: 24, of which 4 were waited for; matrix products, arithmetic and copies ran while one was open for 8% of the time, Pallas kernels for 17%

profile of v7, /device:TPU:1, one launch (start us, length us, event | category | flops | bytes accessed | tf_op | source)
XLA Modules:
  0.0 96.3 jit_solution(7404555513890191063)
XLA Ops:
  0.0 5.7 %dispatch.1 = bf16[8,128,2048]{2,1,0:T(8,128)(2,1)} custom-call(s32[1,512]{1,0:T(1,128)} %bitcast.34, bf16[512,2048]{1,0:T(8,128)(2,1)} %tokens.4), custom_call_target="tpu_custom_call" | custom-call | flops 2147483648 | bytes 6291456 | tf_op jit(solution)/shard_map/dispatch/pallas_call | solution.py:117
  5.7 7.8 %all-to-all-start = ((bf16[8,128,2048]{2,1,0:T(8,128)(2,1)}), bf16[8,128,2048]{2,1,0:T(8,128)(2,1)}, u32[]{:S(2)}, u32[]{:S(2)}) async-start(bf16[8,128,2048]{2,1,0:T(8,128)(2,1)} %dispatch.1), calls=%async_computation | async-start | bytes 8388608 | tf_op jit(solution)/shard_map/all_to_all | solution.py:365
  13.7 3.9 %collective-permute-start.1 = (bf16[64,2560]{1,0:T(8,128)(2,1)S(1)}, bf16[64,2560]{1,0:T(8,128)(2,1)S(1)}, u32[]{:S(2)}, u32[]{:S(2)}) collective-permute-start(bf16[64,2560]{1,0:T(8,128)(2,1)S(1)} %pad_maximum_fusion.1.refs_0_), channel_id=1, source_target_pairs={{0,224},{32,0},{64,32},{96,64},{128,96},{160,128},{192,160},{224,1... | collective-permute-start | bytes 983048 | tf_op jit(solution)/shard_map/ppermute | solution.py:349
  18.3 7.2 %base.2 = (bf16[256,512]{1,0:T(8,128)(2,1)}, bf16[256,512]{1,0:T(8,128)(2,1)}, f32[256,512]{1,0:T(8,128)}, bf16[256,512]{1,0:T(8,128)(2,1)}) custom-call(s32[28]{0:T(128)} %stack.112.table, bf16[512,2048]{1,0:T(8,128)(2,1)} %tokens.4, bf16[2048,2048]{1,0:T(8,128)(2,1)} %weight.3), custom_call_target="tpu_custom_call" | custom-call | flops 2147483648 | bytes 6291456 | tf_op jit(solution)/shard_map/base/pallas_call | solution.py:62
  25.5 2.5 %collective-permute-start.6 = (bf16[256,512]{1,0:T(8,128)(2,1)}, bf16[256,512]{1,0:T(8,128)(2,1)S(1)}, u32[]{:S(2)}, u32[]{:S(2)}) collective-permute-start(bf16[256,512]{1,0:T(8,128)(2,1)} %get-tuple-element.36), channel_id=1, source_target_pairs={{0,3},{1,0},{2,1},{3,2},{4,7},{5,4},{6,5},{7,6},{8,11},{9,8},{10,9... | collective-permute-start | bytes 786440 | tf_op jit(solution)/shard_map/ppermute | solution.py:374
  28.2 7.2 %base.3 = (bf16[256,512]{1,0:T(8,128)(2,1)}, f32[256,512]{1,0:T(8,128)}, f32[256,512]{1,0:T(8,128)}, f32[256,512]{1,0:T(8,128)}) custom-call(s32[28]{0:T(128)} %stack.112.table, bf16[512,2048]{1,0:T(8,128)(2,1)} %tokens.4, bf16[2048,2048]{1,0:T(8,128)(2,1)} %weight.3), custom_call_target="tpu_custom_call" | custom-call | flops 2147483648 | bytes 6291456 | tf_op jit(solution)/shard_map/base/pallas_call | solution.py:62
  35.5 1.9 %add_convert_fusion = bf16[256,512]{1,0:T(8,128)(2,1)} fusion(f32[256,512]{1,0:T(8,128)} %get-tuple-element.35, bf16[256,512]{1,0:T(8,128)(2,1)S(1)} %collective-permute-done.6), kind=kLoop, calls=%fused_computation.5 | loop fusion | flops 393216 | bytes 1048576 | tf_op jit(solution)/shard_map/convert_element_type | solution.py:378
  37.3 2.6 %collective-permute-start.7 = (bf16[256,512]{1,0:T(8,128)(2,1)}, bf16[256,512]{1,0:T(8,128)(2,1)}, u32[]{:S(2)}, u32[]{:S(2)}) collective-permute-start(bf16[256,512]{1,0:T(8,128)(2,1)} %add_convert_fusion), channel_id=1, source_target_pairs={{0,3},{1,0},{2,1},{3,2},{4,7},{5,4},{6,5},{7,6},{8,11},{9,8},{10,9... | collective-permute-start | bytes 786440 | tf_op jit(solution)/shard_map/ppermute | solution.py:378
  40.8 1.4 %collective-permute-start.4 = (bf16[256,512]{1,0:T(8,128)(2,1)}, bf16[256,512]{1,0:T(8,128)(2,1)S(1)}, u32[]{:S(2)}, u32[]{:S(2)}) collective-permute-start(bf16[256,512]{1,0:T(8,128)(2,1)} %get-tuple-element.32), channel_id=1, source_target_pairs={{0,3},{1,0},{2,1},{3,2},{4,7},{5,4},{6,5},{7,6},{8,11},{9,8},{10,9... | collective-permute-start | bytes 786440 | tf_op jit(solution)/shard_map/ppermute | solution.py:376
  42.2 2.6 %collective-permute-start.9 = (bf16[64,2560]{1,0:T(8,128)(2,1)S(1)}, bf16[64,2560]{1,0:T(8,128)(2,1)S(1)}, u32[]{:S(2)}, u32[]{:S(2)}) collective-permute-start(bf16[64,2560]{1,0:T(8,128)(2,1)S(1)} %collective-permute-done.1.refs_2_), channel_id=1, source_target_pairs={{0,224},{32,0},{64,32},{96,64},{128,96},{160,128},{192,160},{224,1... | collective-permute-start | bytes 983048 | tf_op jit(solution)/shard_map/ppermute | solution.py:349
  46.4 3.4 %collective-permute-done.9.refs_4_ = bf16[64,2560]{1,0:T(8,128)(2,1)S(1)} collective-permute-done((bf16[64,2560]{1,0:T(8,128)(2,1)S(1)}, bf16[64,2560]{1,0:T(8,128)(2,1)S(1)}, u32[]{:S(2)}, u32[]{:S(2)}) %collective-permute-start.9) | collective-permute-done | bytes 327712 | tf_op jit(solution)/shard_map/ppermute | solution.py:349
  49.7 3.5 %collective-permute-start.11 = (bf16[64,2560]{1,0:T(8,128)(2,1)S(1)}, bf16[64,2560]{1,0:T(8,128)(2,1)S(1)}, u32[]{:S(2)}, u32[]{:S(2)}) collective-permute-start(bf16[64,2560]{1,0:T(8,128)(2,1)S(1)} %collective-permute-done.9.refs_4_), channel_id=1, source_target_pairs={{0,224},{32,0},{64,32},{96,64},{128,96},{160,128},{192,160},{224,1... | collective-permute-start | bytes 983048 | tf_op jit(solution)/shard_map/ppermute | solution.py:349
  53.5 9.0 %all-to-all-done.rows = bf16[8,128,2048]{2,1,0:T(8,128)(2,1)} async-done(((bf16[8,128,2048]{2,1,0:T(8,128)(2,1)}), bf16[8,128,2048]{2,1,0:T(8,128)(2,1)}, u32[]{:S(2)}, u32[]{:S(2)}) %all-to-all-start) | async-done | bytes 4194336 | tf_op jit(solution)/shard_map/all_to_all | solution.py:365
  62.5 3.7 %down.1.refs_0_ = bf16[8,64,128]{2,1,0:T(8,128)(2,1)S(1)} custom-call(s32[28]{0:T(128)S(1)} %copy-done, bf16[8,128,2048]{2,1,0:T(8,128)(2,1)} %all-to-all-done.rows, bf16[64,2560]{1,0:T(8,128)(2,1)S(1)} %pad_maximum_fusion.1.refs_0_, bf16[64,2560]{1,0:T(8,128)(2,1)S(1)} %collective-permute-done.refs_1_, bf16[64,2560]{1,0:T(8,128)(2,1)S(1)} %collective-permute-done.1.refs_2_, ...), custom_call_target="tpu_custom_call" | custom-call | flops 268435456 | bytes 6291456 | tf_op jit(solution)/shard_map/down/pallas_call | solution.py:172
  67.6 2.4 %collective-permute-start.15 = (bf16[8,64,128]{2,1,0:T(8,128)(2,1)S(1)}, bf16[8,64,128]{2,1,0:T(8,128)(2,1)}, u32[]{:S(2)}, u32[]{:S(2)}) collective-permute-start(bf16[8,64,128]{2,1,0:T(8,128)(2,1)S(1)} %down.1.refs_0_), channel_id=1, source_target_pairs={{0,3},{1,0},{2,1},{3,2},{4,7},{5,4},{6,5},{7,6},{8,11},{9,8},{10,9... | collective-permute-start | bytes 393224 | tf_op jit(solution)/shard_map/ppermute | solution.py:395
  73.1 2.1 %up.1 = (bf16[128,512]{1,0:T(8,128)(2,1)S(1)}, bf16[128,512]{1,0:T(8,128)(2,1)S(1)}, bf16[128,512]{1,0:T(8,128)(2,1)S(1)}, bf16[128,512]{1,0:T(8,128)(2,1)S(1)},...) custom-call(s32[28]{0:T(128)S(1)} %copy-done, ...), custom_call_target="tpu_custom_call" | custom-call | flops 67108864 | bytes 1572864 | tf_op jit(solution)/shard_map/up/pallas_call | solution.py:246
  75.9 6.0 %collective-permute-start.17 = (bf16[128,512]{1,0:T(8,128)(2,1)S(1)}, bf16[128,512]{1,0:T(8,128)(2,1)S(1)}, u32[]{:S(2)}, u32[]{:S(2)}) collective-permute-start(bf16[128,512]{1,0:T(8,128)(2,1)S(1)} %get-tuple-element.43), channel_id=1, source_target_pairs={{0,20},{4,16},{8,28},{12,24},{16,4},{20,0},{24,12},{28,8},{1,21},{... | collective-permute-start | bytes 393224 | tf_op jit(solution)/shard_map/ppermute | solution.py:398
  82.2 1.5 %collective-permute-start.18 = (bf16[128,512]{1,0:T(8,128)(2,1)S(1)}, bf16[128,512]{1,0:T(8,128)(2,1)S(1)}, u32[]{:S(2)}, u32[]{:S(2)}) collective-permute-start(bf16[128,512]{1,0:T(8,128)(2,1)S(1)} %get-tuple-element.44), channel_id=1, source_target_pairs={{0,8},{4,12},{8,16},{12,20},{16,24},{20,28},{24,0},{28,4},{1,9},{5... | collective-permute-start | bytes 393224 | tf_op jit(solution)/shard_map/ppermute | solution.py:398
  83.7 1.3 %collective-permute-start.19 = (bf16[128,512]{1,0:T(8,128)(2,1)S(1)}, bf16[128,512]{1,0:T(8,128)(2,1)S(1)}, u32[]{:S(2)}, u32[]{:S(2)}) collective-permute-start(bf16[128,512]{1,0:T(8,128)(2,1)S(1)} %get-tuple-element.45), channel_id=1, source_target_pairs={{0,24},{4,28},{8,0},{12,4},{16,8},{20,12},{24,16},{28,20},{1,25},{... | collective-permute-start | bytes 393224 | tf_op jit(solution)/shard_map/ppermute | solution.py:398
  86.7 3.5 %collective-permute-start.22 = (bf16[128,512]{1,0:T(8,128)(2,1)S(1)}, bf16[128,512]{1,0:T(8,128)(2,1)S(1)}, u32[]{:S(2)}, u32[]{:S(2)}) collective-permute-start(bf16[128,512]{1,0:T(8,128)(2,1)S(1)} %get-tuple-element.48), channel_id=1, source_target_pairs={{0,28},{4,24},{8,4},{12,0},{16,12},{20,8},{24,20},{28,16},{1,29},{... | collective-permute-start | bytes 393224 | tf_op jit(solution)/shard_map/ppermute | solution.py:398
  90.2 1.3 %fusion.3.place = s32[512,1]{1,0:T(8,128)S(1)} fusion(s32[512,1]{1,0:T(8,128)} %copy.37, pred[512,1]{1,0:T(8,128)(4,1)S(1)} %copy.33, s32[512,1]{1,0:T(8,128)} %copy.30), kind=kLoop, calls=%fused_computation.16 | loop fusion | flops 11264 | bytes 6656 | tf_op jit(solution)/shard_map/add | solution.py:391
  91.5 1.7 %collective-permute-done.21.refs_6_ = bf16[128,512]{1,0:T(8,128)(2,1)S(1)} collective-permute-done((bf16[128,512]{1,0:T(8,128)(2,1)S(1)}, bf16[128,512]{1,0:T(8,128)(2,1)S(1)}, u32[]{:S(2)}, u32[]{:S(2)}) %collective-permute-start.21) | collective-permute-done | bytes 131104 | tf_op jit(solution)/shard_map/ppermute | solution.py:398
  93.2 1.3 %early.1.base = f32[512,512]{1,0:T(8,128)S(1)} custom-call(s32[28]{0:T(128)S(1)} %copy-done, s32[512,1]{1,0:T(8,128)S(1)} %fusion.3.place, f32[512,512]{1,0:T(8,128)S(1)} %pad_maximum_fusion.base, bf16[128,512]{1,0:T(8,128)(2,1)S(1)} %get-tuple-element.41.refs_0_, bf16[128,512]{1,0:T(8,128)(2,1)S(1)} %collective-permute-done.16.refs_1_, ...), custom_call_target="tpu_custom_call" | custom-call | flops 469762048 | bytes 1048576 | tf_op jit(solution)/shard_map/early/pallas_call | solution.py:284
  94.5 1.6 %final.1 = bf16[512,512]{1,0:T(8,128)(2,1)} custom-call(s32[28]{0:T(128)S(1)} %copy-done, s32[512,1]{1,0:T(8,128)S(1)} %fusion.3.place, f32[512,512]{1,0:T(8,128)S(1)} %early.1.base, bf16[128,512]{1,0:T(8,128)(2,1)S(1)} %collective-permute-done.22.refs_0_), custom_call_target="tpu_custom_call" | custom-call | flops 67108864 | bytes 1048576 | tf_op jit(solution)/shard_map/final/pallas_call | solution.py:319
  (57 shorter events, 10.8 us)
Async XLA Ops:
  5.7 56.8 %all-to-all-start = ((bf16[8,128,2048]{2,1,0:T(8,128)(2,1)}), bf16[8,128,2048]{2,1,0:T(8,128)(2,1)}, u32[]{:S(2)}, u32[]{:S(2)}) async-start(bf16[8,128,2048]{2,1,0:T(8,128)(2,1)} %dispatch.1), calls=%async_computation | async-start | bytes 8388608 | tf_op jit(solution)/shard_map/all_to_all | solution.py:365
  13.6 14.4 %collective-permute-start = (bf16[64,2560]{1,0:T(8,128)(2,1)S(1)}, bf16[64,2560]{1,0:T(8,128)(2,1)S(1)}, u32[]{:S(2)}, u32[]{:S(2)}) collective-permute-start(bf16[64,2560]{1,0:T(8,128)(2,1)S(1)} %pad_maximum_fusion.1.refs_0_), channel_id=1, source_target_pairs={{0,32},{32,64},{64,96},{96,128},{128,160},{160,192},{192,224},{224... | collective-permute-start | bytes 983048 | tf_op jit(solution)/shard_map/ppermute | solution.py:346
  13.7 14.3 %collective-permute-start.1 = (bf16[64,2560]{1,0:T(8,128)(2,1)S(1)}, bf16[64,2560]{1,0:T(8,128)(2,1)S(1)}, u32[]{:S(2)}, u32[]{:S(2)}) collective-permute-start(bf16[64,2560]{1,0:T(8,128)(2,1)S(1)} %pad_maximum_fusion.1.refs_0_), channel_id=1, source_target_pairs={{0,224},{32,0},{64,32},{96,64},{128,96},{160,128},{192,160},{224,1... | collective-permute-start | bytes 983048 | tf_op jit(solution)/shard_map/ppermute | solution.py:349
  25.5 10.0 %collective-permute-start.6 = (bf16[256,512]{1,0:T(8,128)(2,1)}, bf16[256,512]{1,0:T(8,128)(2,1)S(1)}, u32[]{:S(2)}, u32[]{:S(2)}) collective-permute-start(bf16[256,512]{1,0:T(8,128)(2,1)} %get-tuple-element.36), channel_id=1, source_target_pairs={{0,3},{1,0},{2,1},{3,2},{4,7},{5,4},{6,5},{7,6},{8,11},{9,8},{10,9... | collective-permute-start | bytes 786440 | tf_op jit(solution)/shard_map/ppermute | solution.py:374
  27.9 17.0 %collective-permute-start.5 = (bf16[256,512]{1,0:T(8,128)(2,1)}, bf16[256,512]{1,0:T(8,128)(2,1)S(1)}, u32[]{:S(2)}, u32[]{:S(2)}) collective-permute-start(bf16[256,512]{1,0:T(8,128)(2,1)} %get-tuple-element.34), channel_id=1, source_target_pairs={{0,1},{1,2},{2,3},{3,0},{4,5},{5,6},{6,7},{7,4},{8,9},{9,10},{10,1... | collective-permute-start | bytes 786440 | tf_op jit(solution)/shard_map/ppermute | solution.py:375
  28.0 14.2 %collective-permute-start.2 = (bf16[256,512]{1,0:T(8,128)(2,1)}, bf16[256,512]{1,0:T(8,128)(2,1)S(1)}, u32[]{:S(2)}, u32[]{:S(2)}) collective-permute-start(bf16[256,512]{1,0:T(8,128)(2,1)} %get-tuple-element.31), channel_id=1, source_target_pairs={{0,1},{1,2},{2,3},{3,0},{4,5},{5,6},{6,7},{7,4},{8,9},{9,10},{10,1... | collective-permute-start | bytes 786440 | tf_op jit(solution)/shard_map/ppermute | solution.py:373
  28.2 16.6 %collective-permute-start.8 = (bf16[64,2560]{1,0:T(8,128)(2,1)S(1)}, bf16[64,2560]{1,0:T(8,128)(2,1)S(1)}, u32[]{:S(2)}, u32[]{:S(2)}) collective-permute-start(bf16[64,2560]{1,0:T(8,128)(2,1)S(1)} %collective-permute-done.refs_1_), channel_id=1, source_target_pairs={{0,32},{32,64},{64,96},{96,128},{128,160},{160,192},{192,224},{224... | collective-permute-start | bytes 983048 | tf_op jit(solution)/shard_map/ppermute | solution.py:346
  37.3 7.8 %collective-permute-start.7 = (bf16[256,512]{1,0:T(8,128)(2,1)}, bf16[256,512]{1,0:T(8,128)(2,1)}, u32[]{:S(2)}, u32[]{:S(2)}) collective-permute-start(bf16[256,512]{1,0:T(8,128)(2,1)} %add_convert_fusion), channel_id=1, source_target_pairs={{0,3},{1,0},{2,1},{3,2},{4,7},{5,4},{6,5},{7,6},{8,11},{9,8},{10,9... | collective-permute-start | bytes 786440 | tf_op jit(solution)/shard_map/ppermute | solution.py:378
  40.8 12.5 %collective-permute-start.4 = (bf16[256,512]{1,0:T(8,128)(2,1)}, bf16[256,512]{1,0:T(8,128)(2,1)S(1)}, u32[]{:S(2)}, u32[]{:S(2)}) collective-permute-start(bf16[256,512]{1,0:T(8,128)(2,1)} %get-tuple-element.32), channel_id=1, source_target_pairs={{0,3},{1,0},{2,1},{3,2},{4,7},{5,4},{6,5},{7,6},{8,11},{9,8},{10,9... | collective-permute-start | bytes 786440 | tf_op jit(solution)/shard_map/ppermute | solution.py:376
  42.2 7.5 %collective-permute-start.9 = (bf16[64,2560]{1,0:T(8,128)(2,1)S(1)}, bf16[64,2560]{1,0:T(8,128)(2,1)S(1)}, u32[]{:S(2)}, u32[]{:S(2)}) collective-permute-start(bf16[64,2560]{1,0:T(8,128)(2,1)S(1)} %collective-permute-done.1.refs_2_), channel_id=1, source_target_pairs={{0,224},{32,0},{64,32},{96,64},{128,96},{160,128},{192,160},{224,1... | collective-permute-start | bytes 983048 | tf_op jit(solution)/shard_map/ppermute | solution.py:349
  44.9 8.4 %collective-permute-start.10 = (bf16[64,2560]{1,0:T(8,128)(2,1)S(1)}, bf16[64,2560]{1,0:T(8,128)(2,1)S(1)}, u32[]{:S(2)}, u32[]{:S(2)}) collective-permute-start(bf16[64,2560]{1,0:T(8,128)(2,1)S(1)} %collective-permute-done.8.refs_3_), channel_id=1, source_target_pairs={{0,32},{32,64},{64,96},{96,128},{128,160},{160,192},{192,224},{224... | collective-permute-start | bytes 983048 | tf_op jit(solution)/shard_map/ppermute | solution.py:346
  45.0 8.3 %collective-permute-start.3 = (bf16[256,512]{1,0:T(8,128)(2,1)S(1)}, bf16[256,512]{1,0:T(8,128)(2,1)S(1)}, u32[]{:S(2)}, u32[]{:S(2)}) collective-permute-start(bf16[256,512]{1,0:T(8,128)(2,1)S(1)} %add_convert_fusion.1), channel_id=1, source_target_pairs={{0,1},{1,2},{2,3},{3,0},{4,5},{5,6},{6,7},{7,4},{8,9},{9,10},{10,1... | collective-permute-start | bytes 786440 | tf_op jit(solution)/shard_map/ppermute | solution.py:377
  49.7 12.7 %collective-permute-start.11 = (bf16[64,2560]{1,0:T(8,128)(2,1)S(1)}, bf16[64,2560]{1,0:T(8,128)(2,1)S(1)}, u32[]{:S(2)}, u32[]{:S(2)}) collective-permute-start(bf16[64,2560]{1,0:T(8,128)(2,1)S(1)} %collective-permute-done.9.refs_4_), channel_id=1, source_target_pairs={{0,224},{32,0},{64,32},{96,64},{128,96},{160,128},{192,160},{224,1... | collective-permute-start | bytes 983048 | tf_op jit(solution)/shard_map/ppermute | solution.py:349
  53.3 9.2 %collective-permute-start.12 = (bf16[64,2560]{1,0:T(8,128)(2,1)S(1)}, bf16[64,2560]{1,0:T(8,128)(2,1)}, u32[]{:S(2)}, u32[]{:S(2)}) collective-permute-start(bf16[64,2560]{1,0:T(8,128)(2,1)S(1)} %collective-permute-done.10.refs_5_), channel_id=1, source_target_pairs={{0,32},{32,64},{64,96},{96,128},{128,160},{160,192},{192,224},{224... | collective-permute-start | bytes 983048 | tf_op jit(solution)/shard_map/ppermute | solution.py:346
  66.2 5.9 %collective-permute-start.13 = (bf16[8,64,128]{2,1,0:T(8,128)(2,1)S(1)}, bf16[8,64,128]{2,1,0:T(8,128)(2,1)}, u32[]{:S(2)}, u32[]{:S(2)}) collective-permute-start(bf16[8,64,128]{2,1,0:T(8,128)(2,1)S(1)} %down.1.refs_0_), channel_id=1, source_target_pairs={{0,2},{1,3},{2,0},{3,1},{4,6},{5,7},{6,4},{7,5},{8,10},{9,11},{10,... | collective-permute-start | bytes 393224 | tf_op jit(solution)/shard_map/ppermute | solution.py:395
  67.3 5.8 %collective-permute-start.14 = (bf16[8,64,128]{2,1,0:T(8,128)(2,1)S(1)}, bf16[8,64,128]{2,1,0:T(8,128)(2,1)}, u32[]{:S(2)}, u32[]{:S(2)}) collective-permute-start(bf16[8,64,128]{2,1,0:T(8,128)(2,1)S(1)} %down.1.refs_0_), channel_id=1, source_target_pairs={{0,1},{1,2},{2,3},{3,0},{4,5},{5,6},{6,7},{7,4},{8,9},{9,10},{10,1... | collective-permute-start | bytes 393224 | tf_op jit(solution)/shard_map/ppermute | solution.py:395
  67.6 5.5 %collective-permute-start.15 = (bf16[8,64,128]{2,1,0:T(8,128)(2,1)S(1)}, bf16[8,64,128]{2,1,0:T(8,128)(2,1)}, u32[]{:S(2)}, u32[]{:S(2)}) collective-permute-start(bf16[8,64,128]{2,1,0:T(8,128)(2,1)S(1)} %down.1.refs_0_), channel_id=1, source_target_pairs={{0,3},{1,0},{2,1},{3,2},{4,7},{5,4},{6,5},{7,6},{8,11},{9,8},{10,9... | collective-permute-start | bytes 393224 | tf_op jit(solution)/shard_map/ppermute | solution.py:395
  75.2 10.3 %collective-permute-start.16 = (bf16[128,512]{1,0:T(8,128)(2,1)S(1)}, bf16[128,512]{1,0:T(8,128)(2,1)S(1)}, u32[]{:S(2)}, u32[]{:S(2)}) collective-permute-start(bf16[128,512]{1,0:T(8,128)(2,1)S(1)} %get-tuple-element.42), channel_id=1, source_target_pairs={{0,16},{4,20},{8,24},{12,28},{16,0},{20,4},{24,8},{28,12},{1,17},{... | collective-permute-start | bytes 393224 | tf_op jit(solution)/shard_map/ppermute | solution.py:398
  75.9 10.7 %collective-permute-start.17 = (bf16[128,512]{1,0:T(8,128)(2,1)S(1)}, bf16[128,512]{1,0:T(8,128)(2,1)S(1)}, u32[]{:S(2)}, u32[]{:S(2)}) collective-permute-start(bf16[128,512]{1,0:T(8,128)(2,1)S(1)} %get-tuple-element.43), channel_id=1, source_target_pairs={{0,20},{4,16},{8,28},{12,24},{16,4},{20,0},{24,12},{28,8},{1,21},{... | collective-permute-start | bytes 393224 | tf_op jit(solution)/shard_map/ppermute | solution.py:398
  82.2 9.3 %collective-permute-start.18 = (bf16[128,512]{1,0:T(8,128)(2,1)S(1)}, bf16[128,512]{1,0:T(8,128)(2,1)S(1)}, u32[]{:S(2)}, u32[]{:S(2)}) collective-permute-start(bf16[128,512]{1,0:T(8,128)(2,1)S(1)} %get-tuple-element.44), channel_id=1, source_target_pairs={{0,8},{4,12},{8,16},{12,20},{16,24},{20,28},{24,0},{28,4},{1,9},{5... | collective-permute-start | bytes 393224 | tf_op jit(solution)/shard_map/ppermute | solution.py:398
  83.7 7.8 %collective-permute-start.19 = (bf16[128,512]{1,0:T(8,128)(2,1)S(1)}, bf16[128,512]{1,0:T(8,128)(2,1)S(1)}, u32[]{:S(2)}, u32[]{:S(2)}) collective-permute-start(bf16[128,512]{1,0:T(8,128)(2,1)S(1)} %get-tuple-element.45), channel_id=1, source_target_pairs={{0,24},{4,28},{8,0},{12,4},{16,8},{20,12},{24,16},{28,20},{1,25},{... | collective-permute-start | bytes 393224 | tf_op jit(solution)/shard_map/ppermute | solution.py:398
  85.0 6.5 %collective-permute-start.20 = (bf16[128,512]{1,0:T(8,128)(2,1)S(1)}, bf16[128,512]{1,0:T(8,128)(2,1)S(1)}, u32[]{:S(2)}, u32[]{:S(2)}) collective-permute-start(bf16[128,512]{1,0:T(8,128)(2,1)S(1)} %get-tuple-element.46), channel_id=1, source_target_pairs={{0,4},{4,0},{8,12},{12,8},{16,20},{20,16},{24,28},{28,24},{1,5},{5... | collective-permute-start | bytes 393224 | tf_op jit(solution)/shard_map/ppermute | solution.py:398
  85.6 7.6 %collective-permute-start.21 = (bf16[128,512]{1,0:T(8,128)(2,1)S(1)}, bf16[128,512]{1,0:T(8,128)(2,1)S(1)}, u32[]{:S(2)}, u32[]{:S(2)}) collective-permute-start(bf16[128,512]{1,0:T(8,128)(2,1)S(1)} %get-tuple-element.47), channel_id=1, source_target_pairs={{0,12},{4,8},{8,20},{12,16},{16,28},{20,24},{24,4},{28,0},{1,13},{... | collective-permute-start | bytes 393224 | tf_op jit(solution)/shard_map/ppermute | solution.py:398
  86.7 7.8 %collective-permute-start.22 = (bf16[128,512]{1,0:T(8,128)(2,1)S(1)}, bf16[128,512]{1,0:T(8,128)(2,1)S(1)}, u32[]{:S(2)}, u32[]{:S(2)}) collective-permute-start(bf16[128,512]{1,0:T(8,128)(2,1)S(1)} %get-tuple-element.48), channel_id=1, source_target_pairs={{0,28},{4,24},{8,4},{12,0},{16,12},{20,8},{24,20},{28,16},{1,29},{... | collective-permute-start | bytes 393224 | tf_op jit(solution)/shard_map/ppermute | solution.py:398
  (6 other events, 89.4 us)
